TPU v7x, 32 devices: a whole 2x2x4 slice. The times are simulated.
32 devices in a mesh: dp: 8 (over z, y), head: 4 (over x, core).
Axes of the slice: x: 2, y: 2, z: 4, core: 2. Of those that a mesh axis runs over, the one named last changes fastest.
Arguments:
- layer_input: bfloat16 [16, 2048, 768], P('dp', 'head'), may hold values from -6 to 6
- doc_lengths: int32 [16, 6], P('dp'), may hold values from 1 to 1024, 2048 in all within a row
- ln1_gain: bfloat16 [2, 768], P(None, 'dp'), may hold values from 0.5 to 1.5
- ln1_bias: bfloat16 [2, 768], P(None, 'dp'), may hold values from -1.5 to 1.5
- qkv_weight: bfloat16 [2, 768, 2304], P(None, 'dp', 'head'), may hold values from -0.0625 to 0.0625
- out_weight: bfloat16 [2, 768, 768], P(None, 'head', 'dp'), may hold values from -2 to 2
- ln2_gain: bfloat16 [2, 768], P(None, 'dp'), may hold values from 0.5 to 1.5
- ln2_bias: bfloat16 [2, 768], P(None, 'dp'), may hold values from -1.5 to 1.5
- in_weight: bfloat16 [2, 768, 3072], P(None, 'dp', 'head'), may hold values from -0.21875 to 0.21875
- down_weight: bfloat16 [2, 3072, 768], P(None, 'head', 'dp'), may hold values from -0.109375 to 0.109375
- cotangent: bfloat16 [16, 2048, 768], P('dp', 'head'), may hold values from -6 to 6
Outputs:
- layer_output: bfloat16 [16, 2048, 768], P('dp', 'head')
- input_grad: float32 [16, 2048, 768], P('dp', 'head')
- ln1_gain_grad: float32 [2, 768], P(None, ('dp', 'head'))
- ln1_bias_grad: float32 [2, 768], P(None, ('dp', 'head'))
- qkv_grad: float32 [2, 768, 2304], P(None, 'dp', 'head')
- out_grad: float32 [2, 768, 768], P(None, 'head', 'dp')
- ln2_gain_grad: float32 [2, 768], P(None, ('dp', 'head'))
- ln2_bias_grad: float32 [2, 768], P(None, ('dp', 'head'))
- in_grad: float32 [2, 768, 3072], P(None, 'dp', 'head')
- down_grad: float32 [2, 3072, 768], P(None, 'head', 'dp')
Inputs may be any that keep to these rules, and one draw needn't show every extreme that they name: `doc_lengths`: each row's 6 lengths sum to 2048, and the largest of them is exactly 1024.
All inputs are finite; a program needn't handle non-finite values.
Results may differ from a plain program's by a relative error of at most 0.014.
Values may be sent and summed in bfloat16 or wider, within the bound.
No kernel may reach another device: no remote copies, remote signals or barrier semaphores. Data moves between devices by JAX's collectives and lax.ppermute only.
A program may use at most 448 MiB of HBM per device.

v0:
```python
from functools import partial
import math

import jax
import jax.numpy as jnp
from jax import lax
from jax.sharding import PartitionSpec as P

HD = 64
ROW = 2048
BLOCK = 512


NORM_EPS = 1e-05
HIGHEST_PRECISION = lax.Precision.HIGHEST


def entering(shard, axis, join, neutral):
    place = lax.axis_index(axis)
    gathered = jax.tree.map(
        lambda a, kind: lax.all_gather(a.astype(kind), axis),
        shard,
        (jnp.bfloat16, jnp.bfloat16, jnp.bfloat16),
    )
    state = jax.tree.map(lambda a, e: jnp.zeros_like(a) + jnp.asarray(e, a.dtype), shard, neutral)

    def one(hop, state):
        return join(
            state,
            jax.tree.map(
                lambda a, own: lax.dynamic_index_in_dim(a, hop, 0, False).astype(own.dtype),
                gathered,
                shard,
            ),
        )

    return lax.fori_loop(0, place, one, state)


def entering_2(shard, axis, combine, identity):
    size, here = (lax.axis_size(axis), lax.axis_index(axis))
    everything = jax.tree.map(
        lambda part, kind: lax.all_gather(part.astype(kind), axis),
        shard,
        jax.tree.map(lambda a: jnp.bfloat16 if a.dtype == jnp.float32 else a.dtype, shard),
    )
    start = jax.tree.map(
        lambda part, zero: jnp.broadcast_to(jnp.asarray(zero, part.dtype), part.shape),
        shard,
        identity,
    )

    def hop(k, before):
        at = size - 1 - k
        reached = at > here
        new = combine(
            before, jax.tree.map(lambda part, own: part[at].astype(own.dtype), everything, shard)
        )
        return jax.tree.map(lambda a, b: jnp.where(reached, a, b), new, before)

    return lax.fori_loop(0, size, hop, start)


def doc_place(lengths_row):
    doc_ends = jnp.cumsum(lengths_row)
    doc_starts = doc_ends - lengths_row
    position = jnp.arange(ROW, dtype=jnp.int32)
    inside = (
        (position[:, None] >= doc_starts[None, :]) & (position[:, None] < doc_ends[None, :])
    ).astype(jnp.int32)
    labels = jnp.arange(lengths_row.shape[0], dtype=jnp.int32)
    doc_index = jnp.sum(inside * labels[None, :], axis=1)
    doc_start = jnp.sum(inside * doc_starts[None, :], axis=1)
    doc_size = jnp.sum(inside * lengths_row[None, :], axis=1)
    angles = math.pi / 2 * (position - doc_start).astype(jnp.float32) / doc_size.astype(jnp.float32)
    return (doc_index, angles)


def layer_norm(stream, gain_vec, bias_vec):
    average = jnp.mean(stream, axis=-1, keepdims=True)
    centered = stream - average
    variance = jnp.mean(centered * centered, axis=-1, keepdims=True)
    return centered * lax.rsqrt(variance + NORM_EPS) * gain_vec + bias_vec


def features(values, angles):
    positive = jax.nn.relu(values)
    return jnp.concatenate(
        [positive * jnp.cos(angles)[:, None, None], positive * jnp.sin(angles)[:, None, None]],
        axis=-1,
    )


def attend(query_rows, key_rows, value_rows, kv_in, key_in, doc_in, doc_index, angles):
    row_count, heads_here, head_width = value_rows.shape
    blocks = row_count // BLOCK
    query_feat = features(query_rows, angles).reshape(blocks, BLOCK, heads_here, 2 * head_width)
    key_feat = features(key_rows, angles).reshape(blocks, BLOCK, heads_here, 2 * head_width)
    value_blocks = value_rows.reshape(blocks, BLOCK, heads_here, head_width)
    doc_blocks = doc_index.reshape(blocks, BLOCK)
    causal = jnp.arange(BLOCK)[:, None] >= jnp.arange(BLOCK)[None, :]

    def block_step(carried_in, pieces):
        kv_state, key_total, last_doc = carried_in
        query_block, key_block, value_block, doc_block = pieces
        same_doc = ((doc_block[:, None] == doc_block[None, :]) & causal).astype(jnp.float32)
        weights = (
            jnp.einsum("ihf,jhf->hij", query_block, key_block, precision=HIGHEST_PRECISION)
            * same_doc[None]
        )
        numerator = jnp.einsum("hij,jhe->ihe", weights, value_block, precision=HIGHEST_PRECISION)
        denominator = jnp.sum(weights, axis=2).T
        from_before = (doc_block == last_doc).astype(jnp.float32)[:, None]
        numerator = numerator + from_before[:, :, None] * jnp.einsum(
            "ihf,hfe->ihe", query_block, kv_state, precision=HIGHEST_PRECISION
        )
        denominator = denominator + from_before * jnp.einsum(
            "ihf,hf->ih", query_block, key_total, precision=HIGHEST_PRECISION
        )
        attended = numerator / (denominator + 1.0)[:, :, None]
        tail_doc = doc_block[BLOCK - 1]
        keep_flag = (last_doc == tail_doc).astype(jnp.float32)
        member = (doc_block == tail_doc).astype(jnp.float32)[:, None, None]
        masked = key_block * member
        kv_state = keep_flag * kv_state + jnp.einsum(
            "jhf,jhe->hfe", masked, value_block, precision=HIGHEST_PRECISION
        )
        key_total = keep_flag * key_total + jnp.sum(masked, axis=0)
        return ((kv_state, key_total, tail_doc), attended)

    initial = (kv_in, key_in, doc_in)
    _, attended = lax.scan(
        jax.checkpoint(block_step), initial, (query_feat, key_feat, value_blocks, doc_blocks)
    )
    return attended.reshape(row_count, heads_here, head_width)


def summary(key_rows, value_rows, doc_index, angles):
    key_feat = features(key_rows, angles)
    member = (doc_index == doc_index[doc_index.shape[0] - 1]).astype(jnp.float32)[:, None, None]
    masked = key_feat * member
    kv_local = jnp.einsum("jhf,jhe->hfe", masked, value_rows, precision=HIGHEST_PRECISION)
    return (kv_local, jnp.sum(masked, axis=0))


def join_states(earlier, later):
    kv_early, key_early, doc_early = earlier
    kv_late, key_late, doc_late = later
    empty_late = doc_late < 0.0
    same_doc = doc_late == doc_early
    kv_joined = jnp.where(empty_late, kv_early, jnp.where(same_doc, kv_early + kv_late, kv_late))
    key_joined = jnp.where(
        empty_late, key_early, jnp.where(same_doc, key_early + key_late, key_late)
    )
    return (kv_joined, key_joined, jnp.where(empty_late, doc_early, doc_late))


def join_grads(earlier, later):
    kv_high, key_high, doc_high = earlier
    kv_lower, key_lower, doc_lower = later
    empty_lower = doc_lower < -1.5
    same_doc = doc_high == doc_lower
    kv_joined = jnp.where(empty_lower, kv_high, jnp.where(same_doc, kv_lower + kv_high, kv_lower))
    key_joined = jnp.where(
        empty_lower, key_high, jnp.where(same_doc, key_lower + key_high, key_lower)
    )
    return (kv_joined, key_joined, jnp.where(empty_lower, doc_high, doc_lower))


def contract_rows(left, right):
    return lax.dot_general(
        left, right, (((0,), (0,)), ((), ())), preferred_element_type=jnp.float32
    )


def times_transposed(left, right):
    return lax.dot_general(
        left, right, (((1,), (1,)), ((), ())), preferred_element_type=jnp.float32
    )


def gather_layer(weights, layer_index):
    gain_one, bias_one, qkv_part, out_part, gain_two, bias_two, in_part, down_part = [
        member[layer_index] for member in weights
    ]
    return (
        lax.all_gather(gain_one, "dp", axis=0, tiled=True),
        lax.all_gather(bias_one, "dp", axis=0, tiled=True),
        lax.all_gather(qkv_part, "dp", axis=0, tiled=True),
        lax.all_gather(out_part, "dp", axis=1, tiled=True),
        lax.all_gather(gain_two, "dp", axis=0, tiled=True),
        lax.all_gather(bias_two, "dp", axis=0, tiled=True),
        lax.all_gather(in_part, "dp", axis=0, tiled=True),
        lax.all_gather(down_part, "dp", axis=1, tiled=True),
    )


def gather_again(weights, layer_index):
    gain_one, bias_one, qkv_part, out_part, gain_two, bias_two, in_part, down_part = [
        member[layer_index] for member in weights
    ]
    return (
        lax.all_gather(gain_one, "dp", axis=0, tiled=True),
        lax.all_gather(bias_one, "dp", axis=0, tiled=True),
        lax.all_gather(qkv_part, "dp", axis=0, tiled=True),
        lax.all_gather(out_part, "dp", axis=1, tiled=True),
        lax.all_gather(gain_two, "dp", axis=0, tiled=True),
        lax.all_gather(bias_two, "dp", axis=0, tiled=True),
        lax.all_gather(in_part, "dp", axis=0, tiled=True),
        lax.all_gather(down_part, "dp", axis=1, tiled=True),
    )


def widen(gathered):
    gain_one, bias_one, qkv_part, out_part, gain_two, bias_two, in_part, down_part = gathered
    qkv_full, out_full, in_full, down_full = (
        lax.all_gather(qkv_part, "head", axis=1, tiled=True),
        lax.all_gather(out_part, "head", axis=0, tiled=True),
        lax.all_gather(in_part, "head", axis=1, tiled=True),
        lax.all_gather(down_part, "head", axis=0, tiled=True),
    )
    return (gain_one, bias_one, qkv_full, out_full, gain_two, bias_two, in_full, down_full)


def shards(
    layer_input,
    doc_lengths,
    ln1_gain,
    ln1_bias,
    qkv_weight,
    out_weight,
    ln2_gain,
    ln2_bias,
    in_weight,
    down_weight,
    cotangent,
):
    weights = (
        ln1_gain,
        ln1_bias,
        qkv_weight,
        out_weight,
        ln2_gain,
        ln2_bias,
        in_weight,
        down_weight,
    )
    batches, shard_rows, model_width = layer_input.shape
    layers = qkv_weight.shape[0]
    groups = lax.axis_size("head")
    heads_group = out_weight.shape[1] // HD
    all_heads = groups * heads_group
    first_row = lax.axis_index("head") * shard_rows
    outputs = []
    input_parts = []
    weight_sums = [None] * layers
    norm_sums = [None] * layers
    for batch_index in range(batches):
        doc_index, angles = doc_place(doc_lengths[batch_index])
        local_doc = lax.dynamic_slice_in_dim(doc_index, first_row, shard_rows, 0)
        local_angles = lax.dynamic_slice_in_dim(angles, first_row, shard_rows, 0)
        stream = layer_input[batch_index].astype(jnp.float32)
        saved = []
        for layer_index in range(layers):
            gathered = gather_layer(weights, layer_index)
            gathered = widen(gathered)
            gain_one, bias_one, qkv_full, out_full, gain_two, bias_two, in_full, down_full = (
                gathered
            )
            normed, norm_back_one = jax.vjp(
                layer_norm, stream, gain_one.astype(jnp.float32), bias_one.astype(jnp.float32)
            )
            normed_low = normed.astype(jnp.bfloat16)
            mixed = jnp.dot(normed_low, qkv_full, preferred_element_type=jnp.float32).astype(
                jnp.bfloat16
            )
            mixed_values = mixed.astype(jnp.float32).reshape(shard_rows, groups, 3, heads_group, HD)
            query_rows = mixed_values[:, :, 0].reshape(shard_rows, all_heads, HD)
            key_rows = mixed_values[:, :, 1].reshape(shard_rows, all_heads, HD)
            value_rows = mixed_values[:, :, 2].reshape(shard_rows, all_heads, HD)
            local_state, summary_back = jax.vjp(
                partial(summary, doc_index=local_doc, angles=local_angles), key_rows, value_rows
            )
            tail_doc = local_doc[shard_rows - 1].astype(jnp.float32)
            kv_start = jnp.zeros((all_heads, 2 * HD, HD), jnp.float32)
            key_start = jnp.zeros((all_heads, 2 * HD), jnp.float32)
            kv_in, key_in, doc_in = entering(
                (local_state[0], local_state[1], tail_doc),
                "head",
                join_states,
                (kv_start, key_start, jnp.array(-1.0, jnp.float32)),
            )
            attended, attend_back = jax.vjp(
                partial(
                    attend,
                    doc_in=doc_in.astype(jnp.int32),
                    doc_index=local_doc,
                    angles=local_angles,
                ),
                query_rows,
                key_rows,
                value_rows,
                kv_in,
                key_in,
            )
            attended_low = attended.reshape(shard_rows, all_heads * HD).astype(jnp.bfloat16)
            stream = stream + jnp.dot(attended_low, out_full, preferred_element_type=jnp.float32)
            attention_keep = (normed_low, attend_back, summary_back, doc_in, tail_doc)
            normed_two, norm_back_two = jax.vjp(
                layer_norm, stream, gain_two.astype(jnp.float32), bias_two.astype(jnp.float32)
            )
            normed_two_low = normed_two.astype(jnp.bfloat16)
            ffn_rows = normed_two_low
            pre_act = jnp.dot(ffn_rows, in_full, preferred_element_type=jnp.float32)
            act_low = jax.nn.gelu(pre_act).astype(jnp.bfloat16)
            stream = stream + jnp.dot(act_low, down_full, preferred_element_type=jnp.float32)
            saved.append(
                (
                    gathered,
                    norm_back_one,
                    attention_keep,
                    attended_low,
                    norm_back_two,
                    ffn_rows,
                    pre_act,
                    act_low,
                )
            )
        outputs.append(stream.astype(jnp.bfloat16))
        grad_stream = cotangent[batch_index].astype(jnp.float32)
        for layer_index in reversed(range(layers)):
            (
                gathered,
                norm_back_one,
                attention_keep,
                attended_low,
                norm_back_two,
                ffn_rows,
                pre_act,
                act_low,
            ) = saved[layer_index]
            gathered = gather_again(weights, layer_index)
            gathered = widen(gathered)
            gain_one, bias_one, qkv_full, out_full, gain_two, bias_two, in_full, down_full = (
                gathered
            )
            grad_low = grad_stream.astype(jnp.bfloat16)
            grad_here = grad_low
            down_term = contract_rows(act_low, grad_here)
            act_grad = times_transposed(grad_here, down_full)
            _, gelu_back = jax.vjp(jax.nn.gelu, pre_act)
            pre_grad = gelu_back(act_grad)[0].astype(jnp.bfloat16)
            in_term = contract_rows(ffn_rows, pre_grad)
            normed_grad = times_transposed(pre_grad, in_full)
            stream_part, gain_two_part, bias_two_part = norm_back_two(normed_grad)
            grad_stream = grad_stream + stream_part
            grad_low = grad_stream.astype(jnp.bfloat16)
            grad_here = grad_low
            row_count = grad_here.shape[0]
            out_term = contract_rows(attended_low, grad_here)
            attention_rows, attend_back, summary_back, doc_in, tail_doc = attention_keep
            heads_here = out_full.shape[0] // HD
            attended_grad = times_transposed(grad_here, out_full).reshape(row_count, heads_here, HD)
            query_grad, key_grad, value_grad, kv_grad, key_total_grad = attend_back(attended_grad)
            after_kv, after_key, after_doc = entering_2(
                (kv_grad, key_total_grad, doc_in),
                "head",
                join_grads,
                (
                    jnp.zeros_like(kv_grad),
                    jnp.zeros_like(key_total_grad),
                    jnp.array(-2.0, jnp.float32),
                ),
            )
            carried = (after_doc == tail_doc).astype(jnp.float32)
            key_more, value_more = summary_back((carried * after_kv, carried * after_key))
            key_grad = key_grad + key_more
            value_grad = value_grad + value_more
            mixed_grad = jnp.stack(
                [
                    query_grad.reshape(row_count, groups, heads_group, HD),
                    key_grad.reshape(row_count, groups, heads_group, HD),
                    value_grad.reshape(row_count, groups, heads_group, HD),
                ],
                axis=2,
            )
            mixed_grad = mixed_grad.reshape(row_count, 3 * all_heads * HD).astype(jnp.bfloat16)
            qkv_term = contract_rows(attention_rows, mixed_grad)
            normed_grad = times_transposed(mixed_grad, qkv_full)
            stream_part, gain_one_part, bias_one_part = norm_back_one(normed_grad)
            grad_stream = grad_stream + stream_part
            norm_parts = (gain_one_part, bias_one_part, gain_two_part, bias_two_part)
            if batch_index == 0:
                norm_sums[layer_index] = norm_parts
            else:
                norm_sums[layer_index] = tuple(
                    (left + right for left, right in zip(norm_sums[layer_index], norm_parts))
                )
            shares = (
                lax.psum_scatter(qkv_term, "dp", scatter_dimension=0, tiled=True),
                lax.psum_scatter(out_term, "dp", scatter_dimension=1, tiled=True),
                lax.psum_scatter(in_term, "dp", scatter_dimension=0, tiled=True),
                lax.psum_scatter(down_term, "dp", scatter_dimension=1, tiled=True),
            )
            if batch_index == 0:
                weight_sums[layer_index] = shares
            else:
                weight_sums[layer_index] = tuple(
                    (left + right for left, right in zip(weight_sums[layer_index], shares))
                )
        input_parts.append(grad_stream)
    layer_output = jnp.stack(outputs)
    input_grad = jnp.stack(input_parts)
    stacked_norms = [
        jnp.stack([norm_sums[layer_index][member] for layer_index in range(layers)])
        for member in range(4)
    ]
    gain_one_grad, bias_one_grad, gain_two_grad, bias_two_grad = (
        lax.psum_scatter(stacked_norms[0], ("dp", "head"), scatter_dimension=1, tiled=True),
        lax.psum_scatter(stacked_norms[1], ("dp", "head"), scatter_dimension=1, tiled=True),
        lax.psum_scatter(stacked_norms[2], ("dp", "head"), scatter_dimension=1, tiled=True),
        lax.psum_scatter(stacked_norms[3], ("dp", "head"), scatter_dimension=1, tiled=True),
    )
    stacked_weights = [
        jnp.stack([weight_sums[layer_index][member] for layer_index in range(layers)])
        for member in range(4)
    ]
    qkv_grad, out_grad, in_grad, down_grad = stacked_weights
    qkv_grad, out_grad, in_grad, down_grad = (
        lax.psum_scatter(
            qkv_grad.astype(jnp.bfloat16), "head", scatter_dimension=2, tiled=True
        ).astype(jnp.float32),
        lax.psum_scatter(
            out_grad.astype(jnp.bfloat16), "head", scatter_dimension=1, tiled=True
        ).astype(jnp.float32),
        lax.psum_scatter(
            in_grad.astype(jnp.bfloat16), "head", scatter_dimension=2, tiled=True
        ).astype(jnp.float32),
        lax.psum_scatter(
            down_grad.astype(jnp.bfloat16), "head", scatter_dimension=1, tiled=True
        ).astype(jnp.float32),
    )
    return (
        layer_output,
        input_grad,
        gain_one_grad,
        bias_one_grad,
        qkv_grad,
        out_grad,
        gain_two_grad,
        bias_two_grad,
        in_grad,
        down_grad,
    )


def solution(mesh):
    in_specs = (
        P("dp", "head", None),
        P("dp", None),
        P(None, "dp"),
        P(None, "dp"),
        P(None, "dp", "head"),
        P(None, "head", "dp"),
        P(None, "dp"),
        P(None, "dp"),
        P(None, "dp", "head"),
        P(None, "head", "dp"),
        P("dp", "head", None),
    )
    out_specs = (
        P("dp", "head", None),
        P("dp", "head", None),
        P(None, ("dp", "head")),
        P(None, ("dp", "head")),
        P(None, "dp", "head"),
        P(None, "head", "dp"),
        P(None, ("dp", "head")),
        P(None, ("dp", "head")),
        P(None, "dp", "head"),
        P(None, "head", "dp"),
    )
    return jax.shard_map(shards, mesh=mesh, in_specs=in_specs, out_specs=out_specs, check_vma=False)
```

profile of v0, /device:TPU:0, one launch (start us, length us, event | category | flops | bytes accessed | tf_op | source)
XLA Modules:
  0.0 2464.3 jit_solution(18146583765625273901)
XLA Ops:
  13.1 36.0 %all-gather.2 = bf16[1,768,576]{2,1,0:T(8,128)(2,1)S(1)} all-gather(bf16[1,96,576]{2,1,0:T(8,128)(2,1)S(1)} %get-tuple-element.2249), channel_id=4, replica_groups=mesh['dp'=8,'head'=4] {'dp'}, dimensions={1}, use_global_device_ids=true | all-gather | bytes 995328 | tf_op jit(solution)/shard_map/all_gather | solution.py:189
  50.5 33.2 %all-gather.6 = bf16[1,192,768]{1,0,2:T(2,128)(2,1)S(1)} all-gather(bf16[1,192,96]{1,0,2:T(2,128)(2,1)S(1)} %copy.889), channel_id=8, replica_groups=mesh['dp'=8,'head'=4] {'dp'}, dimensions={2}, use_global_device_ids=true | all-gather | bytes 331776 | tf_op jit(solution)/shard_map/all_gather | solution.py:190
  86.2 17.9 all-gather.69.cloned.1.call-done
  104.1 34.0 %all-gather.16 = bf16[1,768,576]{2,1,0:T(8,128)(2,1)S(1)} all-gather(bf16[1,96,576]{2,1,0:T(8,128)(2,1)S(1)} %get-tuple-element.2248), channel_id=18, replica_groups=mesh['dp'=8,'head'=4] {'dp'}, dimensions={1}, use_global_device_ids=true | all-gather | bytes 995328 | tf_op jit(solution)/shard_map/all_gather | solution.py:189
  139.7 32.9 %all-gather.20 = bf16[1,192,768]{1,0,2:T(2,128)(2,1)S(1)} all-gather(bf16[1,192,96]{1,0,2:T(2,128)(2,1)S(1)} %copy.890), channel_id=22, replica_groups=mesh['dp'=8,'head'=4] {'dp'}, dimensions={2}, use_global_device_ids=true | all-gather | bytes 331776 | tf_op jit(solution)/shard_map/all_gather | solution.py:190
  190.0 34.0 %all-reduce.19 = (bf16[768]{0:T(1024)(128)(2,1)S(1)}, bf16[768]{0:T(1024)(128)(2,1)S(1)}, bf16[768]{0:T(1024)(128)(2,1)S(1)}, bf16[768]{0:T(1024)(128)(2,1)S(1)}...) all-reduce(bf16[768]{0:T(1024)(128)(2,1)S(1)} %dynamic-update-slice, ...), channel_id=3, replica_groups=mesh['dp'=8,'head'=4] {'dp'}, use_global_device_ids=true, to_apply=%add.1 | all-reduce | flops 6144 | bytes 24576
  311.8 31.7 %all-gather.40 = bf16[4,12,128]{2,1,0:T(8,128)(2,1)} all-gather(bf16[1,12,128]{2,1,0:T(8,128)(2,1)S(1)} %bitcast.1030), channel_id=7, replica_groups=mesh['dp'=8,'head'=4] {'head'}, dimensions={0}, use_global_device_ids=true | all-gather | bytes 15360 | tf_op jit(solution)/shard_map/all_gather | solution.py:21
  345.2 13.7 all-gather.4
  378.6 12.3 multiply_reduce_fusion.3
  408.5 12.1 multiply_reduce_fusion.1
  476.2 30.4 %all-gather.41 = bf16[4,12,128]{2,1,0:T(8,128)(2,1)S(1)} all-gather(bf16[1,12,128]{2,1,0:T(8,128)(2,1)S(1)} %bitcast.1031), channel_id=21, replica_groups=mesh['dp'=8,'head'=4] {'head'}, dimensions={0}, use_global_device_ids=true | all-gather | bytes 15360 | tf_op jit(solution)/shard_map/all_gather | solution.py:21
  558.2 16.6 all-gather.43
  590.6 12.1 multiply_reduce_fusion.2
  624.4 12.4 multiply_reduce_fusion
  710.0 14.0 multiply_reduce_fusion.5
  741.4 12.2 multiply_reduce_fusion.7
  806.7 12.8 fusion.246
  821.8 19.4 all-gather.36
  857.2 36.8 %while.42 = (s32[]{:T(128)}, f32[12,128,64]{2,1,0:T(8,128)}, f32[12,128]{1,0:T(8,128)}, f32[]{:T(128)}, s32[]{:T(128)}, /*index=5*/bf16[4]{0:T(256)(128)(2,1)}, ...) while((s32[]{:T(128)}, f32[12,128,64]{2,1,0:T(8,128)}, ...), condition=%wide.region_61.62_spmd.clone, body=%wide.region_60.61_spmd.clone.sunk | while | flops 599052 | bytes 1785099 | solution.py:61
  905.0 23.9 fusion.21
  929.0 14.6 bitcast_add_fusion.1
  960.5 15.1 fusion.260
  994.3 37.2 %while.40 = (s32[]{:T(128)}, f32[12,128,64]{2,1,0:T(8,128)}, f32[12,128]{1,0:T(8,128)}, f32[]{:T(128)}, s32[]{:T(128)}, /*index=5*/bf16[4]{0:T(256)(128)(2,1)}, ...) while((s32[]{:T(128)}, f32[12,128,64]{2,1,0:T(8,128)}, ...), condition=%wide.region_45.46_spmd.clone, body=%wide.region_44.45_spmd.clone.sunk | while | flops 599052 | bytes 1785099 | solution.py:61
  1041.2 24.5 fusion.17
  1065.7 14.6 bitcast_add_fusion.3
  1096.9 16.4 add_convert_fusion
  1113.3 15.1 add_convert_fusion.1
  1180.4 12.0 multiply_reduce_fusion.4
  1226.2 18.0 while.43
  1257.8 12.5 fusion.239
  1284.0 23.9 fusion.23
  1308.0 15.8 bitcast_add_fusion
  1331.8 11.9 multiply_reduce_fusion.6
  1388.6 34.8 %while.41 = (s32[]{:T(128)}, f32[12,128,64]{2,1,0:T(8,128)}, f32[12,128]{1,0:T(8,128)S(1)}, f32[]{:T(128)}, s32[]{:T(128)}, /*index=5*/bf16[4]{0:T(256)(128)(2,1...) while((s32[]{:T(128)}, f32[12,128,64]{2,1,0:T(8,128)}, ...), condition=%wide.region_53.54_spmd.clone, body=%wide.region_52.53_spmd.clone.sunk | while | flops 599052 | bytes 1785099 | solution.py:61
  1435.1 10.4 fusion.253
  1445.5 22.2 fusion.19
  1476.2 14.5 bitcast_add_fusion.2
  1507.0 15.5 fusion.24
  1531.9 11.9 fusion.32
  1638.8 43.5 %reduce-scatter.25.cloned.1.call-done = f32[96,2304]{1,0:T(8,128)} async-done(((f32[768,2304]{1,0:T(8,128)}), f32[96,2304]{1,0:T(8,128)}) %reduce-scatter.25.cloned.1.call-update) | async-done | bytes 884752 | tf_op jit(solution)/shard_map/reduce_scatter | solution.py:400
  1693.0 155.2 %reduce-scatter.39.cloned.1.call-done = f32[3072,96]{0,1:T(8,128)} async-done(((f32[3072,768]{0,1:T(8,128)}), f32[3072,96]{0,1:T(8,128)}) %reduce-scatter.39.cloned.1.call-update) | async-done | bytes 1179664 | tf_op jit(solution)/shard_map/reduce_scatter | solution.py:403
  1850.4 163.9 %reduce-scatter.37.cloned.1.call-done = f32[3072,96]{0,1:T(8,128)} async-done(((f32[3072,768]{0,1:T(8,128)}), f32[3072,96]{0,1:T(8,128)}) %reduce-scatter.37.cloned.1.call-update) | async-done | bytes 1179664 | tf_op jit(solution)/shard_map/reduce_scatter | solution.py:403
  2018.0 43.8 %all-reduce.18 = (f32[2,768]{1,0:T(2,128)S(1)}, f32[2,768]{1,0:T(2,128)S(1)}, f32[2,768]{1,0:T(2,128)S(1)}, f32[2,768]{1,0:T(2,128)S(1)}) all-reduce(f32[2,768]{1,0:T(2,128)S(1)} %pad_maximum_fusion.16, f32[2,768]{1,0:T(2,128)S(1)} %pad_maximum_fusion.17, ...), channel_id=50, replica_groups=mesh['dp'=8,'head'=4] {'dp','head'}, use_global_device_ids=true, to_apply=%region_76.77.clone | all-reduce | flops 6144 | bytes 49152
  2063.7 117.7 %reduce-scatter.35.cloned.1.call-done = f32[96,3072]{1,0:T(8,128)} async-done(((f32[768,3072]{1,0:T(8,128)}), f32[96,3072]{1,0:T(8,128)}) %reduce-scatter.35.cloned.1.call-update) | async-done | bytes 1179664 | tf_op jit(solution)/shard_map/reduce_scatter | solution.py:402
  2183.5 163.9 %reduce-scatter.33.cloned.1.call-done = f32[96,3072]{1,0:T(8,128)} async-done(((f32[768,3072]{1,0:T(8,128)}), f32[96,3072]{1,0:T(8,128)}) %reduce-scatter.33.cloned.1.call-update) | async-done | bytes 1179664 | tf_op jit(solution)/shard_map/reduce_scatter | solution.py:402
  2372.3 26.4 %reduce-scatter.41.cloned.1.call-done = bf16[576,192]{1,0:T(8,128)(2,1)} async-done(((bf16[2304,192]{1,0:T(8,128)(2,1)}), bf16[576,192]{1,0:T(8,128)(2,1)}) %reduce-scatter.41.cloned.1.call-update) | async-done | bytes 221200
  2400.9 26.3 %reduce-scatter.23.cloned.1.call-done = bf16[2,768,96]{1,2,0:T(8,128)(2,1)} async-done(((bf16[2,3072,96]{1,2,0:T(8,128)(2,1)}), bf16[2,768,96]{1,2,0:T(8,128)(2,1)}) %reduce-scatter.23.cloned.1.call-update) | async-done | bytes 294928 | tf_op jit(solution)/shard_map/reduce_scatter | solution.py:439
  2429.0 26.4 %reduce-scatter.21.cloned.1.call-done = bf16[2,96,768]{2,1,0:T(8,128)(2,1)} async-done(((bf16[2,96,3072]{2,1,0:T(8,128)(2,1)}), bf16[2,96,768]{2,1,0:T(8,128)(2,1)}) %reduce-scatter.21.cloned.1.call-update) | async-done | bytes 294928 | tf_op jit(solution)/shard_map/reduce_scatter | solution.py:436
  (1415 shorter events, 977.5 us)
Async XLA Ops:
  7.2 78.3 %all-gather.65.cloned.1.call-start = ((), (), s32[]{:S(2)}) async-start(), calls=%async_computation.16 | async-start | bytes 1327104 | tf_op jit(solution)/shard_map/all_gather | solution.py:193
  9.0 95.1 %all-gather.69.cloned.1.call-start = ((), (), s32[]{:S(2)}) async-start(), calls=%async_computation.18 | async-start | bytes 1327104 | tf_op jit(solution)/shard_map/all_gather | solution.py:194
  10.8 163.6 %all-gather.77.cloned.1.call-start = ((), (), s32[]{:S(2)}) async-start(), calls=%async_computation.22 | async-start | bytes 1327104 | tf_op jit(solution)/shard_map/all_gather | solution.py:193
  11.5 223.1 %all-gather.81.cloned.1.call-start = ((), (), s32[]{:S(2)}) async-start(), calls=%async_computation.24 | async-start | bytes 1327104 | tf_op jit(solution)/shard_map/all_gather | solution.py:194
  12.1 223.1 %all-gather.61.cloned.1.call-start = ((), (), s32[]{:S(2)}) async-start(), calls=%async_computation.14 | async-start | bytes 4423680 | tf_op jit(solution)/shard_map/all_gather | solution.py:217
  50.3 350.4 %all-gather.63.cloned.1.call-start = ((), (), s32[]{:S(2)}) async-start(), calls=%async_computation.15 | async-start | bytes 1474560 | tf_op jit(solution)/shard_map/all_gather | solution.py:218
  85.4 348.4 %all-gather.67.cloned.1.call-start = ((), (), s32[]{:S(2)}) async-start(), calls=%async_computation.17 | async-start | bytes 5898240 | tf_op jit(solution)/shard_map/all_gather | solution.py:219
  86.1 355.2 %all-gather.71.cloned.1.call-start = ((), (), s32[]{:S(2)}) async-start(), calls=%async_computation.19 | async-start | bytes 5898240 | tf_op jit(solution)/shard_map/all_gather | solution.py:220
  104.1 345.2 %all-gather.73.cloned.1.call-start = ((), (), s32[]{:S(2)}) async-start(), calls=%async_computation.20 | async-start | bytes 4423680 | tf_op jit(solution)/shard_map/all_gather | solution.py:217
  138.2 92.5 %copy-start.71 = (bf16[2,512,768]{2,1,0:T(8,128)(2,1)S(1)}, bf16[2,512,768]{2,1,0:T(8,128)(2,1)}, u32[]{:S(2)}) copy-start(bf16[2,512,768]{2,1,0:T(8,128)(2,1)} %param.27) | copy-start | bytes 4718596
  139.5 476.4 %all-gather.75.cloned.1.call-start = ((), (), s32[]{:S(2)}) async-start(), calls=%async_computation.21 | async-start | bytes 1474560 | tf_op jit(solution)/shard_map/all_gather | solution.py:218
  174.3 478.7 %all-gather.79.cloned.1.call-start = ((), (), s32[]{:S(2)}) async-start(), calls=%async_computation.23 | async-start | bytes 5898240 | tf_op jit(solution)/shard_map/all_gather | solution.py:219
  175.0 491.4 %all-gather.83.cloned.1.call-start = ((), (), s32[]{:S(2)}) async-start(), calls=%async_computation.25 | async-start | bytes 5898240 | tf_op jit(solution)/shard_map/all_gather | solution.py:220
  175.8 58.8 %copy-start.241 = (s32[512]{0:T(512)}, s32[512]{0:T(512)S(1)}, u32[]{:S(2)}) copy-start(s32[512]{0:T(512)S(1)} %dynamic_slice.276) | copy-start | bytes 6148
  177.1 57.5 %copy-start.238 = (s32[512]{0:T(512)}, s32[512]{0:T(512)S(1)}, u32[]{:S(2)}) copy-start(s32[512]{0:T(512)S(1)} %dynamic_slice.274) | copy-start | bytes 6148
  228.5 75.8 %copy-start.276 = (f32[512]{0:T(512)}, f32[512]{0:T(512)S(1)}, u32[]{:S(2)}) copy-start(f32[512]{0:T(512)S(1)} %sin.4) | copy-start | bytes 6148
  229.2 56.2 %copy-start.233 = (f32[512]{0:T(512)}, f32[512]{0:T(512)S(1)}, u32[]{:S(2)}) copy-start(f32[512]{0:T(512)S(1)} %compare_convert_fusion.10) | copy-start | bytes 6148
  229.9 113.6 %copy-start.229 = (f32[512]{0:T(512)}, f32[512]{0:T(512)S(1)}, u32[]{:S(2)}) copy-start(f32[512]{0:T(512)S(1)} %compare_convert_fusion.13) | copy-start | bytes 6148
  234.6 1397.1 %reduce-scatter.31.cloned.1.call-start = ((), (), s32[]{:S(2)}) async-start(), calls=%async_computation.29 | async-start | bytes 2654208 | tf_op jit(solution)/shard_map/reduce_scatter | solution.py:401
  279.8 128.8 %copy-start.9 = (f32[512,12,128]{2,0,1:T(8,128)}, f32[512,12,128]{2,0,1:T(8,128)S(1)}, u32[]{:S(2)}) copy-start(f32[512,12,128]{2,0,1:T(8,128)S(1)} %get-tuple-element.1428) | copy-start | bytes 9437188
  297.5 108.3 %copy-start.202 = (f32[12,128]{1,0:T(8,128)}, f32[12,128]{1,0:T(8,128)S(1)}, u32[]{:S(2)}) copy-start(f32[12,128]{1,0:T(8,128)S(1)} %get-tuple-element.1430) | copy-start | bytes 18436
  430.7 86.9 %copy-start.284 = (f32[512]{0:T(512)}, f32[512]{0:T(512)S(1)}, u32[]{:S(2)}) copy-start(f32[512]{0:T(512)S(1)} %broadcast_multiply_fusion.10) | copy-start | bytes 6148
  432.1 85.4 %copy-start.302 = (f32[512]{0:T(512)}, f32[512]{0:T(512)S(1)}, u32[]{:S(2)}) copy-start(f32[512]{0:T(512)S(1)} %fusion.507) | copy-start | bytes 6148
  585.6 119.4 %copy-start.206 = (f32[12,128]{1,0:T(8,128)}, f32[12,128]{1,0:T(8,128)S(1)}, u32[]{:S(2)}) copy-start(f32[12,128]{1,0:T(8,128)S(1)} %get-tuple-element.1416) | copy-start | bytes 18436
  619.1 69.1 %copy-start.331 = (f32[512]{0:T(512)}, f32[512]{0:T(512)S(1)}, u32[]{:S(2)}) copy-start(f32[512]{0:T(512)S(1)} %broadcast_multiply_fusion.12) | copy-start | bytes 6148
  698.7 68.7 %copy-start.263 = (f32[512]{0:T(512)}, f32[512]{0:T(512)S(1)}, u32[]{:S(2)}) copy-start(f32[512]{0:T(512)S(1)} %get-tuple-element.2288) | copy-start | bytes 6148
  704.8 114.7 %copy-start.266 = (f32[512]{0:T(512)}, f32[512]{0:T(512)S(1)}, u32[]{:S(2)}) copy-start(f32[512]{0:T(512)S(1)} %get-tuple-element.2290) | copy-start | bytes 6148
  782.2 850.6 %reduce-scatter.29.cloned.1.call-start = ((), (), s32[]{:S(2)}) async-start(), calls=%async_computation.28 | async-start | bytes 2654208 | tf_op jit(solution)/shard_map/reduce_scatter | solution.py:401
  1169.9 87.8 %copy-start.49 = (f32[512,768]{0,1:T(8,128)}, f32[512,768]{0,1:T(8,128)S(1)}, u32[]{:S(2)}) copy-start(f32[512,768]{0,1:T(8,128)S(1)} %fusion.336) | copy-start | bytes 4718596
  1177.7 67.1 %copy-start.268 = (f32[512]{0:T(512)}, f32[512]{0:T(512)S(1)}, u32[]{:S(2)}) copy-start(f32[512]{0:T(512)S(1)} %get-tuple-element.2283) | copy-start | bytes 6148
  1192.4 65.3 %copy-start.208 = (f32[512,12]{0,1:T(8,128)}, f32[512,12]{0,1:T(8,128)S(1)}, u32[]{:S(2)}) copy-start(f32[512,12]{0,1:T(8,128)S(1)} %get-tuple-element.2175) | copy-start | bytes 73732
  1226.1 410.7 %reduce-scatter.27.cloned.1.call-start = ((), (), s32[]{:S(2)}) async-start(), calls=%async_computation.27 | async-start | bytes 7962624 | tf_op jit(solution)/shard_map/reduce_scatter | solution.py:400
  1275.5 406.7 %reduce-scatter.25.cloned.1.call-start = ((), (), s32[]{:S(2)}) async-start(), calls=%async_computation.26 | async-start | bytes 7962624 | tf_op jit(solution)/shard_map/reduce_scatter | solution.py:400
  1278.4 79.9 %copy-start.270 = (f32[512]{0:T(512)}, f32[512]{0:T(512)S(1)}, u32[]{:S(2)}) copy-start(f32[512]{0:T(512)S(1)} %get-tuple-element.2285) | copy-start | bytes 6148
  1556.8 291.4 %reduce-scatter.39.cloned.1.call-start = ((), (), s32[]{:S(2)}) async-start(), calls=%async_computation.33 | async-start | bytes 10616832 | tf_op jit(solution)/shard_map/reduce_scatter | solution.py:403
  1573.1 441.1 %reduce-scatter.37.cloned.1.call-start = ((), (), s32[]{:S(2)}) async-start(), calls=%async_computation.32 | async-start | bytes 10616832 | tf_op jit(solution)/shard_map/reduce_scatter | solution.py:403
  1588.5 592.9 %reduce-scatter.35.cloned.1.call-start = ((), (), s32[]{:S(2)}) async-start(), calls=%async_computation.31 | async-start | bytes 10616832 | tf_op jit(solution)/shard_map/reduce_scatter | solution.py:402
  1600.5 746.9 %reduce-scatter.33.cloned.1.call-start = ((), (), s32[]{:S(2)}) async-start(), calls=%async_computation.30 | async-start | bytes 10616832 | tf_op jit(solution)/shard_map/reduce_scatter | solution.py:402
  1612.5 757.9 %reduce-scatter.43.cloned.1.call-start = ((), (), s32[]{:S(2)}) async-start(), calls=%async_computation.35 | async-start | bytes 491520
  1636.7 762.0 %reduce-scatter.41.cloned.1.call-start = ((), (), s32[]{:S(2)}) async-start(), calls=%async_computation.34 | async-start | bytes 1474560
  1692.9 324.9 %copy-start.358 = (f32[1,768]{1,0:T(1,128)S(1)}, f32[1,768]{1,0:T(1,128)}, u32[]{:S(2)}) copy-start(f32[1,768]{1,0:T(1,128)} %add.1001) | copy-start | bytes 9220
  1692.9 324.9 %copy-start.359 = (f32[1,768]{1,0:T(1,128)S(1)}, f32[1,768]{1,0:T(1,128)}, u32[]{:S(2)}) copy-start(f32[1,768]{1,0:T(1,128)} %add.999) | copy-start | bytes 9220
  1693.0 325.0 %copy-start.357 = (f32[1,768]{1,0:T(1,128)S(1)}, f32[1,768]{1,0:T(1,128)}, u32[]{:S(2)}) copy-start(f32[1,768]{1,0:T(1,128)} %add.997) | copy-start | bytes 9220
  1693.0 325.0 %copy-start.360 = (f32[1,768]{1,0:T(1,128)S(1)}, f32[1,768]{1,0:T(1,128)}, u32[]{:S(2)}) copy-start(f32[1,768]{1,0:T(1,128)} %add.995) | copy-start | bytes 9220
  1693.0 325.0 %copy-start.312 = (f32[2,768]{1,0:T(2,128)S(1)}, f32[2,768]{1,0:T(2,128)}, u32[]{:S(2)}) copy-start(f32[2,768]{1,0:T(2,128)} %pad_maximum_fusion.18) | copy-start | bytes 18436
  1693.0 325.0 %copy-start.313 = (f32[2,768]{1,0:T(2,128)S(1)}, f32[2,768]{1,0:T(2,128)}, u32[]{:S(2)}) copy-start(f32[2,768]{1,0:T(2,128)} %pad_maximum_fusion.19) | copy-start | bytes 18436
  1693.0 734.2 %reduce-scatter.23.cloned.1.call-start = ((), (), s32[]{:S(2)}) async-start(), calls=%async_computation.13 | async-start | bytes 1474560 | tf_op jit(solution)/shard_map/reduce_scatter | solution.py:439
  2017.8 437.5 %reduce-scatter.21.cloned.1.call-start = ((), (), s32[]{:S(2)}) async-start(), calls=%async_computation.12 | async-start | bytes 1474560 | tf_op jit(solution)/shard_map/reduce_scatter | solution.py:436
  (398 other events, 3864.4 us)
Sparse Core Ops, SparseCore 0:
  10.8 49.5 all-gather.64
  63.1 40.9 all-gather.68
  106.8 48.4 all-gather.76
  158.0 40.8 all-gather.80
  200.9 29.5 all-gather.60
  231.8 17.4 all-gather.62
  250.9 37.5 all-gather.66
  290.0 38.3 all-gather.70
  330.0 35.0 all-gather.72
  366.5 17.4 all-gather.74
  385.5 37.4 all-gather.78
  424.4 37.4 all-gather.82
  782.3 76.7 reduce-scatter.30
  1226.2 65.2 reduce-scatter.28
  1295.0 128.0 reduce-scatter.26
  1556.9 125.2 reduce-scatter.24
  1685.7 162.4 reduce-scatter.38
  1851.7 162.5 reduce-scatter.36
  2017.8 163.4 reduce-scatter.34
  2184.8 162.5 reduce-scatter.32
  2350.5 19.8 reduce-scatter.42
  2373.0 25.6 reduce-scatter.40
  2401.4 25.6 reduce-scatter.22
  2429.6 25.7 reduce-scatter.20
where the time goes:
time: 2480 us; the launch traced here: 2460 us
  matrix products  826 us (33%)
  waiting for transfers between devices  749 us (30%)
  blocking collectives  422 us (17%)
  local copies, waits for them, and re-layouts  212 us (9%)
  other arithmetic  195 us (8%)
  loops' own time  33.3 us (1%)
    reduce_scatter x2, waiting for transfers between devices, shards(): lax.psum_scatter(down_term, 'dp', scatter_dimension=1, tiled=True)  319 us
    reduce_scatter x2, waiting for transfers between devices, shards(): lax.psum_scatter(in_term, 'dp', scatter_dimension=0, tiled=True)  282 us
    dot_general x16, matrix products, block_step(): jnp.einsum('ihf,jhf->hij', query_block, key_block, precision=HIGHEST_PREC...  253 us
    dot_general x16, matrix products, block_step(): jnp.einsum('hij,jhe->ihe', weights, value_block, precision=HIGHEST_PRECIS...  165 us
    all_gather x8, blocking collectives, entering(): lax.all_gather(a.astype(kind), axis)  125 us
    unnamed x4, blocking collectives  91 us
    dot_general x16, matrix products, contract_rows(): lax.dot_general(left, right, (((0,), (0,)), ((), ())), preferred_element_...  77.5 us
    dot_general x16, matrix products, block_step(): jnp.einsum('ihf,hfe->ihe', query_block, kv_state, precision=HIGHEST_PRECI...  74.1 us
  transfers between devices with their start and end apart: 24, of which 10 were waited for; matrix products, arithmetic and copies ran while one was open for 44% of the time, Pallas kernels for 0%

commit v1 on v0

v1 whole, which is shorter than its diff:
```python
import math

import jax
import jax.numpy as jnp
from jax import lax
from jax.sharding import PartitionSpec as P

HD = 64
ROW = 2048
NORM_EPS = 1e-05
BF = jnp.bfloat16
F32 = jnp.float32


def xor_groups(n):
    groups, span = [[1]], 2
    while span < n:
        radix = min(4, n // span)
        groups.append([span * k for k in range(1, radix)])
        span *= radix
    return groups[::-1]


def swap(x, axis, mask):
    n = lax.axis_size(axis)
    return lax.ppermute(x, axis, [(i, i ^ mask) for i in range(n)])


def forward_shift(x, by):
    n = lax.axis_size("head")
    return lax.ppermute(x, "head", [(i, i + by) for i in range(n - by)])


def backward_shift(x, by):
    n = lax.axis_size("head")
    return lax.ppermute(x, "head", [(i + by, i) for i in range(n - by)])


def block_order(groups):
    order = [0]
    for masks in groups:
        order = order + [r ^ m for m in masks for r in order]
    return order


def spread(x, axis, masks, dim):
    return jnp.concatenate([x] + [swap(x, axis, m) for m in masks], axis=dim)


def pair_columns(own, other):
    pieces = []
    for at in range(0, own.shape[1], HD):
        pieces += [own[:, at : at + HD], other[:, at : at + HD]]
    return jnp.concatenate(pieces, axis=1)


def plain_columns(own, other):
    return jnp.concatenate([own, other], axis=1)


def gather(shard, groups, join, last):
    x = shard
    for masks in groups[:-1]:
        x = spread(x, "dp", masks, 0)
    if last == "x":
        x = spread(x, "dp", groups[-1], 0)
        half = join(x, swap(x, "head", 2))
    else:
        half = join(x, swap(x, "head", 2))
        half = spread(half, "dp", groups[-1], 0)
    return half, swap(half, "head", 1)


def split_pairs(x):
    own = [x[:, at : at + HD] for at in range(0, x.shape[1], 2 * HD)]
    other = [x[:, at + HD : at + 2 * HD] for at in range(0, x.shape[1], 2 * HD)]
    return jnp.concatenate(own, axis=1), jnp.concatenate(other, axis=1)


def split_plain(x):
    c = x.shape[1] // 2
    return x[:, :c], x[:, c:]


def add_rows(x, axis, masks):
    rows = x.shape[0] // (len(masks) + 1)
    total = x[:rows].astype(F32)
    for j, m in enumerate(masks):
        piece = x[(j + 1) * rows : (j + 2) * rows].astype(BF)
        total = total + swap(piece, axis, m).astype(F32)
    return total


def reduce_scatter(own, other, groups, split, first):
    total = own + swap(other.astype(BF), "head", 1).astype(F32)
    rest = groups[::-1]
    if first == "y":
        total = add_rows(total, "dp", rest[0])
        rest = rest[1:]
    keep, send = split(total)
    total = keep + swap(send.astype(BF), "head", 2).astype(F32)
    for masks in rest:
        total = add_rows(total, "dp", masks)
    return total


def norm(stream, gain, bias):
    mean = jnp.mean(stream, axis=-1, keepdims=True)
    centred = stream - mean
    rstd = lax.rsqrt(jnp.mean(centred * centred, axis=-1, keepdims=True) + NORM_EPS)
    return (centred * rstd * gain + bias).astype(BF), (mean, rstd)


def norm_back(stream, stats, gain, grad):
    mean, rstd = stats
    xhat = (stream - mean) * rstd
    gain_grad = jnp.sum(grad * xhat, axis=0)
    bias_grad = jnp.sum(grad, axis=0)
    g = grad * gain
    back = rstd * (
        g - jnp.mean(g, axis=-1, keepdims=True) - xhat * jnp.mean(g * xhat, axis=-1, keepdims=True)
    )
    return back, gain_grad, bias_grad


def gelu_and_slope(x):
    c = math.sqrt(2.0 / math.pi)
    t = jnp.tanh(c * (x + 0.044715 * (x * x * x)))
    half = 0.5 * (1.0 + t)
    slope = half + 0.5 * x * (1.0 - t * t) * (c * (1.0 + 3 * 0.044715 * (x * x)))
    return (x * half).astype(BF), slope.astype(BF)


def dot(a, b):
    return lax.dot_general(a, b, (((1,), (0,)), ((), ())), preferred_element_type=F32)


def dot_t(a, b):
    return lax.dot_general(a, b, (((1,), (1,)), ((), ())), preferred_element_type=F32)


def t_dot(a, b):
    return lax.dot_general(a, b, (((0,), (0,)), ((), ())), preferred_element_type=F32)


def places(lengths, position):
    n = lengths.shape[0]
    upto = jnp.arange(n)[:, None] <= jnp.arange(n)[None, :]
    ends = jnp.sum(jnp.where(upto, lengths[:, None], 0), axis=0)
    passed = (position[:, None] >= ends[None, :]).astype(jnp.int32)
    doc = jnp.sum(passed, axis=1)
    start = jnp.sum(passed * lengths[None, :], axis=1)
    here = (doc[:, None] == jnp.arange(n)[None, :]).astype(jnp.int32)
    size = jnp.sum(here * lengths[None, :], axis=1)
    return doc, start, size


STATE_ROWS = 144


def heads_of(x, b, rows):
    return x[b * rows : (b + 1) * rows].reshape(rows, -1, HD)


def qkv_of(mixed, b, rows):
    width = mixed.shape[1] // 3
    q, k, v = [heads_of(mixed[:, i * width : (i + 1) * width], b, rows) for i in range(3)]
    return jax.nn.relu(q).astype(F32), jax.nn.relu(k).astype(F32), v.astype(F32), q, k


def pack_state(kv, ks):
    heads = kv.shape[1]
    kv = kv.reshape(2, heads // 2, 2, HD, HD).transpose(1, 0, 3, 2, 4).reshape(heads // 2, 2 * HD, 2 * HD)
    ks = ks.reshape(2, heads // 2, 2 * HD).transpose(1, 0, 2)
    pad = jnp.zeros((heads // 2, STATE_ROWS - 2 * HD - 2, 2 * HD), F32)
    return jnp.concatenate([kv, ks, pad], axis=1).astype(BF)


def unpack_state(st):
    pairs = st.shape[0]
    st = st.astype(F32)
    kv = st[:, : 2 * HD].reshape(pairs, 2, HD, 2, HD).transpose(1, 0, 3, 2, 4).reshape(2, 2 * pairs, HD, HD)
    ks = st[:, 2 * HD : 2 * HD + 2].transpose(1, 0, 2).reshape(2, 2 * pairs, HD)
    return kv, ks


def local_state(mixed, info, rows):
    out = []
    for b in range(2):
        _, rk, v, _, _ = qkv_of(mixed, b, rows)
        w = jnp.stack([info["memcos"][b], info["memsin"][b]])
        kf = (w[:, :, None, None] * rk[None]).astype(BF)
        kv = jnp.einsum("stha,the->shae", kf, v.astype(BF), preferred_element_type=F32)
        ks = jnp.sum(kf.astype(F32), axis=1)
        out.append(pack_state(kv, ks))
    return jnp.stack(out)


def attend(mixed, state, info, rows):
    atts, dens = [], []
    for b in range(2):
        rq, rk, v, _, _ = qkv_of(mixed, b, rows)
        s = jnp.einsum("tha,uha->htu", rq.astype(BF), rk.astype(BF), preferred_element_type=F32)
        w = (s * info["mask"][b][None]).astype(BF)
        num = jnp.einsum("htu,uhe->the", w, v.astype(BF), preferred_element_type=F32)
        den = jnp.sum(w.astype(F32), axis=2).T
        kv, ks = unpack_state(state[b])
        f = jnp.stack([info["fbcos"][b], info["fbsin"][b]])
        qf = (f[:, :, None, None] * rq[None]).astype(BF)
        num = num + jnp.einsum("stha,shae->the", qf, kv.astype(BF), preferred_element_type=F32)
        den = den + jnp.sum(qf.astype(F32) * ks[:, None], axis=(0, 3))
        inv = 1.0 / (den + 1.0)
        atts.append((num * inv[:, :, None]).astype(BF).reshape(rows, -1))
        dens.append(jnp.broadcast_to(inv[:, :, None], num.shape).reshape(rows, -1))
    return jnp.concatenate(atts), jnp.concatenate(dens)


def state_grad(mixed, gatt, att, inv, info, rows):
    out = []
    for b in range(2):
        rq, _, _, _, _ = qkv_of(mixed, b, rows)
        gnum = heads_of(gatt, b, rows) * heads_of(inv, b, rows)
        e = jnp.sum(gnum * heads_of(att, b, rows).astype(F32), axis=2)
        f = jnp.stack([info["fbcos"][b], info["fbsin"][b]])
        qf = (f[:, :, None, None] * rq[None]).astype(BF)
        gkv = jnp.einsum("stha,the->shae", qf, gnum.astype(BF), preferred_element_type=F32)
        gks = -jnp.sum(qf.astype(F32) * e[None, :, :, None], axis=1)
        out.append(pack_state(gkv, gks))
    return jnp.stack(out)


def attend_back(mixed, gatt, att, inv, state, gstate, info, rows):
    out = []
    for b in range(2):
        rq, rk, v, q, k = qkv_of(mixed, b, rows)
        gnum = heads_of(gatt, b, rows) * heads_of(inv, b, rows)
        e = jnp.sum(gnum * heads_of(att, b, rows).astype(F32), axis=2)
        gn, vb, rqb, rkb = gnum.astype(BF), v.astype(BF), rq.astype(BF), rk.astype(BF)
        s = jnp.einsum("tha,uha->htu", rqb, rkb, preferred_element_type=F32)
        w = (s * info["mask"][b][None]).astype(BF)
        gw = jnp.einsum("the,uhe->htu", gn, vb, preferred_element_type=F32) - e.T[:, :, None]
        gs = (gw * info["mask"][b][None]).astype(BF)
        gq = jnp.einsum("htu,uha->tha", gs, rkb, preferred_element_type=F32)
        gk = jnp.einsum("htu,tha->uha", gs, rqb, preferred_element_type=F32)
        gv = jnp.einsum("htu,the->uhe", w, gn, preferred_element_type=F32)
        kv, ks = unpack_state(state[b])
        f = jnp.stack([info["fbcos"][b], info["fbsin"][b]])
        gqf = jnp.einsum("the,shae->stha", gn, kv.astype(BF), preferred_element_type=F32)
        gqf = gqf - e[None, :, :, None] * ks[:, None]
        gq = gq + jnp.sum(f[:, :, None, None] * gqf, axis=0)
        gkv, gks = unpack_state(gstate[b])
        m = jnp.stack([info["memcos"][b], info["memsin"][b]])
        gkf = jnp.einsum("uhe,shae->suha", vb, gkv.astype(BF), preferred_element_type=F32) + gks[:, None]
        gk = gk + jnp.sum(m[:, :, None, None] * gkf, axis=0)
        kf = (m[:, :, None, None] * rk[None]).astype(BF)
        gv = gv + jnp.einsum("suha,shae->uhe", kf, gkv.astype(BF), preferred_element_type=F32)
        gq = jnp.where(q > 0, gq, 0.0)
        gk = jnp.where(k > 0, gk, 0.0)
        out.append(jnp.concatenate([g.reshape(rows, -1) for g in (gq, gk, gv)], axis=1))
    return jnp.concatenate(out).astype(BF)


def regroup(states, mask, roll):
    own, other = states
    if mask & 1:
        own, other = other, own
    if roll is True:
        return jnp.roll(own, HD, axis=-1), jnp.roll(other, HD, axis=-1)
    if roll is False:
        return own, other
    return tuple(jnp.where(roll, jnp.roll(x, HD, axis=-1), x) for x in (own, other))


def exchange(states, shift, roll, flags):
    first = regroup([shift(x, 1) for x in states], 1, roll)
    second = regroup([shift(x, 2) for x in states], 2, True)
    scale = [f.astype(F32)[:, None, None, None] for f in flags]
    return [
        (a.astype(F32) * scale[0] + b.astype(F32) * scale[1]).astype(BF)
        for a, b in zip(first, second)
    ]


def shards(
    layer_input,
    doc_lengths,
    ln1_gain,
    ln1_bias,
    qkv_weight,
    out_weight,
    ln2_gain,
    ln2_bias,
    in_weight,
    down_weight,
    cotangent,
):
    batches, rows, width = layer_input.shape
    layers = qkv_weight.shape[0]
    n_dp = lax.axis_size("dp")
    d, h = lax.axis_index("dp"), lax.axis_index("head")
    block = width // n_dp
    groups = xor_groups(n_dp)
    order = block_order(groups)
    tokens = batches * rows

    first_row = h * rows
    info = {k: [] for k in ("memcos", "memsin", "fbcos", "fbsin", "mask")}
    from1, from2, to1, to2 = [], [], [], []
    for b in range(batches):
        lengths = doc_lengths[b]
        position = first_row + jnp.arange(rows, dtype=jnp.int32)
        doc, start, size = places(lengths, position)
        angle = math.pi / 2 * (position - start).astype(F32) / size.astype(F32)
        cos, sin = jnp.cos(angle), jnp.sin(angle)
        edges = jnp.stack(
            [first_row - rows - 1, first_row - 1, first_row, first_row + rows - 1, first_row + rows, first_row + 2 * rows]
        )
        at, _, _ = places(lengths, edges)
        from1.append((h >= 1) & (at[1] == at[2]))
        from2.append((h >= 2) & (at[0] == at[2]))
        to1.append((h <= 2) & (at[3] == at[4]))
        to2.append((h <= 1) & (at[3] == at[5]))
        fb = (doc == at[2]).astype(F32)
        mem = (doc == at[3]).astype(F32)
        same = (doc[:, None] == doc[None, :]) & (position[:, None] >= position[None, :])
        info["mask"].append(
            jnp.where(same, cos[:, None] * cos[None, :] + sin[:, None] * sin[None, :], 0.0)
        )
        for name, weight in (("mem", mem), ("fb", fb)):
            info[name + "cos"].append(weight * cos)
            info[name + "sin"].append(weight * sin)
    from1, from2, to1, to2 = [jnp.stack(f) for f in (from1, from2, to1, to2)]

    target = jnp.arange(width)
    source = (jnp.array(order)[target // block] ^ d) * block + target % block
    permutation = (jnp.arange(width)[:, None] == source[None, :]).astype(BF)
    x = dot(layer_input.reshape(tokens, width), permutation)
    cot = dot(cotangent.reshape(tokens, width), permutation)

    params = jnp.concatenate([ln1_gain, ln1_bias, ln2_gain, ln2_bias], axis=0)[None]
    for masks in groups:
        params = spread(params, "dp", masks, 0)
    params = params.transpose(1, 0, 2).reshape(4, layers, width).astype(F32)

    weights = []
    for l in range(layers):
        qkvo = jnp.concatenate([qkv_weight[l], out_weight[l].T], axis=1)
        one = gather(qkvo, groups, pair_columns, "x")
        two = gather(in_weight[l], groups, plain_columns, "y")
        three = gather(down_weight[l].T, groups, plain_columns, "x")
        weights.append((one, two, three))

    saved = []
    stream = x
    q3 = 3 * 6 * HD
    for l in range(layers):
        qkvo, w_in, w_down = weights[l]
        w_qkv = [w[:, :q3] for w in qkvo]
        w_out = [w[:, q3:] for w in qkvo]
        normed1, stats1 = norm(stream, params[0, l], params[1, l])
        mixed = [dot(normed1, w).astype(BF) for w in w_qkv]
        states = [local_state(m, info, rows) for m in mixed]
        state = exchange(states, forward_shift, h == 2, (from1, from2))
        att, inv = zip(*[attend(m, s, info, rows) for m, s in zip(mixed, state)])
        mid = stream + sum(dot_t(a, w) for a, w in zip(att, w_out))
        normed2, stats2 = norm(mid, params[2, l], params[3, l])
        act, slope = zip(*[gelu_and_slope(dot(normed2, w)) for w in w_in])
        out = mid + sum(dot_t(a, w) for a, w in zip(act, w_down))
        saved.append((stream, normed1, stats1, mixed, state, att, inv, mid, normed2, stats2, act, slope, w_qkv, w_out, w_in, w_down))
        stream = out

    layer_output = dot_t(stream.astype(BF), permutation).astype(BF).reshape(layer_input.shape)

    grad = cot
    grads = [None] * layers
    norm_grads = [None] * layers
    for l in reversed(range(layers)):
        (stream, normed1, stats1, mixed, state, att, inv, mid, normed2, stats2, act, slope, w_qkv, w_out, w_in, w_down) = saved[l]
        low = grad.astype(BF)
        down_g = reduce_scatter(t_dot(low, act[0]), t_dot(low, act[1]), groups, split_plain, "x")
        gpre = [(dot(low, w) * s.astype(F32)).astype(BF) for w, s in zip(w_down, slope)]
        in_g = reduce_scatter(t_dot(normed2, gpre[0]), t_dot(normed2, gpre[1]), groups, split_plain, "y")
        gn2 = sum(dot_t(g, w) for g, w in zip(gpre, w_in))
        back, gain2_g, bias2_g = norm_back(mid, stats2, params[2, l], gn2)
        grad = grad + back
        low = grad.astype(BF)
        out_g = reduce_scatter(t_dot(low, att[0]), t_dot(low, att[1]), groups, split_pairs, "x")
        gatt = [dot(low, w) for w in w_out]
        gstates = [state_grad(m, g, a, i, info, rows) for m, g, a, i in zip(mixed, gatt, att, inv)]
        gstate = exchange(gstates, backward_shift, h == 1, (to1, to2))
        gmixed = [
            attend_back(m, g, a, i, s, gs, info, rows)
            for m, g, a, i, s, gs in zip(mixed, gatt, att, inv, state, gstate)
        ]
        qkv_g = reduce_scatter(t_dot(normed1, gmixed[0]), t_dot(normed1, gmixed[1]), groups, split_pairs, "y")
        gn1 = sum(dot_t(g, w) for g, w in zip(gmixed, w_qkv))
        back, gain1_g, bias1_g = norm_back(stream, stats1, params[0, l], gn1)
        grad = grad + back
        grads[l] = (qkv_g, out_g.T, in_g, down_g.T)
        norm_grads[l] = (gain1_g, bias1_g, gain2_g, bias2_g)

    high = lax.reduce_precision(grad, 8, 7)
    input_grad = dot_t(high.astype(BF), permutation) + dot_t((grad - high).astype(BF), permutation)
    input_grad = input_grad.reshape(layer_input.shape)

    small = jnp.stack([norm_grads[l][i] for i in range(4) for l in range(layers)])
    small = small + swap(small, "head", 1)
    small = small + swap(small, "head", 2)
    small = small.reshape(4 * layers, n_dp, block).transpose(1, 0, 2)
    for masks in groups[::-1]:
        count = small.shape[0] // (len(masks) + 1)
        total = small[:count]
        for j, m in enumerate(masks):
            total = total + swap(small[(j + 1) * count : (j + 2) * count], "dp", m)
        small = total
    part = block // lax.axis_size("head")
    small = lax.dynamic_slice_in_dim(small.reshape(4, layers, block), h * part, part, 2)

    qkv_grad, out_grad, in_grad, down_grad = [jnp.stack([grads[l][i] for l in range(layers)]) for i in range(4)]
    return (
        layer_output,
        input_grad,
        small[0],
        small[1],
        qkv_grad,
        out_grad,
        small[2],
        small[3],
        in_grad,
        down_grad,
    )


def solution(mesh):
    in_specs = (
        P("dp", "head", None),
        P("dp", None),
        P(None, "dp"),
        P(None, "dp"),
        P(None, "dp", "head"),
        P(None, "head", "dp"),
        P(None, "dp"),
        P(None, "dp"),
        P(None, "dp", "head"),
        P(None, "head", "dp"),
        P("dp", "head", None),
    )
    out_specs = (
        P("dp", "head", None),
        P("dp", "head", None),
        P(None, ("dp", "head")),
        P(None, ("dp", "head")),
        P(None, "dp", "head"),
        P(None, "head", "dp"),
        P(None, ("dp", "head")),
        P(None, ("dp", "head")),
        P(None, "dp", "head"),
        P(None, "head", "dp"),
    )
    return jax.shard_map(shards, mesh=mesh, in_specs=in_specs, out_specs=out_specs, check_vma=False)
```

time: 2480 us -> 1220 us (0.49)
  waiting for transfers between devices: 749 us -> 214 us
  matrix products: 826 us -> 372 us
  blocking collectives: 422 us -> 0 us
  starting transfers between devices: 2.26 us -> 155 us
  local copies, waits for them, and re-layouts: 212 us -> 294 us
  other arithmetic: 195 us -> 147 us
  loops' own time: 33.3 us -> 0 us
    reduce_scatter x10 -> x0, waiting for transfers between devices: 697 us -> none  [the longest x2 319 us: shards(): lax.psum_scatter(down_term, 'dp', scatter_dimension=1, tiled=True)]
    dot_general x128 -> x148, matrix products: 826 us -> 372 us  [the longest x18 82.6 us: dot_t(): lax.dot_general(a, b, (((1,), (1,)), ((), ())), preferred_element_type=F32)]
    all_gather x20 -> x0, blocking collectives: 331 us -> none  [the longest x8 125 us: entering(): lax.all_gather(a.astype(kind), axis)]
    ppermute x0 -> x110, waiting for transfers between devices: none -> 214 us  [the longest x94 191 us: swap(): return lax.ppermute(x, axis, [(i, i ^ mask) for i in range(n)])]
    ppermute x0 -> x110, starting transfers between devices: none -> 155 us  [the longest x94 118 us: swap(): return lax.ppermute(x, axis, [(i, i ^ mask) for i in range(n)])]
    unnamed x4 -> x0, blocking collectives: 91 us -> none
    dynamic_slice x50 -> x0, local copies, waits for them, and re-layouts: 55.3 us -> none  [the longest x48 55.2 us: hop(): part[at].astype(own.dtype)]
    concatenate x0 -> x32, local copies, waits for them, and re-layouts: none -> 53.1 us  [the longest x6 25.3 us: pair_columns(): return jnp.concatenate(pieces, axis=1)]
  transfers between devices with their start and end apart: 24 -> 110, of which waited for: 10 -> 37; matrix products, arithmetic and copies ran while one was open for 44% -> 58% of each run, Pallas kernels for 0% -> 0%
where the time goes in v1:
time: 1220 us; the launch traced here: 1200 us
  matrix products  372 us (30%)
  local copies, waits for them, and re-layouts  294 us (24%)
  waiting for transfers between devices  214 us (18%)
  starting transfers between devices  155 us (13%)
  other arithmetic  147 us (12%)
  between operations  17.5 us (1%)
    ppermute x94, waiting for transfers between devices, swap(): return lax.ppermute(x, axis, [(i, i ^ mask) for i in range(n)])  191 us
    ppermute x94, starting transfers between devices, swap(): return lax.ppermute(x, axis, [(i, i ^ mask) for i in range(n)])  118 us
    dot_general x18, matrix products, dot_t(): lax.dot_general(a, b, (((1,), (1,)), ((), ())), preferred_element_type=F32)  82.6 us
    dot_general x18, matrix products, dot(): lax.dot_general(a, b, (((1,), (0,)), ((), ())), preferred_element_type=F32)  76.1 us
    dot_general x16, matrix products, t_dot(): lax.dot_general(a, b, (((0,), (0,)), ((), ())), preferred_element_type=F32)  70.9 us
    unnamed x838, local copies, waits for them, and re-layouts  55.4 us
    dot_general x8, matrix products, attend_back(): gv = jnp.einsum('htu,the->uhe', w, gn, preferred_element_type=F32)  28.6 us
    dot_general x8, matrix products, attend(): jnp.einsum('tha,uha->htu', rq.astype(BF), rk.astype(BF), preferred_elemen...  28.5 us
  transfers between devices with their start and end apart: 110, of which 37 were waited for; matrix products, arithmetic and copies ran while one was open for 58% of the time, Pallas kernels for 0%

profile of v1, /device:TPU:0, one launch (start us, length us, event | category | flops | bytes accessed | tf_op | source)
XLA Modules:
  0.0 1198.3 jit_solution(1947410688964051580)
XLA Ops:
  2.1 5.0 collective-permute-start.2
  84.9 7.5 collective-permute-start.37
  95.7 8.6 collective-permute-done.41
  111.9 5.9 collective-permute-done.42
  128.1 21.4 %collective-permute-done.29 = bf16[384,768]{1,0:T(8,128)(2,1)S(1)} collective-permute-done((bf16[384,768]{1,0:T(8,128)(2,1)S(1)}, bf16[384,768]{1,0:T(8,128)(2,1)S(1)}, u32[]{:S(2)}, u32[]{:S(2)}) %collective-permute-start.29) | collective-permute-done | bytes 589856 | tf_op jit(solution)/shard_map/ppermute | solution.py:26
  150.1 12.1 %collective-permute-done.7 = bf16[384,768]{1,0:T(8,128)(2,1)S(1)} collective-permute-done((bf16[384,768]{1,0:T(8,128)(2,1)S(1)}, bf16[384,768]{1,0:T(8,128)(2,1)S(1)}, u32[]{:S(2)}, u32[]{:S(2)}) %collective-permute-start.7) | collective-permute-done | bytes 589856 | tf_op jit(solution)/shard_map/ppermute | solution.py:26
  166.4 8.4 collective-permute-done.22
  181.0 10.1 collective-permute-done.30
  193.5 22.9 %collective-permute-done.8 = bf16[768,768]{1,0:T(8,128)(2,1)S(1)} collective-permute-done((bf16[768,768]{1,0:T(8,128)(2,1)S(1)}, bf16[768,768]{1,0:T(8,128)(2,1)S(1)}, u32[]{:S(2)}, u32[]{:S(2)}) %collective-permute-start.8) | collective-permute-done | bytes 1179680 | tf_op jit(solution)/shard_map/ppermute | solution.py:26
  219.5 6.0 concatenate.492
  225.6 5.4 concatenate.491
  232.2 6.0 concatenate.523
  238.2 5.3 concatenate.522
  291.6 14.4 %pad_maximum_fusion.2 = bf16[768,1536]{1,0:T(8,128)(2,1)} fusion(bf16[384,1536]{1,0:T(8,128)(2,1)} %collective-permute-done.40, bf16[384,768]{1,0:T(8,128)(2,1)S(1)} %copy-done.176, bf16[96,768]{1,0:T(8,128)(2,1)S(1)} %copy-done.217, bf16[96,768]{1,0:T(8,128)(2,1)S(1)} %copy-done.220, bf16[96,768]{1,0:T(8,128)(2,1)S(1)} %copy-done.223, ...), kind=kLoop, calls=%fused_computation.143 | loop fusion | flops 14155776 | bytes 4718592 | tf_op jit(solution)/shard_map/concatenate | solution.py:47
  306.0 5.1 pad_maximum_fusion
  363.2 4.4 convert_reduce_fusion.4
  379.5 7.3 collective-permute-start.10
  427.2 5.0 fusion.476
  432.2 5.3 fusion.409
  437.6 6.3 fusion.406
  443.9 4.6 fusion.472
  498.7 5.0 collective-permute-start.35
  589.4 4.9 fusion.477
  594.3 4.5 convolution_convert_fusion.4
  598.8 7.6 multiply_convert_fusion.10
  621.4 7.5 multiply_convert_fusion.11
  628.9 6.1 multiply_reduce_fusion
  702.3 6.2 fusion.407
  708.5 10.7 fusion.43
  766.9 13.6 %convolution_convert_fusion.8 = bf16[768,1152]{1,0:T(8,128)(2,1)} fusion(bf16[1024,768]{0,1:T(8,128)(2,1)S(1)} %copy-done.208, bf16[512,384]{0,1:T(8,128)(2,1)S(1)} %bitcast.1360, bf16[512,384]{0,1:T(8,128)(2,1)S(1)} %bitcast.1378, bf16[512,384]{0,1:T(8,128)(2,1)S(1)} %bitcast.1372, bf16[512,384]{0,1:T(8,128)(2,1)S(1)} %bitcast.1364, ...), kind=kOutput, calls=%fused_computation.96 | convolution fusion | flops 1826979840 | bytes 5701632 | tf_op jit(solution)/shard_map/dot_general | solution.py:143
  788.9 4.7 convolution_convert_fusion.5
  793.6 7.8 multiply_convert_fusion.4
  805.3 7.3 multiply_convert_fusion.5
  812.7 5.5 fusion.480
  818.3 10.0 multiply_reduce_fusion.1
  894.8 11.9 collective-permute-done.53
  941.4 14.2 %convolution_convert_fusion.9 = bf16[768,1152]{1,0:T(8,128)(2,1)} fusion(bf16[1024,768]{0,1:T(8,128)(2,1)S(1)} %copy-done.202, bf16[512,384]{0,1:T(8,128)(2,1)S(1)} %bitcast.1358, bf16[512,384]{0,1:T(8,128)(2,1)S(1)} %bitcast.1380, bf16[512,384]{0,1:T(8,128)(2,1)S(1)} %bitcast.1370, bf16[512,384]{0,1:T(8,128)(2,1)S(1)} %bitcast.1362, ...), kind=kOutput, calls=%fused_computation.97 | convolution fusion | flops 1826979840 | bytes 5701632 | tf_op jit(solution)/shard_map/dot_general | solution.py:143
  959.6 4.5 multiply_reduce_fusion.3
  965.5 6.3 multiply_add_fusion
  991.9 5.4 collective-permute-done.81
  1040.7 5.3 convert_add_fusion
  1100.2 15.2 %collective-permute-done.105 = bf16[768,768]{1,0:T(8,128)(2,1)S(1)} collective-permute-done((bf16[768,768]{1,0:T(8,128)(2,1)}, bf16[768,768]{1,0:T(8,128)(2,1)S(1)}, u32[]{:S(2)}, u32[]{:S(2)}) %collective-permute-start.105) | collective-permute-done | bytes 1179680 | tf_op jit(solution)/shard_map/ppermute | solution.py:26
  1124.9 15.7 %collective-permute-done.99 = bf16[768,768]{1,0:T(8,128)(2,1)S(1)} collective-permute-done((bf16[768,768]{1,0:T(8,128)(2,1)}, bf16[768,768]{1,0:T(8,128)(2,1)S(1)}, u32[]{:S(2)}, u32[]{:S(2)}) %collective-permute-start.99) | collective-permute-done | bytes 1179680 | tf_op jit(solution)/shard_map/ppermute | solution.py:26
  1145.6 7.7 collective-permute-done.94
  1158.0 6.4 collective-permute-done.108
  1164.5 11.5 collective-permute-done.96
  1176.3 5.1 collective-permute-start.91
  1187.0 6.8 collective-permute-done.90
  (1682 shorter events, 786.7 us)
Async XLA Ops:
  2.1 49.6 %collective-permute-start.2 = (bf16[1,8,96]{2,1,0:T(8,128)(2,1)}, bf16[1,8,96]{2,1,0:T(8,128)(2,1)}, u32[]{:S(2)}, u32[]{:S(2)}) collective-permute-start(bf16[1,8,96]{2,1,0:T(8,128)(2,1)} %maximum_bitcast_fusion), channel_id=1, source_target_pairs={{0,24},{4,28},{8,16},{12,20},{16,8},{20,12},{24,0},{28,4},{1,25},{... | collective-permute-start | bytes 4616 | tf_op jit(solution)/shard_map/ppermute | solution.py:26
  7.1 47.5 %collective-permute-start.1 = (bf16[1,8,96]{2,1,0:T(8,128)(2,1)}, bf16[1,8,96]{2,1,0:T(8,128)(2,1)}, u32[]{:S(2)}, u32[]{:S(2)}) collective-permute-start(bf16[1,8,96]{2,1,0:T(8,128)(2,1)} %maximum_bitcast_fusion), channel_id=1, source_target_pairs={{0,16},{4,20},{8,24},{12,28},{16,0},{20,4},{24,8},{28,12},{1,17},{... | collective-permute-start | bytes 4616 | tf_op jit(solution)/shard_map/ppermute | solution.py:26
  7.1 47.5 %collective-permute-start = (bf16[1,8,96]{2,1,0:T(8,128)(2,1)}, bf16[1,8,96]{2,1,0:T(8,128)(2,1)}, u32[]{:S(2)}, u32[]{:S(2)}) collective-permute-start(bf16[1,8,96]{2,1,0:T(8,128)(2,1)} %maximum_bitcast_fusion), channel_id=1, source_target_pairs={{0,8},{4,12},{8,0},{12,4},{16,24},{20,28},{24,16},{28,20},{1,9},{5... | collective-permute-start | bytes 4616 | tf_op jit(solution)/shard_map/ppermute | solution.py:26
  9.4 83.1 %collective-permute-start.16 = (bf16[96,768]{1,0:T(8,128)(2,1)S(1)}, bf16[96,768]{1,0:T(8,128)(2,1)}, u32[]{:S(2)}, u32[]{:S(2)}) collective-permute-start(bf16[96,768]{1,0:T(8,128)(2,1)S(1)} %get-tuple-element.283), channel_id=1, source_target_pairs={{0,24},{4,28},{8,16},{12,20},{16,8},{20,12},{24,0},{28,4},{1,25},{... | collective-permute-start | bytes 442376 | tf_op jit(solution)/shard_map/ppermute | solution.py:26
  13.2 79.3 %collective-permute-start.15 = (bf16[96,768]{1,0:T(8,128)(2,1)S(1)}, bf16[96,768]{1,0:T(8,128)(2,1)}, u32[]{:S(2)}, u32[]{:S(2)}) collective-permute-start(bf16[96,768]{1,0:T(8,128)(2,1)S(1)} %get-tuple-element.283), channel_id=1, source_target_pairs={{0,16},{4,20},{8,24},{12,28},{16,0},{20,4},{24,8},{28,12},{1,17},{... | collective-permute-start | bytes 442376 | tf_op jit(solution)/shard_map/ppermute | solution.py:26
  81.9 23.5 %collective-permute-start.38 = (bf16[96,768]{1,0:T(8,128)(2,1)S(1)}, bf16[96,768]{1,0:T(8,128)(2,1)S(1)}, u32[]{:S(2)}, u32[]{:S(2)}) collective-permute-start(bf16[96,768]{1,0:T(8,128)(2,1)S(1)} %copy-done.168), channel_id=1, source_target_pairs={{0,24},{4,28},{8,16},{12,20},{16,8},{20,12},{24,0},{28,4},{1,25},{... | collective-permute-start | bytes 442376 | tf_op jit(solution)/shard_map/ppermute | solution.py:26
  84.9 24.7 %collective-permute-start.37 = (bf16[96,768]{1,0:T(8,128)(2,1)S(1)}, bf16[96,768]{1,0:T(8,128)(2,1)S(1)}, u32[]{:S(2)}, u32[]{:S(2)}) collective-permute-start(bf16[96,768]{1,0:T(8,128)(2,1)S(1)} %copy-done.168), channel_id=1, source_target_pairs={{0,16},{4,20},{8,24},{12,28},{16,0},{20,4},{24,8},{28,12},{1,17},{... | collective-permute-start | bytes 442376 | tf_op jit(solution)/shard_map/ppermute | solution.py:26
  117.8 44.9 %collective-permute-start.17 = (bf16[384,768]{1,0:T(8,128)(2,1)S(1)}, bf16[384,768]{1,0:T(8,128)(2,1)S(1)}, u32[]{:S(2)}, u32[]{:S(2)}) collective-permute-start(bf16[384,768]{1,0:T(8,128)(2,1)S(1)} %pad_maximum_fusion.27), channel_id=1, source_target_pairs={{0,2},{1,3},{2,0},{3,1},{4,6},{5,7},{6,4},{7,5},{8,10},{9,11},{10,... | collective-permute-start | bytes 1769480 | tf_op jit(solution)/shard_map/ppermute | solution.py:26
  120.7 55.5 %collective-permute-start.44 = (bf16[384,768]{1,0:T(8,128)(2,1)S(1)}, bf16[384,768]{1,0:T(8,128)(2,1)S(1)}, u32[]{:S(2)}, u32[]{:S(2)}) collective-permute-start(bf16[384,768]{1,0:T(8,128)(2,1)S(1)} %pad_maximum_fusion.31), channel_id=1, source_target_pairs={{0,4},{4,0},{8,12},{12,8},{16,20},{20,16},{24,28},{28,24},{1,5},{5... | collective-permute-start | bytes 1769480 | tf_op jit(solution)/shard_map/ppermute | solution.py:26
  122.4 27.1 %collective-permute-start.29 = (bf16[384,768]{1,0:T(8,128)(2,1)S(1)}, bf16[384,768]{1,0:T(8,128)(2,1)S(1)}, u32[]{:S(2)}, u32[]{:S(2)}) collective-permute-start(bf16[384,768]{1,0:T(8,128)(2,1)S(1)} %pad_maximum_fusion.29), channel_id=1, source_target_pairs={{0,4},{4,0},{8,12},{12,8},{16,20},{20,16},{24,28},{28,24},{1,5},{5... | collective-permute-start | bytes 1769480 | tf_op jit(solution)/shard_map/ppermute | solution.py:26
  122.9 39.2 %collective-permute-start.7 = (bf16[384,768]{1,0:T(8,128)(2,1)S(1)}, bf16[384,768]{1,0:T(8,128)(2,1)S(1)}, u32[]{:S(2)}, u32[]{:S(2)}) collective-permute-start(bf16[384,768]{1,0:T(8,128)(2,1)S(1)} %pad_maximum_fusion.26), channel_id=1, source_target_pairs={{0,4},{4,0},{8,12},{12,8},{16,20},{20,16},{24,28},{28,24},{1,5},{5... | collective-permute-start | bytes 1769480 | tf_op jit(solution)/shard_map/ppermute | solution.py:26
  126.5 48.3 %collective-permute-start.22 = (bf16[384,768]{1,0:T(8,128)(2,1)S(1)}, bf16[384,768]{1,0:T(8,128)(2,1)S(1)}, u32[]{:S(2)}, u32[]{:S(2)}) collective-permute-start(bf16[384,768]{1,0:T(8,128)(2,1)S(1)} %pad_maximum_fusion.28), channel_id=1, source_target_pairs={{0,4},{4,0},{8,12},{12,8},{16,20},{20,16},{24,28},{28,24},{1,5},{5... | collective-permute-start | bytes 1769480 | tf_op jit(solution)/shard_map/ppermute | solution.py:26
  149.5 141.6 %collective-permute-start.40 = (bf16[384,1536]{1,0:T(8,128)(2,1)}, bf16[384,1536]{1,0:T(8,128)(2,1)}, u32[]{:S(2)}, u32[]{:S(2)}) collective-permute-start(bf16[384,1536]{1,0:T(8,128)(2,1)} %pad_maximum_fusion.5), channel_id=1, source_target_pairs={{0,4},{4,0},{8,12},{12,8},{16,20},{20,16},{24,28},{28,24},{1,5},{5... | collective-permute-start | bytes 3538952 | tf_op jit(solution)/shard_map/ppermute | solution.py:26
  162.2 28.9 %collective-permute-start.30 = (bf16[768,768]{1,0:T(8,128)(2,1)S(1)}, bf16[768,768]{1,0:T(8,128)(2,1)S(1)}, u32[]{:S(2)}, u32[]{:S(2)}) collective-permute-start(bf16[768,768]{1,0:T(8,128)(2,1)S(1)} %constant_dynamic-update-slice_fusion.15), channel_id=1, source_target_pairs={{0,2},{1,3},{2,0},{3,1},{4,6},{5,7},{6,4},{7,5},{8,10},{9,11},{10,... | collective-permute-start | bytes 3538952 | tf_op jit(solution)/shard_map/ppermute | solution.py:26
  162.8 53.6 %collective-permute-start.8 = (bf16[768,768]{1,0:T(8,128)(2,1)S(1)}, bf16[768,768]{1,0:T(8,128)(2,1)S(1)}, u32[]{:S(2)}, u32[]{:S(2)}) collective-permute-start(bf16[768,768]{1,0:T(8,128)(2,1)S(1)} %constant_dynamic-update-slice_fusion), channel_id=1, source_target_pairs={{0,2},{1,3},{2,0},{3,1},{4,6},{5,7},{6,4},{7,5},{8,10},{9,11},{10,... | collective-permute-start | bytes 3538952 | tf_op jit(solution)/shard_map/ppermute | solution.py:26
  174.8 131.2 %collective-permute-start.18 = (bf16[384,1536]{1,0:T(8,128)(2,1)}, bf16[384,1536]{1,0:T(8,128)(2,1)}, u32[]{:S(2)}, u32[]{:S(2)}) collective-permute-start(bf16[384,1536]{1,0:T(8,128)(2,1)} %pad_maximum_fusion.4), channel_id=1, source_target_pairs={{0,4},{4,0},{8,12},{12,8},{16,20},{20,16},{24,28},{28,24},{1,5},{5... | collective-permute-start | bytes 3538952 | tf_op jit(solution)/shard_map/ppermute | solution.py:26
  176.2 86.4 %collective-permute-start.23 = (bf16[768,768]{1,0:T(8,128)(2,1)}, bf16[768,768]{1,0:T(8,128)(2,1)}, u32[]{:S(2)}, u32[]{:S(2)}) collective-permute-start(bf16[768,768]{1,0:T(8,128)(2,1)} %constant_dynamic-update-slice_fusion.10), channel_id=1, source_target_pairs={{0,2},{1,3},{2,0},{3,1},{4,6},{5,7},{6,4},{7,5},{8,10},{9,11},{10,... | collective-permute-start | bytes 3538952 | tf_op jit(solution)/shard_map/ppermute | solution.py:26
  191.1 65.4 %collective-permute-start.45 = (bf16[768,768]{1,0:T(8,128)(2,1)}, bf16[768,768]{1,0:T(8,128)(2,1)}, u32[]{:S(2)}, u32[]{:S(2)}) collective-permute-start(bf16[768,768]{1,0:T(8,128)(2,1)} %constant_dynamic-update-slice_fusion.20), channel_id=1, source_target_pairs={{0,2},{1,3},{2,0},{3,1},{4,6},{5,7},{6,4},{7,5},{8,10},{9,11},{10,... | collective-permute-start | bytes 3538952 | tf_op jit(solution)/shard_map/ppermute | solution.py:26
  243.5 206.6 %collective-permute-start.31 = (bf16[768,1536]{1,0:T(8,128)(2,1)}, bf16[768,1536]{1,0:T(8,128)(2,1)}, u32[]{:S(2)}, u32[]{:S(2)}) collective-permute-start(bf16[768,1536]{1,0:T(8,128)(2,1)} %concatenate.523), channel_id=1, source_target_pairs={{0,1},{1,0},{2,3},{3,2},{4,5},{5,4},{6,7},{7,6},{8,9},{9,8},{10,11... | collective-permute-start | bytes 7077896 | tf_op jit(solution)/shard_map/ppermute | solution.py:26
  256.4 54.7 %collective-permute-start.9 = (bf16[768,1536]{1,0:T(8,128)(2,1)}, bf16[768,1536]{1,0:T(8,128)(2,1)}, u32[]{:S(2)}, u32[]{:S(2)}) collective-permute-start(bf16[768,1536]{1,0:T(8,128)(2,1)} %concatenate.492), channel_id=1, source_target_pairs={{0,1},{1,0},{2,3},{3,2},{4,5},{5,4},{6,7},{7,6},{8,9},{9,8},{10,11... | collective-permute-start | bytes 7077896 | tf_op jit(solution)/shard_map/ppermute | solution.py:26
  265.9 171.7 %collective-permute-start.25 = (bf16[768,1536]{1,0:T(8,128)(2,1)}, bf16[768,1536]{1,0:T(8,128)(2,1)}, u32[]{:S(2)}, u32[]{:S(2)}) collective-permute-start(bf16[768,1536]{1,0:T(8,128)(2,1)} %pad_maximum_fusion.1), channel_id=1, source_target_pairs={{0,1},{1,0},{2,3},{3,2},{4,5},{5,4},{6,7},{7,6},{8,9},{9,8},{10,11... | collective-permute-start | bytes 7077896 | tf_op jit(solution)/shard_map/ppermute | solution.py:26
  291.1 307.8 %collective-permute-start.47 = (bf16[768,1536]{1,0:T(8,128)(2,1)}, bf16[768,1536]{1,0:T(8,128)(2,1)}, u32[]{:S(2)}, u32[]{:S(2)}) collective-permute-start(bf16[768,1536]{1,0:T(8,128)(2,1)} %pad_maximum_fusion.3), channel_id=1, source_target_pairs={{0,1},{1,0},{2,3},{3,2},{4,5},{5,4},{6,7},{7,6},{8,9},{9,8},{10,11... | collective-permute-start | bytes 7077896 | tf_op jit(solution)/shard_map/ppermute | solution.py:26
  306.0 283.4 %collective-permute-start.46 = (bf16[768,1536]{1,0:T(8,128)(2,1)}, bf16[768,1536]{1,0:T(8,128)(2,1)}, u32[]{:S(2)}, u32[]{:S(2)}) collective-permute-start(bf16[768,1536]{1,0:T(8,128)(2,1)} %pad_maximum_fusion.2), channel_id=1, source_target_pairs={{0,1},{1,0},{2,3},{3,2},{4,5},{5,4},{6,7},{7,6},{8,9},{9,8},{10,11... | collective-permute-start | bytes 7077896 | tf_op jit(solution)/shard_map/ppermute | solution.py:26
  387.5 39.7 %collective-permute-start.24 = (bf16[768,1536]{1,0:T(8,128)(2,1)}, bf16[768,1536]{1,0:T(8,128)(2,1)}, u32[]{:S(2)}, u32[]{:S(2)}) collective-permute-start(bf16[768,1536]{1,0:T(8,128)(2,1)} %pad_maximum_fusion), channel_id=1, source_target_pairs={{0,1},{1,0},{2,3},{3,2},{4,5},{5,4},{6,7},{7,6},{8,9},{9,8},{10,11... | collective-permute-start | bytes 7077896 | tf_op jit(solution)/shard_map/ppermute | solution.py:26
  498.7 51.3 %collective-permute-start.35 = (bf16[2,3,144,128]{3,2,1,0:T(8,128)(2,1)}, bf16[2,3,144,128]{3,2,1,0:T(8,128)(2,1)}, u32[]{:S(2)}, u32[]{:S(2)}) collective-permute-start(bf16[2,3,144,128]{3,2,1,0:T(8,128)(2,1)} %get-tuple-element.353), channel_id=1, source_target_pairs={{0,2},{1,3},{4,6},{5,7},{8,10},{9,11},{12,14},{13,15},{16,18},{17,... | collective-permute-start | bytes 663560 | tf_op jit(solution)/shard_map/ppermute | solution.py:31
  503.6 53.1 %collective-permute-start.32 = (bf16[2,3,144,128]{3,2,1,0:T(8,128)(2,1)}, bf16[2,3,144,128]{3,2,1,0:T(8,128)(2,1)S(1)}, u32[]{:S(2)}, u32[]{:S(2)}) collective-permute-start(bf16[2,3,144,128]{3,2,1,0:T(8,128)(2,1)} %get-tuple-element.353), channel_id=1, source_target_pairs={{0,1},{1,2},{2,3},{4,5},{5,6},{6,7},{8,9},{9,10},{10,11},{12,13},{... | collective-permute-start | bytes 663560 | tf_op jit(solution)/shard_map/ppermute | solution.py:31
  676.5 43.6 %collective-permute-start.51 = (bf16[2,3,144,128]{3,2,1,0:T(8,128)(2,1)}, bf16[2,3,144,128]{3,2,1,0:T(8,128)(2,1)}, u32[]{:S(2)}, u32[]{:S(2)}) collective-permute-start(bf16[2,3,144,128]{3,2,1,0:T(8,128)(2,1)} %get-tuple-element.351), channel_id=1, source_target_pairs={{2,0},{3,1},{6,4},{7,5},{10,8},{11,9},{14,12},{15,13},{18,16},{19,... | collective-permute-start | bytes 663560 | tf_op jit(solution)/shard_map/ppermute | solution.py:36
  677.8 45.9 %collective-permute-start.48 = (bf16[2,3,144,128]{3,2,1,0:T(8,128)(2,1)}, bf16[2,3,144,128]{3,2,1,0:T(8,128)(2,1)S(1)}, u32[]{:S(2)}, u32[]{:S(2)}) collective-permute-start(bf16[2,3,144,128]{3,2,1,0:T(8,128)(2,1)} %get-tuple-element.351), channel_id=1, source_target_pairs={{1,0},{2,1},{3,2},{5,4},{6,5},{7,6},{9,8},{10,9},{11,10},{13,12},{... | collective-permute-start | bytes 663560 | tf_op jit(solution)/shard_map/ppermute | solution.py:36
  679.1 43.4 %collective-permute-start.50 = (bf16[2,3,144,128]{3,2,1,0:T(8,128)(2,1)}, bf16[2,3,144,128]{3,2,1,0:T(8,128)(2,1)}, u32[]{:S(2)}, u32[]{:S(2)}) collective-permute-start(bf16[2,3,144,128]{3,2,1,0:T(8,128)(2,1)} %get-tuple-element.352), channel_id=1, source_target_pairs={{1,0},{2,1},{3,2},{5,4},{6,5},{7,6},{9,8},{10,9},{11,10},{13,12},{... | collective-permute-start | bytes 663560 | tf_op jit(solution)/shard_map/ppermute | solution.py:36
  680.4 40.9 %collective-permute-start.49 = (bf16[2,3,144,128]{3,2,1,0:T(8,128)(2,1)}, bf16[2,3,144,128]{3,2,1,0:T(8,128)(2,1)}, u32[]{:S(2)}, u32[]{:S(2)}) collective-permute-start(bf16[2,3,144,128]{3,2,1,0:T(8,128)(2,1)} %get-tuple-element.352), channel_id=1, source_target_pairs={{2,0},{3,1},{6,4},{7,5},{10,8},{11,9},{14,12},{15,13},{18,16},{19,... | collective-permute-start | bytes 663560 | tf_op jit(solution)/shard_map/ppermute | solution.py:36
  685.2 347.7 %collective-permute-start.92 = (bf16[768,1536]{1,0:T(8,128)(2,1)}, bf16[768,1536]{1,0:T(8,128)(2,1)}, u32[]{:S(2)}, u32[]{:S(2)}) collective-permute-start(bf16[768,1536]{1,0:T(8,128)(2,1)} %convolution_convert_fusion.6), channel_id=1, source_target_pairs={{0,1},{1,0},{2,3},{3,2},{4,5},{5,4},{6,7},{7,6},{8,9},{9,8},{10,11... | collective-permute-start | bytes 7077896 | tf_op jit(solution)/shard_map/ppermute | solution.py:26
  720.1 265.2 %collective-permute-start.80 = (bf16[768,384]{0,1:T(8,128)(2,1)}, bf16[768,384]{0,1:T(8,128)(2,1)}, u32[]{:S(2)}, u32[]{:S(2)}) collective-permute-start(bf16[768,384]{0,1:T(8,128)(2,1)} %convolution_convert_fusion.10), channel_id=1, source_target_pairs={{0,1},{1,0},{2,3},{3,2},{4,5},{5,4},{6,7},{7,6},{8,9},{9,8},{10,11... | collective-permute-start | bytes 1769480 | tf_op jit(solution)/shard_map/ppermute | solution.py:26
  871.4 35.5 %collective-permute-start.52 = (bf16[2,3,144,128]{3,2,1,0:T(8,128)(2,1)S(1)}, bf16[2,3,144,128]{3,2,1,0:T(8,128)(2,1)S(1)}, u32[]{:S(2)}, u32[]{:S(2)}) collective-permute-start(bf16[2,3,144,128]{3,2,1,0:T(8,128)(2,1)S(1)} %get-tuple-element.349), channel_id=1, source_target_pairs={{1,0},{2,1},{3,2},{5,4},{6,5},{7,6},{9,8},{10,9},{11,10},{13,12},{... | collective-permute-start | bytes 663560 | tf_op jit(solution)/shard_map/ppermute | solution.py:36
  878.2 28.6 %collective-permute-start.54 = (bf16[2,3,144,128]{3,2,1,0:T(8,128)(2,1)S(1)}, bf16[2,3,144,128]{3,2,1,0:T(8,128)(2,1)S(1)}, u32[]{:S(2)}, u32[]{:S(2)}) collective-permute-start(bf16[2,3,144,128]{3,2,1,0:T(8,128)(2,1)S(1)} %get-tuple-element.350), channel_id=1, source_target_pairs={{1,0},{2,1},{3,2},{5,4},{6,5},{7,6},{9,8},{10,9},{11,10},{13,12},{... | collective-permute-start | bytes 663560 | tf_op jit(solution)/shard_map/ppermute | solution.py:36
  984.1 40.9 %collective-permute-start.68 = (bf16[768,1152]{1,0:T(8,128)(2,1)S(1)}, bf16[768,1152]{1,0:T(8,128)(2,1)S(1)}, u32[]{:S(2)}, u32[]{:S(2)}) collective-permute-start(bf16[768,1152]{1,0:T(8,128)(2,1)S(1)} %copy-done.384), channel_id=1, source_target_pairs={{0,1},{1,0},{2,3},{3,2},{4,5},{5,4},{6,7},{7,6},{8,9},{9,8},{10,11... | collective-permute-start | bytes 5308424 | tf_op jit(solution)/shard_map/ppermute | solution.py:26
  985.3 42.9 %collective-permute-start.62 = (bf16[768,1152]{1,0:T(8,128)(2,1)S(1)}, bf16[768,1152]{1,0:T(8,128)(2,1)S(1)}, u32[]{:S(2)}, u32[]{:S(2)}) collective-permute-start(bf16[768,1152]{1,0:T(8,128)(2,1)S(1)} %copy-done.385), channel_id=1, source_target_pairs={{0,1},{1,0},{2,3},{3,2},{4,5},{5,4},{6,7},{7,6},{8,9},{9,8},{10,11... | collective-permute-start | bytes 5308424 | tf_op jit(solution)/shard_map/ppermute | solution.py:26
  1024.2 24.1 %collective-permute-start.86 = (bf16[768,1536]{1,0:T(8,128)(2,1)S(1)}, bf16[768,1536]{1,0:T(8,128)(2,1)S(1)}, u32[]{:S(2)}, u32[]{:S(2)}) collective-permute-start(bf16[768,1536]{1,0:T(8,128)(2,1)S(1)} %copy-done.383), channel_id=1, source_target_pairs={{0,1},{1,0},{2,3},{3,2},{4,5},{5,4},{6,7},{7,6},{8,9},{9,8},{10,11... | collective-permute-start | bytes 7077896 | tf_op jit(solution)/shard_map/ppermute | solution.py:26
  1025.0 28.7 %collective-permute-start.98 = (bf16[768,1536]{1,0:T(8,128)(2,1)S(1)}, bf16[768,1536]{1,0:T(8,128)(2,1)S(1)}, u32[]{:S(2)}, u32[]{:S(2)}) collective-permute-start(bf16[768,1536]{1,0:T(8,128)(2,1)S(1)} %copy-done.382), channel_id=1, source_target_pairs={{0,1},{1,0},{2,3},{3,2},{4,5},{5,4},{6,7},{7,6},{8,9},{9,8},{10,11... | collective-permute-start | bytes 7077896 | tf_op jit(solution)/shard_map/ppermute | solution.py:26
  1028.2 30.1 %collective-permute-start.69 = (bf16[384,1152]{1,0:T(8,128)(2,1)S(1)}, bf16[384,1152]{1,0:T(8,128)(2,1)S(1)}, u32[]{:S(2)}, u32[]{:S(2)}) collective-permute-start(bf16[384,1152]{1,0:T(8,128)(2,1)S(1)} %slice.2005), channel_id=1, source_target_pairs={{0,4},{4,0},{8,12},{12,8},{16,20},{20,16},{24,28},{28,24},{1,5},{5... | collective-permute-start | bytes 2654216 | tf_op jit(solution)/shard_map/ppermute | solution.py:26
  1032.9 37.0 %collective-permute-start.63 = (bf16[384,1152]{1,0:T(8,128)(2,1)}, bf16[384,1152]{1,0:T(8,128)(2,1)}, u32[]{:S(2)}, u32[]{:S(2)}) collective-permute-start(bf16[384,1152]{1,0:T(8,128)(2,1)} %slice.2006), channel_id=1, source_target_pairs={{0,4},{4,0},{8,12},{12,8},{16,20},{20,16},{24,28},{28,24},{1,5},{5... | collective-permute-start | bytes 2654216 | tf_op jit(solution)/shard_map/ppermute | solution.py:26
  1047.2 48.8 %collective-permute-start.93 = (bf16[384,1536]{1,0:T(8,128)(2,1)}, bf16[384,1536]{1,0:T(8,128)(2,1)}, u32[]{:S(2)}, u32[]{:S(2)}) collective-permute-start(bf16[384,1536]{1,0:T(8,128)(2,1)} %slice.2003), channel_id=1, source_target_pairs={{0,4},{4,0},{8,12},{12,8},{16,20},{20,16},{24,28},{28,24},{1,5},{5... | collective-permute-start | bytes 3538952 | tf_op jit(solution)/shard_map/ppermute | solution.py:26
  1086.2 29.2 %collective-permute-start.105 = (bf16[768,768]{1,0:T(8,128)(2,1)}, bf16[768,768]{1,0:T(8,128)(2,1)S(1)}, u32[]{:S(2)}, u32[]{:S(2)}) collective-permute-start(bf16[768,768]{1,0:T(8,128)(2,1)} %slice.2001), channel_id=1, source_target_pairs={{0,2},{1,3},{2,0},{3,1},{4,6},{5,7},{6,4},{7,5},{8,10},{9,11},{10,... | collective-permute-start | bytes 3538952 | tf_op jit(solution)/shard_map/ppermute | solution.py:26
  1088.2 35.2 %collective-permute-start.87 = (bf16[384,1536]{1,0:T(8,128)(2,1)}, bf16[384,1536]{1,0:T(8,128)(2,1)S(1)}, u32[]{:S(2)}, u32[]{:S(2)}) collective-permute-start(bf16[384,1536]{1,0:T(8,128)(2,1)} %slice.2004), channel_id=1, source_target_pairs={{0,4},{4,0},{8,12},{12,8},{16,20},{20,16},{24,28},{28,24},{1,5},{5... | collective-permute-start | bytes 3538952 | tf_op jit(solution)/shard_map/ppermute | solution.py:26
  1092.9 47.7 %collective-permute-start.99 = (bf16[768,768]{1,0:T(8,128)(2,1)}, bf16[768,768]{1,0:T(8,128)(2,1)S(1)}, u32[]{:S(2)}, u32[]{:S(2)}) collective-permute-start(bf16[768,768]{1,0:T(8,128)(2,1)} %slice.2002), channel_id=1, source_target_pairs={{0,2},{1,3},{2,0},{3,1},{4,6},{5,7},{6,4},{7,5},{8,10},{9,11},{10,... | collective-permute-start | bytes 3538952 | tf_op jit(solution)/shard_map/ppermute | solution.py:26
  1117.5 24.9 %collective-permute-start.106 = (bf16[384,768]{1,0:T(8,128)(2,1)S(1)}, bf16[384,768]{1,0:T(8,128)(2,1)S(1)}, u32[]{:S(2)}, u32[]{:S(2)}) collective-permute-start(bf16[384,768]{1,0:T(8,128)(2,1)S(1)} %slice.2007), channel_id=1, source_target_pairs={{0,4},{4,0},{8,12},{12,8},{16,20},{20,16},{24,28},{28,24},{1,5},{5... | collective-permute-start | bytes 1769480 | tf_op jit(solution)/shard_map/ppermute | solution.py:26
  1118.8 34.5 %collective-permute-start.94 = (bf16[384,768]{1,0:T(8,128)(2,1)S(1)}, bf16[384,768]{1,0:T(8,128)(2,1)S(1)}, u32[]{:S(2)}, u32[]{:S(2)}) collective-permute-start(bf16[384,768]{1,0:T(8,128)(2,1)S(1)} %slice.2009), channel_id=1, source_target_pairs={{0,2},{1,3},{2,0},{3,1},{4,6},{5,7},{6,4},{7,5},{8,10},{9,11},{10,... | collective-permute-start | bytes 1769480 | tf_op jit(solution)/shard_map/ppermute | solution.py:26
  1123.8 52.3 %collective-permute-start.88 = (bf16[384,768]{1,0:T(8,128)(2,1)S(1)}, bf16[384,768]{1,0:T(8,128)(2,1)S(1)}, u32[]{:S(2)}, u32[]{:S(2)}) collective-permute-start(bf16[384,768]{1,0:T(8,128)(2,1)S(1)} %slice.2010), channel_id=1, source_target_pairs={{0,2},{1,3},{2,0},{3,1},{4,6},{5,7},{6,4},{7,5},{8,10},{9,11},{10,... | collective-permute-start | bytes 1769480 | tf_op jit(solution)/shard_map/ppermute | solution.py:26
  1141.1 40.9 %collective-permute-start.100 = (bf16[384,768]{1,0:T(8,128)(2,1)S(1)}, bf16[384,768]{1,0:T(8,128)(2,1)S(1)}, u32[]{:S(2)}, u32[]{:S(2)}) collective-permute-start(bf16[384,768]{1,0:T(8,128)(2,1)S(1)} %slice.2008), channel_id=1, source_target_pairs={{0,4},{4,0},{8,12},{12,8},{16,20},{20,16},{24,28},{28,24},{1,5},{5... | collective-permute-start | bytes 1769480 | tf_op jit(solution)/shard_map/ppermute | solution.py:26
  (473 other events, 4198.9 us)

commit v2 on v1

v2 whole, which is shorter than its diff:
```python
from functools import partial
import math

import jax
import jax.numpy as jnp
from jax import lax
from jax.experimental import pallas as pl
from jax.experimental.pallas import tpu as pltpu
from jax.sharding import PartitionSpec as P

HD = 64
ROW = 2048
NORM_EPS = 1e-05
BF = jnp.bfloat16
F32 = jnp.float32


def xor_groups(n):
    groups, span = [[1]], 2
    while span < n:
        radix = min(4, n // span)
        groups.append([span * k for k in range(1, radix)])
        span *= radix
    return groups[::-1]


def swap(x, axis, mask):
    n = lax.axis_size(axis)
    return lax.ppermute(x, axis, [(i, i ^ mask) for i in range(n)])


def forward_shift(x, by):
    n = lax.axis_size("head")
    return lax.ppermute(x, "head", [(i, i + by) for i in range(n - by)])


def backward_shift(x, by):
    n = lax.axis_size("head")
    return lax.ppermute(x, "head", [(i + by, i) for i in range(n - by)])


def block_order(groups):
    order = [0]
    for masks in groups:
        order = order + [r ^ m for m in masks for r in order]
    return order


def spread(x, axis, masks, dim):
    return jnp.concatenate([x] + [swap(x, axis, m) for m in masks], axis=dim)


def pair_columns(own, other):
    heads = own.shape[1] // (4 * HD)
    pieces = []
    for part, j in [(part, j) for j in range(heads) for part in range(3)] + [(3, j) for j in range(heads)]:
        at = (part * heads + j) * HD
        pieces += [own[:, at : at + HD], other[:, at : at + HD]]
    return jnp.concatenate(pieces, axis=1)


def split_pairs(parts, x):
    heads = x.shape[1] // (2 * HD * parts)
    starts = [(j * parts + part) * 2 * HD for part in range(parts) for j in range(heads)]
    return tuple(
        jnp.concatenate([x[:, at + side : at + side + HD] for at in starts], axis=1) for side in (0, HD)
    )


def split_plain(x):
    c = x.shape[1] // 2
    return x[:, :c], x[:, c:]


class Transfers:
    def __init__(self, steps):
        self.steps, self.coming, self.result = steps, None, None
        self.wanted = next(steps)

    def give(self, arrived):
        try:
            self.wanted = self.steps.send(arrived)
        except StopIteration as end:
            self.wanted, self.result = [], end.value


def finish(value, chains):
    while True:
        chains = [chain for chain in chains if chain.result is None]
        if not chains:
            return value
        value = advance(value, *chains)


def shift_steps(state, shift):
    arrived = yield [(state, lambda array: shift(array, 1)), (state, lambda array: shift(array, 2))]
    return arrived


def together(values):
    return lax.optimization_barrier(values)


def start(*chains):
    for chain in chains:
        chain.coming = [exchange(array) for array, exchange in chain.wanted]


def advance(value, *chains):
    value, arrived = together((value, [chain.coming for chain in chains]))
    for chain, pieces in zip(chains, arrived):
        chain.give(pieces)
    value, sends = together((value, [[array for array, _ in chain.wanted] for chain in chains]))
    for chain, arrays in zip(chains, sends):
        chain.coming = [exchange(array) for array, (_, exchange) in zip(arrays, chain.wanted)]
    return value


def to(axis, mask):
    return lambda array: swap(array, axis, mask)


def spread_steps(x, masks):
    arrived = yield [(x, to("dp", m)) for m in masks]
    return jnp.concatenate([x] + arrived, axis=0)


def outer_steps(x, groups):
    for masks in groups[:-1]:
        x = yield from spread_steps(x, masks)
    return x


def heads_steps(shard, groups):
    x = yield from outer_steps(shard, groups)
    masks = groups[-1]
    c = x.shape[1] // 2
    qk, vo = x[:, :c], x[:, c:]
    arrived = yield [(qk, to("dp", m)) for m in masks] + [(vo, to("head", 2))]
    qk = jnp.concatenate([qk] + arrived[:-1], axis=0)
    vo = jnp.concatenate([vo, arrived[-1]], axis=1)
    arrived = yield [(qk, to("head", 2))] + [(vo, to("dp", m)) for m in masks]
    vo = jnp.concatenate([vo] + arrived[1:], axis=0)
    own = jnp.concatenate([qk, vo[:, :c]], axis=1)
    other = jnp.concatenate([arrived[0], vo[:, c:]], axis=1)
    half = pair_columns(own, other)
    arrived = yield [(half, to("head", 1))]
    return half, arrived[0]


def hidden_steps(shard, groups):
    x = yield from outer_steps(shard, groups)
    masks = groups[-1]
    c = x.shape[1] // 2
    up, down = x[:, :c], x[:, c:]
    arrived = yield [(up, to("dp", m)) for m in masks] + [(down, to("head", 2))]
    up = jnp.concatenate([up] + arrived[:-1], axis=0)
    down = jnp.concatenate([down, arrived[-1]], axis=1)
    arrived = yield [(up, to("head", 2))] + [(down, to("dp", m)) for m in masks]
    up = jnp.concatenate([up, arrived[0]], axis=1)
    down = jnp.concatenate([down] + arrived[1:], axis=0)
    arrived = yield [(up, to("head", 1)), (down, to("head", 1))]
    return (up, arrived[0]), (down, arrived[1])


def row_steps(x, masks):
    rows = x.shape[0] // (len(masks) + 1)
    arrived = yield [(x[(j + 1) * rows : (j + 2) * rows].astype(BF), to("dp", m)) for j, m in enumerate(masks)]
    return x[:rows].astype(F32) + sum(piece.astype(F32) for piece in arrived)


def sum_steps(left, right, groups, split, first):
    c = right.shape[1] // 2
    arrived = yield [(t_dot(left, right[:, c:]).astype(BF), to("head", 1))]
    total = t_dot(left, right[:, :c]) + arrived[0].astype(F32)
    rest = groups[::-1]
    if first == "y":
        total = yield from row_steps(total, rest[0])
        rest = rest[1:]
    keep, send = split(total)
    arrived = yield [(send.astype(BF), to("head", 2))]
    total = keep + arrived[0].astype(F32)
    for masks in rest:
        total = yield from row_steps(total, masks)
    return total


def dot(a, b):
    return lax.dot_general(a, b, (((1,), (0,)), ((), ())), preferred_element_type=F32)


def dot_t(a, b):
    return lax.dot_general(a, b, (((1,), (1,)), ((), ())), preferred_element_type=F32)


def t_dot(a, b):
    return lax.dot_general(a, b, (((0,), (0,)), ((), ())), preferred_element_type=F32)


def places(lengths, position):
    n = lengths.shape[0]
    upto = jnp.arange(n)[:, None] <= jnp.arange(n)[None, :]
    ends = jnp.sum(jnp.where(upto, lengths[:, None], 0), axis=0)
    passed = (position[:, None] >= ends[None, :]).astype(jnp.int32)
    doc = jnp.sum(passed, axis=1)
    start = jnp.sum(passed * lengths[None, :], axis=1)
    here = (doc[:, None] == jnp.arange(n)[None, :]).astype(jnp.int32)
    size = jnp.sum(here * lengths[None, :], axis=1)
    return doc, start, size


STATE_ROWS = 144
PAIR = 2 * HD
QKV = 3 * PAIR
VMEM_LIMIT = 56 * 2**20


def run(kernel, grid, ins, outs, scratch=(), flops=0, size=0, name=None):
    in_specs, arrays = [], []
    for array, block, index in ins:
        arrays.append(array)
        if block is None:
            in_specs.append(pl.BlockSpec(memory_space=index))
        else:
            in_specs.append(pl.BlockSpec(block, index))
    return pl.pallas_call(
        kernel,
        grid=grid,
        in_specs=in_specs,
        out_specs=[pl.BlockSpec(block, index) for _, _, block, index in outs],
        out_shape=[jax.ShapeDtypeStruct(shape, dtype) for shape, dtype, _, _ in outs],
        scratch_shapes=list(scratch),
        compiler_params=pltpu.CompilerParams(
            dimension_semantics=("arbitrary",) * len(grid), vmem_limit_bytes=VMEM_LIMIT
        ),
        cost_estimate=pl.CostEstimate(flops=int(flops), bytes_accessed=int(size), transcendentals=0),
        name=name,
    )(*arrays)


def low_lanes(shape):
    return lax.broadcasted_iota(jnp.int32, shape, 1) < HD


def relu(x):
    return jnp.maximum(x, jnp.zeros_like(x))


def moments(x):
    mean = jnp.mean(x, axis=-1, keepdims=True)
    centred = x - mean
    rstd = lax.rsqrt(jnp.mean(centred * centred, axis=-1, keepdims=True) + NORM_EPS)
    return centred * rstd, rstd


def project_kernel(row, x_ref, par_ref, own_ref, other_ref, normed_ref, mixed_ref):
    xhat, _ = moments(x_ref[...])
    normed = (xhat * par_ref[row : row + 1, :] + par_ref[row + 2 : row + 3, :]).astype(BF)
    normed_ref[...] = normed
    half = own_ref.shape[1]
    mixed_ref[:, :half] = dot(normed, own_ref[...]).astype(BF)
    mixed_ref[:, half:] = dot(normed, other_ref[...]).astype(BF)


def project(x, params, row, own, other):
    tokens, width = x.shape
    half = 3 * width // 2
    rows = min(256, tokens)
    return run(
        partial(project_kernel, row),
        (tokens // rows,),
        [
            (x, (rows, width), lambda i: (i, 0)),
            (params, params.shape, lambda i: (0, 0)),
            (own, (width, half), lambda i: (0, 0)),
            (other, (width, half), lambda i: (0, 0)),
        ],
        [
            ((tokens, width), BF, (rows, width), lambda i: (i, 0)),
            ((tokens, 2 * half), BF, (rows, 2 * half), lambda i: (i, 0)),
        ],
        flops=2 * tokens * width * 2 * half,
        size=tokens * width * 6 + tokens * half * 4 + width * half * 4,
        name="project",
    )


def packed(c, s, c_sum, s_sum):
    lo = low_lanes((HD, PAIR))
    first = jnp.where(lo, c[:HD], c[HD:])
    second = jnp.where(lo, s[:HD], s[HD:])
    at = lax.broadcasted_iota(jnp.int32, (STATE_ROWS - PAIR, PAIR), 0)
    sums = jnp.where(at == 0, c_sum, jnp.where(at == 1, s_sum, 0.0))
    return jnp.concatenate([first, second, sums], axis=0).astype(BF)


def unpacked(st):
    lo = low_lanes((HD, PAIR))
    both = []
    for at in (0, HD):
        x = st[at : at + HD]
        both.append(jnp.concatenate([jnp.where(lo, x, 0.0), jnp.where(lo, 0.0, x)], axis=0))
    return both[0], both[1], st[PAIR : PAIR + 1], st[PAIR + 1 : PAIR + 2]


def received(near_ref, far_ref, flag_ref, b):
    near = near_ref[0, 0].astype(F32)
    far = far_ref[0, 0].astype(F32)
    return (
        near * flag_ref[b, 0]
        + pltpu.roll(near, HD, 1) * flag_ref[b, 1]
        + pltpu.roll(far, HD, 1) * flag_ref[b, 2]
    )


def state_kernel(col_ref, mixed_ref, out_ref):
    k = relu(mixed_ref[:, PAIR : 2 * PAIR]).astype(F32)
    v = mixed_ref[:, 2 * PAIR :]
    kc = (k * col_ref[:, 2:3]).astype(BF)
    ks = (k * col_ref[:, 3:4]).astype(BF)
    out_ref[0, 0] = packed(
        t_dot(kc, v),
        t_dot(ks, v),
        jnp.sum(kc.astype(F32), axis=0, keepdims=True),
        jnp.sum(ks.astype(F32), axis=0, keepdims=True),
    )


def pair_grid(mixed, rows):
    tokens, width = mixed.shape
    return (tokens // rows, width // QKV)


def local_state(mixed, col, rows):
    grid = pair_grid(mixed, rows)
    return run(
        state_kernel,
        grid,
        [
            (col, (rows, col.shape[1]), lambda b, p: (b, 0)),
            (mixed, (rows, QKV), lambda b, p: (b, p)),
        ],
        [(grid + (STATE_ROWS, PAIR), BF, (1, 1, STATE_ROWS, PAIR), lambda b, p: (b, p, 0, 0))],
        flops=4 * mixed.shape[0] * mixed.shape[1] * PAIR,
        size=mixed.size * 2,
        name="local_state",
    )[0]


def mask_of(col_ref, row_ref):
    rows = col_ref.shape[0]
    shape = (rows, rows)
    t = lax.broadcasted_iota(jnp.int32, shape, 0)
    u = lax.broadcasted_iota(jnp.int32, shape, 1)
    cosine = col_ref[:, 4:5] * row_ref[0:1, :] + col_ref[:, 5:6] * row_ref[1:2, :]
    same = col_ref[:, 6:7] == row_ref[2:3, :]
    return cosine, same, t, u


def attend_kernel(flag_ref, col_ref, row_ref, mixed_ref, near_ref, far_ref, att_ref, inv_ref, mask_ref):
    b, p = pl.program_id(0), pl.program_id(1)
    rows = mixed_ref.shape[0]

    @pl.when(p == 0)
    def _():
        cosine, same, t, u = mask_of(col_ref, row_ref)
        mask_ref[...] = jnp.where(same & (t >= u), cosine, 0.0)

    c, s, c_sum, s_sum = unpacked(received(near_ref, far_ref, flag_ref, b))
    q, k, v = [relu(mixed_ref[:, i * PAIR : (i + 1) * PAIR]) if i < 2 else mixed_ref[:, 2 * PAIR :] for i in range(3)]
    lo = low_lanes((rows, PAIR))
    qf = q.astype(F32)
    qc, qs = qf * col_ref[:, 0:1], qf * col_ref[:, 1:2]
    inter = dot(jnp.concatenate([qc, qs], axis=1).astype(BF), jnp.concatenate([c, s], axis=0).astype(BF))
    ones = jnp.where(
        (lax.broadcasted_iota(jnp.int32, (PAIR, PAIR), 0) < HD) == low_lanes((PAIR, PAIR)), 1.0, 0.0
    ).astype(BF)
    inter_den = dot((qc * c_sum + qs * s_sum).astype(BF), ones)
    zero = jnp.zeros_like(q)
    q_of = [jnp.where(lo, q, zero), jnp.where(lo, zero, q)]
    v_one = jnp.concatenate([v, jnp.ones_like(v)], axis=1)
    step = min(256, rows)
    for at in range(0, rows, step):
        end = at + step
        here = slice(at, end)
        mask = mask_ref[here, :end]
        parts = []
        for head in range(2):
            w = (dot_t(q_of[head][here], k[:end]) * mask).astype(BF)
            parts.append(dot(w, v_one[:end]))
        pick = low_lanes((step, PAIR))
        num = jnp.where(pick, parts[0][:, :PAIR], parts[1][:, :PAIR]) + inter[here]
        den = jnp.where(pick, parts[0][:, PAIR:], parts[1][:, PAIR:]) + inter_den[here]
        inv = 1.0 / (den + 1.0)
        att_ref[here, :] = (num * inv).astype(BF)
        inv_ref[here, :] = inv


def attend(mixed, near, far, flags, col, row, rows):
    grid = pair_grid(mixed, rows)
    tokens = mixed.shape[0]
    pairs = grid[1]
    width = pairs * PAIR
    half = pairs // 2
    return run(
        attend_kernel,
        grid,
        [
            (flags, None, pltpu.SMEM),
            (col, (rows, col.shape[1]), lambda b, p: (b, 0)),
            (row, (row.shape[0], rows), lambda b, p: (0, b)),
            (mixed, (rows, QKV), lambda b, p: (b, p)),
            (near, (1, 1, STATE_ROWS, PAIR), lambda b, p: (b, lax.rem(p + half, pairs), 0, 0)),
            (far, (1, 1, STATE_ROWS, PAIR), lambda b, p: (b, p, 0, 0)),
        ],
        [
            ((tokens, width), BF, (rows, PAIR), lambda b, p: (b, p)),
            ((tokens, width), F32, (rows, PAIR), lambda b, p: (b, p)),
        ],
        scratch=[pltpu.VMEM((rows, rows), F32)],
        flops=2 * tokens * rows * pairs * 2 * 256,
        size=mixed.size * 2 + tokens * width * 6,
        name="attend",
    )


def gelu_and_slope(x):
    c = math.sqrt(2.0 / math.pi)
    k = 0.044715 * c
    x2 = x * x
    half = 0.5 + 0.5 * jnp.tanh(x * (c + k * x2))
    act = x * half
    slope = half + act * (1.0 - half) * (2.0 * c + (6.0 * k) * x2)
    return act.astype(BF), slope.astype(BF)


def hidden_kernel(
    row, x_ref, par_ref, att_ref, oo_ref, ox_ref, io_ref, ix_ref, do_ref, dx_ref,
    mid_ref, normed_ref, act_ref, slope_ref, out_ref,
):
    step = pl.program_id(0)
    tokens = x_ref.shape[0]
    rows = min(256, tokens)
    half = oo_ref.shape[1]

    @pl.when(step == 0)
    def _():
        @pl.loop(0, tokens // rows)
        def _(i):
            here = pl.ds(i * rows, rows)
            mid = x_ref[here, :] + dot_t(att_ref[here, :half], oo_ref[...]) + dot_t(att_ref[here, half:], ox_ref[...])
            mid_ref[here, :] = mid
            xhat, _ = moments(mid)
            normed_ref[here, :] = (xhat * par_ref[row : row + 1, :] + par_ref[row + 2 : row + 3, :]).astype(BF)
            out_ref[here, :] = mid

    def part(in_ref, down_ref):
        @pl.loop(0, tokens // rows)
        def _(i):
            here = pl.ds(i * rows, rows)
            act, slope = gelu_and_slope(dot(normed_ref[here, :], in_ref[...]))
            act_ref[here, :] = act
            slope_ref[here, :] = slope
            out_ref[here, :] += dot_t(act, down_ref[...])

    last_own = pl.num_programs(0) // 2

    @pl.when(step < last_own)
    def _():
        part(io_ref, do_ref)

    @pl.when(step >= last_own)
    def _():
        part(ix_ref, dx_ref)


def own_step(n):
    return lambda i: (0, jnp.minimum(i, n - 1))


def other_step(n):
    return lambda i: (0, jnp.maximum(i - n, 0))


def hidden(x, params, row, att, w_att, w_in, w_down):
    tokens, width = x.shape
    units = 2 * w_in[0].shape[1]
    chunk = width
    n = units // chunk // 2
    o_at = w_att[0].shape[1] // (width // 2) - 1
    whole = lambda i: (0, 0)
    return run(
        partial(hidden_kernel, row),
        (2 * n,),
        [
            (x, (tokens, width), whole),
            (params, params.shape, whole),
            (att, (tokens, width), whole),
            (w_att[0], (width, width // 2), lambda i: (0, o_at)),
            (w_att[1], (width, width // 2), lambda i: (0, o_at)),
            (w_in[0], (width, chunk), own_step(n)),
            (w_in[1], (width, chunk), other_step(n)),
            (w_down[0], (width, chunk), own_step(n)),
            (w_down[1], (width, chunk), other_step(n)),
        ],
        [
            ((tokens, width), F32, (tokens, width), whole),
            ((tokens, width), BF, (tokens, width), whole),
            ((tokens, units), BF, (tokens, chunk), lambda i: (0, i)),
            ((tokens, units), BF, (tokens, chunk), lambda i: (0, i)),
            ((tokens, width), F32, (tokens, width), whole),
        ],
        flops=2 * tokens * width * (2 * units + width),
        size=tokens * width * 16 + tokens * units * 4 + width * units * 4,
        name="hidden",
    )


def hidden_back_kernel(
    row, g_ref, par_ref, mid_ref, slope_ref, io_ref, ix_ref, do_ref, dx_ref,
    gpre_ref, out_ref, norm_ref, low_ref, acc_ref,
):
    step = pl.program_id(0)
    tokens = g_ref.shape[0]
    rows = min(256, tokens)

    @pl.when(step == 0)
    def _():
        low_ref[...] = g_ref[...].astype(BF)
        acc_ref[...] = jnp.zeros_like(acc_ref)
        norm_ref[...] = jnp.zeros_like(norm_ref)

    def part(in_ref, down_ref):
        @pl.loop(0, tokens // rows)
        def _(i):
            here = pl.ds(i * rows, rows)
            gpre = (dot(low_ref[here, :], down_ref[...]) * slope_ref[here, :].astype(F32)).astype(BF)
            gpre_ref[here, :] = gpre
            acc_ref[here, :] += dot_t(gpre, in_ref[...])

    last_own = pl.num_programs(0) // 2

    @pl.when(step < last_own)
    def _():
        part(io_ref, do_ref)

    @pl.when(step >= last_own)
    def _():
        part(ix_ref, dx_ref)

    @pl.when(step == pl.num_programs(0) - 1)
    def _():
        @pl.loop(0, tokens // rows)
        def _(i):
            here = pl.ds(i * rows, rows)
            out_ref[here, :] = g_ref[here, :] + norm_gradient(
                acc_ref[here, :], mid_ref[here, :], par_ref[row : row + 1, :], norm_ref
            )


def norm_gradient(grad, stream, gain, norm_ref):
    xhat, rstd = moments(stream)
    gx = grad * xhat
    norm_ref[0:1, :] += jnp.sum(gx, axis=0, keepdims=True)
    norm_ref[1:2, :] += jnp.sum(grad, axis=0, keepdims=True)
    g = grad * gain
    return rstd * (
        g - jnp.mean(g, axis=-1, keepdims=True) - xhat * jnp.mean(gx * gain, axis=-1, keepdims=True)
    )


def hidden_back(grad, params, row, mid, slope, w_in, w_down):
    tokens, width = grad.shape
    units = slope.shape[1]
    chunk = width
    n = units // chunk // 2
    whole = lambda i: (0, 0)
    return run(
        partial(hidden_back_kernel, row),
        (2 * n,),
        [
            (grad, (tokens, width), whole),
            (params, params.shape, whole),
            (mid, (tokens, width), whole),
            (slope, (tokens, chunk), lambda i: (0, i)),
            (w_in[0], (width, chunk), own_step(n)),
            (w_in[1], (width, chunk), other_step(n)),
            (w_down[0], (width, chunk), own_step(n)),
            (w_down[1], (width, chunk), other_step(n)),
        ],
        [
            ((tokens, units), BF, (tokens, chunk), lambda i: (0, i)),
            ((tokens, width), F32, (tokens, width), whole),
            ((8, width), F32, (8, width), whole),
        ],
        scratch=[pltpu.VMEM((tokens, width), BF), pltpu.VMEM((tokens, width), F32)],
        flops=2 * tokens * width * 2 * units,
        size=tokens * width * 12 + tokens * units * 4 + width * units * 4,
        name="hidden_back",
    )


def head_ones():
    return jnp.where(
        (lax.broadcasted_iota(jnp.int32, (PAIR, PAIR), 0) < HD) == low_lanes((PAIR, PAIR)), 1.0, 0.0
    ).astype(BF)


def state_back_kernel(col_ref, g_ref, oo_ref, ox_ref, q_ref, att_ref, inv_ref, gn_ref, out_ref, low_ref):
    p = pl.program_id(1)

    @pl.when(p == 0)
    def _():
        low_ref[...] = g_ref[...].astype(BF)

    w = jnp.where(p < pl.num_programs(1) // 2, oo_ref[...], ox_ref[...])
    gn = (dot(low_ref[...], w) * inv_ref[...]).astype(BF)
    gn_ref[...] = gn
    e = dot((gn.astype(F32) * att_ref[...].astype(F32)).astype(BF), head_ones())
    q = relu(q_ref[...]).astype(F32)
    qc = (q * col_ref[:, 0:1]).astype(BF)
    qs = (q * col_ref[:, 1:2]).astype(BF)
    out_ref[0, 0] = packed(
        t_dot(qc, gn),
        t_dot(qs, gn),
        -jnp.sum(qc.astype(F32) * e, axis=0, keepdims=True),
        -jnp.sum(qs.astype(F32) * e, axis=0, keepdims=True),
    )


def state_back(grad, mixed, att, inv, w_att, col, rows):
    grid = pair_grid(mixed, rows)
    tokens, width = grad.shape
    pairs = grid[1]
    half = pairs // 2
    o_at = 3 * half
    return run(
        state_back_kernel,
        grid,
        [
            (col, (rows, col.shape[1]), lambda b, p: (b, 0)),
            (grad, (rows, width), lambda b, p: (b, 0)),
            (w_att[0], (width, PAIR), lambda b, p: (0, o_at + jnp.minimum(p, half - 1))),
            (w_att[1], (width, PAIR), lambda b, p: (0, o_at + jnp.maximum(p - half, 0))),
            (mixed, (rows, PAIR), lambda b, p: (b, 3 * p)),
            (att, (rows, PAIR), lambda b, p: (b, p)),
            (inv, (rows, PAIR), lambda b, p: (b, p)),
        ],
        [
            ((tokens, width), BF, (rows, PAIR), lambda b, p: (b, p)),
            (grid + (STATE_ROWS, PAIR), BF, (1, 1, STATE_ROWS, PAIR), lambda b, p: (b, p, 0, 0)),
        ],
        scratch=[pltpu.VMEM((rows, width), BF)],
        flops=2 * tokens * width * 2 * width,
        size=tokens * width * 14,
        name="state_back",
    )


def attend_back_kernel(
    flag_ref, back_flag_ref, col_ref, row_ref, mixed_ref, gn_ref, att_ref,
    near_ref, far_ref, gnear_ref, gfar_ref, out_ref, mask_ref, turned_ref,
):
    b, p = pl.program_id(0), pl.program_id(1)
    rows = mixed_ref.shape[0]

    @pl.when(p == 0)
    def _():
        cosine, same, t, u = mask_of(col_ref, row_ref)
        mask_ref[...] = jnp.where(same & (t >= u), cosine, 0.0)
        turned_ref[...] = jnp.where(same & (t <= u), cosine, 0.0)

    q = relu(mixed_ref[:, :PAIR])
    k = relu(mixed_ref[:, PAIR : 2 * PAIR])
    v = mixed_ref[:, 2 * PAIR :]
    gn = gn_ref[...]
    shape = (rows, PAIR)
    lo = low_lanes(shape)
    lane = lax.broadcasted_iota(jnp.int32, shape, 1)
    zero = jnp.zeros_like(q)
    e = dot((gn.astype(F32) * att_ref[...].astype(F32)).astype(BF), head_ones())
    v_one = jnp.concatenate([v, jnp.where(lane < 2, 1.0, 0.0).astype(BF)], axis=1)
    step = min(256, rows)
    gq_of, gk_of, gv_of = [], [], []
    for head in range(2):
        own = lo if head == 0 else ~lo
        k_own = jnp.where(own, k, zero)
        e_own = e if head == 0 else pltpu.roll(e, HD, 1)
        e_high = e_own.astype(BF)
        e_low = (e_own - e_high.astype(F32)).astype(BF)
        tail = jnp.where(lane == 0, -e_high, jnp.where(lane == 1, -e_low, zero))
        g_tail = jnp.concatenate([jnp.where(own, gn, zero), tail], axis=1)
        gq, gk, gv = [], [], []
        for at in range(0, rows, step):
            end = at + step
            gs = (dot_t(g_tail[at:end], v_one[:end]) * mask_ref[at:end, :end]).astype(BF)
            gq.append(dot(gs, k[:end]))
            turned = turned_ref[at:end, at:]
            w_t = (dot_t(k_own[at:end], q[at:]) * turned).astype(BF)
            gv.append(dot(w_t, gn[at:]))
            gs_t = (dot_t(v_one[at:end], g_tail[at:]) * turned).astype(BF)
            gk.append(dot(gs_t, q[at:]))
        gq_of.append(jnp.concatenate(gq, axis=0))
        gk_of.append(jnp.concatenate(gk, axis=0))
        gv_of.append(jnp.concatenate(gv, axis=0))

    c, s, c_sum, s_sum = unpacked(received(near_ref, far_ref, flag_ref, b))
    gc, gs, gc_sum, gs_sum = unpacked(received(gnear_ref, gfar_ref, back_flag_ref, b))
    gq = jnp.where(lo, gq_of[0], gq_of[1])
    gq += col_ref[:, 0:1] * (dot_t(gn, c.astype(BF)) - e * c_sum)
    gq += col_ref[:, 1:2] * (dot_t(gn, s.astype(BF)) - e * s_sum)
    gk = jnp.where(lo, gk_of[0], gk_of[1])
    gk += col_ref[:, 2:3] * (dot_t(v, gc.astype(BF)) + gc_sum)
    gk += col_ref[:, 3:4] * (dot_t(v, gs.astype(BF)) + gs_sum)
    kf = k.astype(F32)
    gv = jnp.where(lo, gv_of[0], gv_of[1])
    gv += dot((kf * col_ref[:, 2:3]).astype(BF), gc.astype(BF))
    gv += dot((kf * col_ref[:, 3:4]).astype(BF), gs.astype(BF))
    out_ref[:, :PAIR] = jnp.where(q > 0, gq, 0.0).astype(BF)
    out_ref[:, PAIR : 2 * PAIR] = jnp.where(k > 0, gk, 0.0).astype(BF)
    out_ref[:, 2 * PAIR :] = gv.astype(BF)


def attend_back(mixed, gn, att, near, far, gnear, gfar, flags, back_flags, col, row, rows):
    grid = pair_grid(mixed, rows)
    pairs = grid[1]
    half = pairs // 2
    state = (1, 1, STATE_ROWS, PAIR)
    direct = lambda b, p: (b, p, 0, 0)
    crossed = lambda b, p: (b, lax.rem(p + half, pairs), 0, 0)
    return run(
        attend_back_kernel,
        grid,
        [
            (flags, None, pltpu.SMEM),
            (back_flags, None, pltpu.SMEM),
            (col, (rows, col.shape[1]), lambda b, p: (b, 0)),
            (row, (row.shape[0], rows), lambda b, p: (0, b)),
            (mixed, (rows, QKV), lambda b, p: (b, p)),
            (gn, (rows, PAIR), lambda b, p: (b, p)),
            (att, (rows, PAIR), lambda b, p: (b, p)),
            (near, state, crossed),
            (far, state, direct),
            (gnear, state, crossed),
            (gfar, state, direct),
        ],
        [(mixed.shape, BF, (rows, QKV), lambda b, p: (b, p))],
        scratch=[pltpu.VMEM((rows, rows), F32), pltpu.VMEM((rows, rows), F32)],
        flops=6 * mixed.shape[0] * rows * pairs * 2 * 256,
        size=mixed.size * 4 + gn.size * 4,
        name="attend_back",
    )[0]


def project_back_kernel(row, gm_ref, own_ref, other_ref, x_ref, par_ref, g_ref, out_ref, norm_ref):
    @pl.when(pl.program_id(0) == 0)
    def _():
        norm_ref[...] = jnp.zeros_like(norm_ref)

    half = own_ref.shape[1]
    grad = dot_t(gm_ref[:, :half], own_ref[...]) + dot_t(gm_ref[:, half:], other_ref[...])
    out_ref[...] = g_ref[...] + norm_gradient(grad, x_ref[...], par_ref[row : row + 1, :], norm_ref)


def project_back(gmixed, own, other, x, params, row, grad):
    tokens, width = x.shape
    half = gmixed.shape[1] // 2
    rows = min(256, tokens)
    whole = lambda i: (0, 0)
    by_row = lambda i: (i, 0)
    return run(
        partial(project_back_kernel, row),
        (tokens // rows,),
        [
            (gmixed, (rows, 2 * half), by_row),
            (own, (width, half), whole),
            (other, (width, half), whole),
            (x, (rows, width), by_row),
            (params, params.shape, whole),
            (grad, (rows, width), by_row),
        ],
        [
            ((tokens, width), F32, (rows, width), by_row),
            ((8, width), F32, (8, width), whole),
        ],
        flops=2 * tokens * width * 2 * half,
        size=tokens * width * 12 + tokens * half * 4 + width * half * 4,
        name="project_back",
    )


def shards(
    layer_input,
    doc_lengths,
    ln1_gain,
    ln1_bias,
    qkv_weight,
    out_weight,
    ln2_gain,
    ln2_bias,
    in_weight,
    down_weight,
    cotangent,
):
    batches, rows, width = layer_input.shape
    layers = qkv_weight.shape[0]
    n_dp = lax.axis_size("dp")
    d, h = lax.axis_index("dp"), lax.axis_index("head")
    block = width // n_dp
    groups = xor_groups(n_dp)
    order = block_order(groups)
    tokens = batches * rows

    first_row = h * rows
    col, row, flags, back_flags = [], [], [], []
    for b in range(batches):
        lengths = doc_lengths[b]
        position = first_row + jnp.arange(rows, dtype=jnp.int32)
        doc, begin, size = places(lengths, position)
        angle = math.pi / 2 * (position - begin).astype(F32) / size.astype(F32)
        cos, sin = jnp.cos(angle), jnp.sin(angle)
        edges = first_row + jnp.array([-rows - 1, -1, 0, rows - 1, rows, 2 * rows], jnp.int32)
        at, _, _ = places(lengths, edges)
        first = (doc == at[2]).astype(F32)
        final = (doc == at[3]).astype(F32)
        place = doc.astype(F32)
        zero = jnp.zeros_like(cos)
        col.append(jnp.stack([first * cos, first * sin, final * cos, final * sin, cos, sin, place, zero], axis=1))
        row.append(jnp.stack([cos, sin, place, zero, zero, zero, zero, zero]))
        last = lax.axis_size("head") - 1
        near = (h >= 1) & (at[1] == at[2])
        far = (h >= 2) & (at[0] == at[2])
        flags.append(jnp.stack([near & (h != 2), near & (h == 2), far]))
        near = (h <= last - 1) & (at[3] == at[4])
        far = (h <= last - 2) & (at[3] == at[5])
        back_flags.append(jnp.stack([near & (h != 1), near & (h == 1), far]))
    col, row = jnp.concatenate(col), jnp.concatenate(row, axis=1)
    flags, back_flags = jnp.stack(flags).astype(F32), jnp.stack(back_flags).astype(F32)

    target = jnp.arange(width)
    source = (jnp.array(order)[target // block] ^ d) * block + target % block
    permutation = (jnp.arange(width)[:, None] == source[None, :]).astype(BF)
    x = dot(layer_input.reshape(tokens, width), permutation)
    cot = dot(cotangent.reshape(tokens, width), permutation)

    weights = []
    for l in range(layers):
        qkvo = jnp.concatenate([qkv_weight[l], out_weight[l].T], axis=1)
        updown = jnp.concatenate([in_weight[l], down_weight[l].T], axis=1)
        weights.append((Transfers(heads_steps(qkvo, groups)), Transfers(hidden_steps(updown, groups))))
    heads0, hidden0 = weights[0]
    start(heads0)

    params = jnp.concatenate([ln1_gain, ln1_bias, ln2_gain, ln2_bias], axis=0)[None]
    for masks in groups:
        params = spread(params, "dp", masks, 0)
    params = params.transpose(1, 0, 2).reshape(4 * layers, width).astype(F32)

    stream = x
    for _ in range(len(groups) - 2):
        stream = advance(stream, heads0)
    stream = advance(stream, heads0)
    start(hidden0)
    stream = advance(stream, heads0)
    stream = advance(stream, heads0)
    stream = advance(stream, heads0)
    for _ in range(len(groups) - 2):
        stream = advance(stream, hidden0)

    saved = []
    for l in range(layers):
        heads, units = weights[l]
        nheads, nunits = weights[l + 1] if l + 1 < layers else (None, None)
        w_att = heads.result
        if l == 0:
            stream = advance(stream, units)
        normed1, mixed = project(stream, params, l, *w_att)
        if nheads:
            start(nheads)
        mixed = advance(mixed, units)
        state = local_state(mixed, col, rows)
        states = Transfers(shift_steps(state, forward_shift))
        start(states)
        if nheads:
            for _ in range(len(groups) - 2):
                mixed = advance(mixed, nheads)
            mixed = advance(mixed, nheads)
            start(nunits)
        mixed = advance(mixed, states)
        near, far = states.result
        att, inv = attend(mixed, near, far, flags, col, row, rows)
        att = advance(att, units)
        if nheads:
            att = advance(att, nheads)
            for _ in range(len(groups) - 2):
                att = advance(att, nunits)
        att = advance(att, units)
        w_in, w_down = units.result
        mid, normed2, act, slope, out = hidden(stream, params, 2 * layers + l, att, w_att, w_in, w_down)
        saved.append((stream, normed1, mixed, near, far, att, inv, mid, normed2, act, slope, w_att, w_in, w_down))
        stream = out
        if nheads:
            stream = advance(stream, nheads, nunits)
            stream = advance(stream, nheads)

    layer_output = dot_t(stream.astype(BF), permutation).astype(BF).reshape(layer_input.shape)

    grad = cot
    sums = []
    norm_grads = [None] * layers
    for l in reversed(range(layers)):
        stream, normed1, mixed, near, far, att, inv, mid, normed2, act, slope, w_att, w_in, w_down = saved[l]
        previous = sums[-1] if sums else None
        down_g = Transfers(sum_steps(grad.astype(BF), act, groups, split_plain, "y"))
        start(down_g)
        gpre, grad, norm2_g = hidden_back(grad, params, 2 * layers + l, mid, slope, w_in, w_down)
        in_g = Transfers(sum_steps(normed2, gpre, groups, split_plain, "x"))
        start(in_g)
        grad = advance(grad, down_g)
        if previous:
            grad = advance(grad, *previous)
        gn, gstate = state_back(grad, mixed, att, inv, w_att, col, rows)
        gstates = Transfers(shift_steps(gstate, backward_shift))
        start(gstates)
        out_g = Transfers(sum_steps(grad.astype(BF), att, groups, partial(split_pairs, 1), "x"))
        start(out_g)
        gn = advance(gn, in_g)
        if previous:
            gn = advance(gn, previous[2], previous[3])
        gn = advance(gn, gstates)
        gnear, gfar = gstates.result
        gmixed = attend_back(mixed, gn, att, near, far, gnear, gfar, flags, back_flags, col, row, rows)
        gmixed = advance(gmixed, out_g, down_g, in_g)
        qkv_g = Transfers(sum_steps(normed1, gmixed, groups, partial(split_pairs, 3), "y"))
        start(qkv_g)
        if previous:
            gmixed = advance(gmixed, previous[3])
        grad, norm1_g = project_back(gmixed, *w_att, stream, params, l, grad)
        grad = advance(grad, qkv_g, out_g, down_g, in_g)
        sums.append((down_g, in_g, out_g, qkv_g))
        norm_grads[l] = (norm1_g[0], norm1_g[1], norm2_g[0], norm2_g[1])

    high = lax.reduce_precision(grad, 8, 7)
    input_grad = dot_t(high.astype(BF), permutation) + dot_t((grad - high).astype(BF), permutation)
    input_grad = input_grad.reshape(layer_input.shape)

    small = jnp.stack([norm_grads[l][i] for i in range(4) for l in range(layers)])
    small = small + swap(small, "head", 1)
    small = small + swap(small, "head", 2)
    small = small.reshape(4 * layers, n_dp, block).transpose(1, 0, 2)
    for masks in groups[::-1]:
        count = small.shape[0] // (len(masks) + 1)
        total = small[:count]
        for j, m in enumerate(masks):
            total = total + swap(small[(j + 1) * count : (j + 2) * count], "dp", m)
        small = total
    part = block // lax.axis_size("head")
    small = lax.dynamic_slice_in_dim(small.reshape(4, layers, block), h * part, part, 2)

    input_grad = finish(input_grad, [chain for layer in sums for chain in layer])
    sums = sums[::-1]
    down_grad = jnp.stack([s[0].result.T for s in sums])
    in_grad = jnp.stack([s[1].result for s in sums])
    out_grad = jnp.stack([s[2].result.T for s in sums])
    qkv_grad = jnp.stack([s[3].result for s in sums])
    return (
        layer_output,
        input_grad,
        small[0],
        small[1],
        qkv_grad,
        out_grad,
        small[2],
        small[3],
        in_grad,
        down_grad,
    )


def solution(mesh):
    in_specs = (
        P("dp", "head", None),
        P("dp", None),
        P(None, "dp"),
        P(None, "dp"),
        P(None, "dp", "head"),
        P(None, "head", "dp"),
        P(None, "dp"),
        P(None, "dp"),
        P(None, "dp", "head"),
        P(None, "head", "dp"),
        P("dp", "head", None),
    )
    out_specs = (
        P("dp", "head", None),
        P("dp", "head", None),
        P(None, ("dp", "head")),
        P(None, ("dp", "head")),
        P(None, "dp", "head"),
        P(None, "head", "dp"),
        P(None, ("dp", "head")),
        P(None, ("dp", "head")),
        P(None, "dp", "head"),
        P(None, "head", "dp"),
    )
    return jax.shard_map(shards, mesh=mesh, in_specs=in_specs, out_specs=out_specs, check_vma=False)
```

time: 1220 us -> 808 us (0.66)
  Pallas kernels: 0 us -> 295 us
  matrix products: 372 us -> 80.9 us
  local copies, waits for them, and re-layouts: 294 us -> 72 us
  waiting for transfers between devices: 214 us -> 134 us
  other arithmetic: 147 us -> 72.8 us
  starting transfers between devices: 155 us -> 129 us
    pallas_call x0 -> x16, Pallas kernels: none -> 295 us  [run(): pl.pallas_call(kernel, grid=grid, in_specs=in_specs, out_specs=[pl.BlockS...]
    dot_general x96 -> x0, matrix products: 142 us -> none  [the longest x8 28.6 us: attend_back(): gv = jnp.einsum('htu,the->uhe', w, gn, preferred_element_type=F32)]
    ppermute x94 -> x92, waiting for transfers between devices: 191 us -> 88.6 us  [swap(): return lax.ppermute(x, axis, [(i, i ^ mask) for i in range(n)])]
    dot_general x18 -> x3, matrix products: 82.6 us -> 7.2 us  [dot_t(): lax.dot_general(a, b, (((1,), (1,)), ((), ())), preferred_element_type=F32)]
    dot_general x18 -> x2, matrix products: 76.1 us -> 5.97 us  [dot(): lax.dot_general(a, b, (((1,), (0,)), ((), ())), preferred_element_type=F32)]
    convert_element_type x40 -> x7, other arithmetic: 43.6 us -> 1.17 us  [the longest x1 0.58 us: shards(): jnp.stack(back_flags).astype(F32)]
    convert_element_type x42 -> x2, local copies, waits for them, and re-layouts: 41.3 us -> 0.69 us  [shards(): params = params.transpose(1, 0, 2).reshape(4 * layers, width).astype(F32)]
    unnamed x838 -> x210, local copies, waits for them, and re-layouts: 55.4 us -> 16.3 us
  transfers between devices with their start and end apart: 110 -> 100, of which waited for: 37 -> 26; matrix products, arithmetic and copies ran while one was open for 58% -> 18% of each run, Pallas kernels for 0% -> 32%
where the time goes in v2:
time: 808 us; the launch traced here: 796 us
  Pallas kernels  295 us (37%)
  waiting for transfers between devices  134 us (17%)
  starting transfers between devices  129 us (16%)
  matrix products  80.9 us (10%)
  other arithmetic  72.8 us (9%)
  local copies, waits for them, and re-layouts  72 us (9%)
  between operations  13.2 us (2%)
    pallas_call x16, Pallas kernels, run(): pl.pallas_call(kernel, grid=grid, in_specs=in_specs, out_specs=[pl.BlockS...  295 us
    ppermute x92, starting transfers between devices, swap(): return lax.ppermute(x, axis, [(i, i ^ mask) for i in range(n)])  114 us
    ppermute x92, waiting for transfers between devices, swap(): return lax.ppermute(x, axis, [(i, i ^ mask) for i in range(n)])  88.6 us
    dot_general x16, matrix products, t_dot(): lax.dot_general(a, b, (((0,), (0,)), ((), ())), preferred_element_type=F32)  67.7 us
    ppermute x4, waiting for transfers between devices, forward_shift(): return lax.ppermute(x, 'head', [(i, i + by) for i in range(n - by)])  30.4 us
    unnamed x210, local copies, waits for them, and re-layouts  16.3 us
  transfers between devices with their start and end apart: 100, of which 26 were waited for; matrix products, arithmetic and copies ran while one was open for 18% of the time, Pallas kernels for 32%

profile of v2, /device:TPU:0, one launch (start us, length us, event | category | flops | bytes accessed | tf_op | source)
XLA Modules:
  0.0 796.5 jit_solution(17926523299775553597)
XLA Ops:
  13.4 3.5 collective-permute-start.9
  24.1 3.9 collective-permute-done.3
  32.1 9.9 %collective-permute-done.5 = bf16[768,384]{1,0:T(8,128)(2,1)S(1)} collective-permute-done((bf16[768,384]{1,0:T(8,128)(2,1)S(1)}, bf16[768,384]{1,0:T(8,128)(2,1)S(1)}, u32[]{:S(2)}, u32[]{:S(2)}) %collective-permute-start.5) | collective-permute-done | bytes 589856 | tf_op jit(solution)/shard_map/ppermute | solution.py:29
  49.2 5.5 concatenate.121.own_ref.oo_ref
  84.4 9.3 %project.2 = (bf16[1024,768]{1,0:T(8,128)(2,1)}, bf16[1024,2304]{1,0:T(8,128)(2,1)}) custom-call(f32[1024,768]{1,0:T(8,128)} %fusion.24.x_ref, f32[8,768]{1,0:T(8,128)} %reshape.466.par_ref, bf16[768,1536]{1,0:T(8,128)(2,1)} %copy-done.4, bf16[768,1536]{1,0:T(8,128)(2,1)} %collective-permute-done.7.other_ref.ox_ref), custom_call_target="tpu_custom_call" | custom-call | flops 3623878656 | bytes 12976128 | tf_op jit(solution)/shard_map/project/pallas_call | solution.py:226
  102.6 10.2 %local_state.2 = bf16[2,6,144,128]{3,2,1,0:T(8,128)(2,1)} custom-call(f32[1024,8]{1,0:T(8,128)} %copy.75.col_ref, bf16[1024,2304]{1,0:T(8,128)(2,1)} %get-tuple-element.287.mixed_ref.q_ref), custom_call_target="tpu_custom_call" | custom-call | flops 1207959552 | bytes 4718592 | tf_op jit(solution)/shard_map/local_state/pallas_call | solution.py:226
  114.1 3.7 collective-permute-start.21
  119.6 10.3 %collective-permute-done.21.far_ref = bf16[2,6,144,128]{3,2,1,0:T(8,128)(2,1)S(1)} collective-permute-done((bf16[2,6,144,128]{3,2,1,0:T(8,128)(2,1)}, bf16[2,6,144,128]{3,2,1,0:T(8,128)(2,1)S(1)}, u32[]{:S(2)}, u32[]{:S(2)}) %collective-permute-start.21) | collective-permute-done | bytes 442400 | tf_op jit(solution)/shard_map/ppermute | solution.py:34
  130.7 16.2 %attend.2 = (bf16[1024,768]{1,0:T(8,128)(2,1)}, f32[1024,768]{1,0:T(8,128)}) custom-call(f32[2,3]{1,0:T(2,128)} %add_convert_fusion.flag_ref, f32[1024,8]{1,0:T(8,128)} %copy.75.col_ref, f32[8,1024]{1,0:T(8,128)} %pad_maximum_fusion.29.row_ref, bf16[1024,2304]{1,0:T(8,128)(2,1)} %get-tuple-element.287.mixed_ref.q_ref, bf16[2,6,144,128]{3,2,1,0:T(8,128)(2,1)} %copy-done.79, ...), custom_call_target="tpu_custom_call" | custom-call | flops 3221225472 | bytes 9437184 | tf_op jit(solution)/shard_map/attend/pallas_call | solution.py:226
  157.5 5.5 collective-permute-done.24
  172.1 29.7 %hidden.2 = (f32[1024,768]{1,0:T(8,128)}, bf16[1024,768]{1,0:T(8,128)(2,1)}, bf16[1024,3072]{1,0:T(8,128)(2,1)}, bf16[1024,3072]{1,0:T(8,128)(2,1)}, f32[1024,768]{1,0:T(8,128)}) custom-call(f32[1024,768]{1,0:T(8,128)} %fusion.24.x_ref, f32[8,768]{1,0:T(8,128)} %reshape.466.par_ref, bf16[1024,768]{1,0:T(8,128)(2,1)} %get-tuple-element.305.att_ref, ...), custom_call_target="tpu_custom_call" | custom-call | flops 10871635968 | bytes 34603008 | tf_op jit(solution)/shard_map/hidden/pallas_call | solution.py:226
  205.1 5.4 concatenate.139.own_ref.oo_ref
  216.6 9.3 %project.3 = (bf16[1024,768]{1,0:T(8,128)(2,1)}, bf16[1024,2304]{1,0:T(8,128)(2,1)}) custom-call(f32[1024,768]{1,0:T(8,128)} %get-tuple-element.319.x_ref, f32[8,768]{1,0:T(8,128)} %reshape.466.par_ref, bf16[768,1536]{1,0:T(8,128)(2,1)} %copy-done.5, bf16[768,1536]{1,0:T(8,128)(2,1)} %copy-done.10), custom_call_target="tpu_custom_call" | custom-call | flops 3623878656 | bytes 12976128 | tf_op jit(solution)/shard_map/project/pallas_call | solution.py:226
  229.7 10.2 %local_state.3 = bf16[2,6,144,128]{3,2,1,0:T(8,128)(2,1)} custom-call(f32[1024,8]{1,0:T(8,128)} %copy.75.col_ref, bf16[1024,2304]{1,0:T(8,128)(2,1)} %get-tuple-element.328.mixed_ref.q_ref), custom_call_target="tpu_custom_call" | custom-call | flops 1207959552 | bytes 4718592 | tf_op jit(solution)/shard_map/local_state/pallas_call | solution.py:226
  241.2 3.4 collective-permute-start.37
  244.6 20.1 %collective-permute-done.37.far_ref = bf16[2,6,144,128]{3,2,1,0:T(8,128)(2,1)S(1)} collective-permute-done((bf16[2,6,144,128]{3,2,1,0:T(8,128)(2,1)}, bf16[2,6,144,128]{3,2,1,0:T(8,128)(2,1)S(1)}, u32[]{:S(2)}, u32[]{:S(2)}) %collective-permute-start.37) | collective-permute-done | bytes 442400 | tf_op jit(solution)/shard_map/ppermute | solution.py:34
  265.5 16.2 %attend.3 = (bf16[1024,768]{1,0:T(8,128)(2,1)}, f32[1024,768]{1,0:T(8,128)}) custom-call(f32[2,3]{1,0:T(2,128)} %add_convert_fusion.flag_ref, f32[1024,8]{1,0:T(8,128)} %copy.75.col_ref, f32[8,1024]{1,0:T(8,128)} %pad_maximum_fusion.29.row_ref, bf16[1024,2304]{1,0:T(8,128)(2,1)} %get-tuple-element.328.mixed_ref.q_ref, bf16[2,6,144,128]{3,2,1,0:T(8,128)(2,1)} %copy-done.81, ...), custom_call_target="tpu_custom_call" | custom-call | flops 3221225472 | bytes 9437184 | tf_op jit(solution)/shard_map/attend/pallas_call | solution.py:226
  297.9 30.8 %hidden.3 = (f32[1024,768]{1,0:T(8,128)}, bf16[1024,768]{1,0:T(8,128)(2,1)}, bf16[1024,3072]{1,0:T(8,128)(2,1)}, bf16[1024,3072]{1,0:T(8,128)(2,1)}, f32[1024,768]{1,0:T(8,128)}) custom-call(f32[1024,768]{1,0:T(8,128)} %get-tuple-element.319.x_ref, f32[8,768]{1,0:T(8,128)} %reshape.466.par_ref, bf16[1024,768]{1,0:T(8,128)(2,1)} %get-tuple-element.340.att_ref, ...), custom_call_target="tpu_custom_call" | custom-call | flops 10871635968 | bytes 34603008 | tf_op jit(solution)/shard_map/hidden/pallas_call | solution.py:226
  328.7 5.8 convolution_convert_fusion.3
  335.0 25.2 %hidden_back.2 = (bf16[1024,3072]{1,0:T(8,128)(2,1)}, f32[1024,768]{1,0:T(8,128)}, f32[8,768]{1,0:T(8,128)}) custom-call(f32[1024,768]{1,0:T(8,128)} %copy-done.87, f32[8,768]{1,0:T(8,128)} %reshape.466.par_ref, f32[1024,768]{1,0:T(8,128)} %get-tuple-element.344.mid_ref, bf16[1024,3072]{1,0:T(8,128)(2,1)} %get-tuple-element.345.slope_ref, ...), custom_call_target="tpu_custom_call" | custom-call | flops 9663676416 | bytes 31457280 | tf_op jit(solution)/shard_map/hidden_back/pallas_call | solution.py:226
  360.2 6.1 convolution_convert_fusion.2
  378.4 14.3 %state_back.2 = (bf16[1024,768]{1,0:T(8,128)(2,1)}, bf16[2,6,144,128]{3,2,1,0:T(8,128)(2,1)}) custom-call(f32[1024,8]{1,0:T(8,128)} %copy.75.col_ref, f32[1024,768]{1,0:T(8,128)} %get-tuple-element.350.g_ref, bf16[768,1536]{1,0:T(8,128)(2,1)} %copy-done.5, bf16[768,1536]{1,0:T(8,128)(2,1)} %copy-done.10, ...), custom_call_target="tpu_custom_call" | custom-call | flops 2415919104 | bytes 11010048 | tf_op jit(solution)/shard_map/state_back/pallas_call | solution.py:226
  401.3 3.5 collective-permute-start.48
  406.9 9.1 %collective-permute-done.45.gfar_ref = bf16[2,6,144,128]{3,2,1,0:T(8,128)(2,1)} collective-permute-done((bf16[2,6,144,128]{3,2,1,0:T(8,128)(2,1)}, bf16[2,6,144,128]{3,2,1,0:T(8,128)(2,1)}, u32[]{:S(2)}, u32[]{:S(2)}) %collective-permute-start.45) | collective-permute-done | bytes 442400 | tf_op jit(solution)/shard_map/ppermute | solution.py:39
  416.0 31.1 %attend_back.2.gm_ref = bf16[1024,2304]{1,0:T(8,128)(2,1)} custom-call(f32[2,3]{1,0:T(2,128)} %add_convert_fusion.flag_ref, f32[2,3]{1,0:T(2,128)} %add_convert_fusion.1.back_flag_ref, f32[1024,8]{1,0:T(8,128)} %copy.75.col_ref, f32[8,1024]{1,0:T(8,128)} %pad_maximum_fusion.29.row_ref, bf16[1024,2304]{1,0:T(8,128)(2,1)} %get-tuple-element.328.mixed_ref.q_ref, ...), custom_call_target="tpu_custom_call" | custom-call | flops 9663676416 | bytes 12582912 | tf_op jit(solution)/shard_map/attend_back/pallas_call | solution.py:226
  447.1 3.5 fusion.131
  456.5 3.5 convolution_convert_fusion.5
  464.4 4.0 fusion.16
  468.5 10.7 %project_back.2 = (f32[1024,768]{1,0:T(8,128)}, f32[8,768]{1,0:T(8,128)}) custom-call(bf16[1024,2304]{1,0:T(8,128)(2,1)} %attend_back.2.gm_ref, bf16[768,1536]{1,0:T(8,128)(2,1)} %copy-done.5, bf16[768,1536]{1,0:T(8,128)(2,1)} %copy-done.10, f32[1024,768]{1,0:T(8,128)} %get-tuple-element.319.x_ref, f32[8,768]{1,0:T(8,128)} %reshape.466.par_ref, ...), custom_call_target="tpu_custom_call" | custom-call | flops 3623878656 | bytes 17694720 | tf_op jit(solution)/shard_map/project_back/pallas_call | solution.py:226
  482.7 7.7 collective-permute-done.50
  500.2 5.8 convolution_convert_fusion.1
  510.4 25.2 %hidden_back.3 = (bf16[1024,3072]{1,0:T(8,128)(2,1)}, f32[1024,768]{1,0:T(8,128)}, f32[8,768]{1,0:T(8,128)}) custom-call(f32[1024,768]{1,0:T(8,128)} %get-tuple-element.379.g_ref, f32[8,768]{1,0:T(8,128)} %reshape.466.par_ref, f32[1024,768]{1,0:T(8,128)} %get-tuple-element.380.mid_ref, bf16[1024,3072]{1,0:T(8,128)(2,1)} %get-tuple-element.381.slope_ref, ...), custom_call_target="tpu_custom_call" | custom-call | flops 9663676416 | bytes 31457280 | tf_op jit(solution)/shard_map/hidden_back/pallas_call | solution.py:226
  535.6 6.0 convolution_convert_fusion
  541.6 4.4 fusion.1
  546.0 4.7 fusion.4
  560.7 6.3 collective-permute-done.58
  567.0 9.2 %collective-permute-done.60 = bf16[384,192]{1,0:T(8,128)(2,1)S(1)} collective-permute-done((bf16[384,192]{1,0:T(8,128)(2,1)S(1)}, bf16[384,192]{1,0:T(8,128)(2,1)S(1)}, u32[]{:S(2)}, u32[]{:S(2)}) %collective-permute-start.60) | collective-permute-done | bytes 147488 | tf_op jit(solution)/shard_map/ppermute | solution.py:29
  580.6 15.3 %state_back.3 = (bf16[1024,768]{1,0:T(8,128)(2,1)}, bf16[2,6,144,128]{3,2,1,0:T(8,128)(2,1)}) custom-call(f32[1024,8]{1,0:T(8,128)} %copy.75.col_ref, f32[1024,768]{1,0:T(8,128)} %get-tuple-element.398.g_ref, bf16[768,1536]{1,0:T(8,128)(2,1)} %copy-done.4, bf16[768,1536]{1,0:T(8,128)(2,1)} %collective-permute-done.7.other_ref.ox_ref, ...), custom_call_target="tpu_custom_call" | custom-call | flops 2415919104 | bytes 11010048 | tf_op jit(solution)/shard_map/state_back/pallas_call | solution.py:226
  627.4 5.3 collective-permute-done.68.gfar_ref
  634.9 30.7 %attend_back.3.gm_ref = bf16[1024,2304]{1,0:T(8,128)(2,1)} custom-call(f32[2,3]{1,0:T(2,128)} %add_convert_fusion.flag_ref, f32[2,3]{1,0:T(2,128)} %add_convert_fusion.1.back_flag_ref, f32[1024,8]{1,0:T(8,128)} %copy.75.col_ref, f32[8,1024]{1,0:T(8,128)} %pad_maximum_fusion.29.row_ref, bf16[1024,2304]{1,0:T(8,128)(2,1)} %get-tuple-element.287.mixed_ref.q_ref, ...), custom_call_target="tpu_custom_call" | custom-call | flops 9663676416 | bytes 12582912 | tf_op jit(solution)/shard_map/attend_back/pallas_call | solution.py:226
  667.9 3.5 fusion.132
  676.8 10.7 %project_back.3 = (f32[1024,768]{1,0:T(8,128)}, f32[8,768]{1,0:T(8,128)}) custom-call(bf16[1024,2304]{1,0:T(8,128)(2,1)} %attend_back.3.gm_ref, bf16[768,1536]{1,0:T(8,128)(2,1)} %copy-done.4, bf16[768,1536]{1,0:T(8,128)(2,1)} %collective-permute-done.7.other_ref.ox_ref, f32[1024,768]{1,0:T(8,128)} %fusion.24.x_ref, f32[8,768]{1,0:T(8,128)} %reshape.466.par_ref, ...), custom_call_target="tpu_custom_call" | custom-call | flops 3623878656 | bytes 17694720 | tf_op jit(solution)/shard_map/project_back/pallas_call | solution.py:226
  692.6 5.6 convolution_convert_fusion.4
  702.7 4.4 fusion.13
  711.7 3.6 collective-permute-done.99
  719.6 11.2 %collective-permute-done.76 = bf16[768,192]{1,0:T(8,128)(2,1)S(1)} collective-permute-done((bf16[768,192]{1,0:T(8,128)(2,1)S(1)}, bf16[768,192]{1,0:T(8,128)(2,1)S(1)}, u32[]{:S(2)}, u32[]{:S(2)}) %collective-permute-start.76) | collective-permute-done | bytes 294944 | tf_op jit(solution)/shard_map/ppermute | solution.py:29
  744.8 5.4 collective-permute-done.80
  755.6 6.5 collective-permute-done.83
  (574 shorter events, 291.9 us)
Async XLA Ops:
  12.5 64.5 %collective-permute-start.8 = (bf16[96,1536]{1,0:T(8,128)(2,1)}, bf16[96,1536]{1,0:T(8,128)(2,1)}, u32[]{:S(2)}, u32[]{:S(2)}) collective-permute-start(bf16[96,1536]{1,0:T(8,128)(2,1)} %pad_maximum_fusion.23), channel_id=1, source_target_pairs={{0,8},{4,12},{8,0},{12,4},{16,24},{20,28},{24,16},{28,20},{1,9},{5... | collective-permute-start | bytes 884744 | tf_op jit(solution)/shard_map/ppermute | solution.py:29
  13.4 65.0 %collective-permute-start.9 = (bf16[96,1536]{1,0:T(8,128)(2,1)}, bf16[96,1536]{1,0:T(8,128)(2,1)}, u32[]{:S(2)}, u32[]{:S(2)}) collective-permute-start(bf16[96,1536]{1,0:T(8,128)(2,1)} %pad_maximum_fusion.23), channel_id=1, source_target_pairs={{0,16},{4,20},{8,24},{12,28},{16,0},{20,4},{24,8},{28,12},{1,17},{... | collective-permute-start | bytes 884744 | tf_op jit(solution)/shard_map/ppermute | solution.py:29
  20.4 58.5 %collective-permute-start.10 = (bf16[96,1536]{1,0:T(8,128)(2,1)}, bf16[96,1536]{1,0:T(8,128)(2,1)}, u32[]{:S(2)}, u32[]{:S(2)}) collective-permute-start(bf16[96,1536]{1,0:T(8,128)(2,1)} %pad_maximum_fusion.23), channel_id=1, source_target_pairs={{0,24},{4,28},{8,16},{12,20},{16,8},{20,12},{24,0},{28,4},{1,25},{... | collective-permute-start | bytes 884744 | tf_op jit(solution)/shard_map/ppermute | solution.py:29
  42.0 22.1 %collective-permute-start.11 = (bf16[1,8,96]{2,1,0:T(8,128)(2,1)S(1)}, bf16[1,8,96]{2,1,0:T(8,128)(2,1)S(1)}, u32[]{:S(2)}, u32[]{:S(2)}) collective-permute-start(bf16[1,8,96]{2,1,0:T(8,128)(2,1)S(1)} %maximum_bitcast_fusion), channel_id=1, source_target_pairs={{0,8},{4,12},{8,0},{12,4},{16,24},{20,28},{24,16},{28,20},{1,9},{5... | collective-permute-start | bytes 4616 | tf_op jit(solution)/shard_map/ppermute | solution.py:29
  54.8 19.2 %collective-permute-start.7 = (bf16[768,1536]{1,0:T(8,128)(2,1)S(1)}, bf16[768,1536]{1,0:T(8,128)(2,1)}, u32[]{:S(2)}, u32[]{:S(2)}) collective-permute-start(bf16[768,1536]{1,0:T(8,128)(2,1)S(1)} %concatenate.121.own_ref.oo_ref), channel_id=1, source_target_pairs={{0,1},{1,0},{2,3},{3,2},{4,5},{5,4},{6,7},{7,6},{8,9},{9,8},{10,11... | collective-permute-start | bytes 7077896 | tf_op jit(solution)/shard_map/ppermute | solution.py:29
  74.0 38.8 %collective-permute-start.17 = (bf16[96,768]{1,0:T(8,128)(2,1)}, bf16[96,768]{1,0:T(8,128)(2,1)}, u32[]{:S(2)}, u32[]{:S(2)}) collective-permute-start(bf16[96,768]{1,0:T(8,128)(2,1)} %pad_maximum_fusion.27), channel_id=1, source_target_pairs={{0,8},{4,12},{8,0},{12,4},{16,24},{20,28},{24,16},{28,20},{1,9},{5... | collective-permute-start | bytes 442376 | tf_op jit(solution)/shard_map/ppermute | solution.py:29
  74.0 40.1 %collective-permute-start.18 = (bf16[96,768]{1,0:T(8,128)(2,1)}, bf16[96,768]{1,0:T(8,128)(2,1)}, u32[]{:S(2)}, u32[]{:S(2)}) collective-permute-start(bf16[96,768]{1,0:T(8,128)(2,1)} %pad_maximum_fusion.27), channel_id=1, source_target_pairs={{0,16},{4,20},{8,24},{12,28},{16,0},{20,4},{24,8},{28,12},{1,17},{... | collective-permute-start | bytes 442376 | tf_op jit(solution)/shard_map/ppermute | solution.py:29
  77.1 41.3 %collective-permute-start.19 = (bf16[96,768]{1,0:T(8,128)(2,1)}, bf16[96,768]{1,0:T(8,128)(2,1)}, u32[]{:S(2)}, u32[]{:S(2)}) collective-permute-start(bf16[96,768]{1,0:T(8,128)(2,1)} %pad_maximum_fusion.27), channel_id=1, source_target_pairs={{0,24},{4,28},{8,16},{12,20},{16,8},{20,12},{24,0},{28,4},{1,25},{... | collective-permute-start | bytes 442376 | tf_op jit(solution)/shard_map/ppermute | solution.py:29
  96.1 50.8 %collective-permute-start.22 = (bf16[768,768]{1,0:T(8,128)(2,1)}, bf16[768,768]{1,0:T(8,128)(2,1)}, u32[]{:S(2)}, u32[]{:S(2)}) collective-permute-start(bf16[768,768]{1,0:T(8,128)(2,1)} %pad_maximum_fusion.6), channel_id=1, source_target_pairs={{0,2},{1,3},{2,0},{3,1},{4,6},{5,7},{6,4},{7,5},{8,10},{9,11},{10,... | collective-permute-start | bytes 3538952 | tf_op jit(solution)/shard_map/ppermute | solution.py:29
  97.4 49.5 %collective-permute-start.23 = (bf16[384,1536]{1,0:T(8,128)(2,1)}, bf16[384,1536]{1,0:T(8,128)(2,1)}, u32[]{:S(2)}, u32[]{:S(2)}) collective-permute-start(bf16[384,1536]{1,0:T(8,128)(2,1)} %pad_maximum_fusion.7), channel_id=1, source_target_pairs={{0,4},{4,0},{8,12},{12,8},{16,20},{20,16},{24,28},{28,24},{1,5},{5... | collective-permute-start | bytes 3538952 | tf_op jit(solution)/shard_map/ppermute | solution.py:29
  157.5 44.3 %collective-permute-start.30 = (bf16[96,1536]{1,0:T(8,128)(2,1)}, bf16[96,1536]{1,0:T(8,128)(2,1)S(1)}, u32[]{:S(2)}, u32[]{:S(2)}) collective-permute-start(bf16[96,1536]{1,0:T(8,128)(2,1)} %pad_maximum_fusion.24), channel_id=1, source_target_pairs={{0,8},{4,12},{8,0},{12,4},{16,24},{20,28},{24,16},{28,20},{1,9},{5... | collective-permute-start | bytes 884744 | tf_op jit(solution)/shard_map/ppermute | solution.py:29
  163.0 38.8 %collective-permute-start.31 = (bf16[96,1536]{1,0:T(8,128)(2,1)}, bf16[96,1536]{1,0:T(8,128)(2,1)S(1)}, u32[]{:S(2)}, u32[]{:S(2)}) collective-permute-start(bf16[96,1536]{1,0:T(8,128)(2,1)} %pad_maximum_fusion.24), channel_id=1, source_target_pairs={{0,16},{4,20},{8,24},{12,28},{16,0},{20,4},{24,8},{28,12},{1,17},{... | collective-permute-start | bytes 884744 | tf_op jit(solution)/shard_map/ppermute | solution.py:29
  164.1 37.8 %collective-permute-start.32 = (bf16[96,1536]{1,0:T(8,128)(2,1)}, bf16[96,1536]{1,0:T(8,128)(2,1)S(1)}, u32[]{:S(2)}, u32[]{:S(2)}) collective-permute-start(bf16[96,1536]{1,0:T(8,128)(2,1)} %pad_maximum_fusion.24), channel_id=1, source_target_pairs={{0,24},{4,28},{8,16},{12,20},{16,8},{20,12},{24,0},{28,4},{1,25},{... | collective-permute-start | bytes 884744 | tf_op jit(solution)/shard_map/ppermute | solution.py:29
  167.9 34.0 %collective-permute-start.28 = (bf16[768,384]{1,0:T(8,128)(2,1)S(1)}, bf16[768,384]{1,0:T(8,128)(2,1)S(1)}, u32[]{:S(2)}, u32[]{:S(2)}) collective-permute-start(bf16[768,384]{1,0:T(8,128)(2,1)S(1)} %pad_maximum_fusion.13), channel_id=1, source_target_pairs={{0,2},{1,3},{2,0},{3,1},{4,6},{5,7},{6,4},{7,5},{8,10},{9,11},{10,... | collective-permute-start | bytes 1769480 | tf_op jit(solution)/shard_map/ppermute | solution.py:29
  171.1 30.8 %collective-permute-start.29 = (bf16[384,768]{1,0:T(8,128)(2,1)S(1)}, bf16[384,768]{1,0:T(8,128)(2,1)S(1)}, u32[]{:S(2)}, u32[]{:S(2)}) collective-permute-start(bf16[384,768]{1,0:T(8,128)(2,1)S(1)} %pad_maximum_fusion.17), channel_id=1, source_target_pairs={{0,4},{4,0},{8,12},{12,8},{16,20},{20,16},{24,28},{28,24},{1,5},{5... | collective-permute-start | bytes 1769480 | tf_op jit(solution)/shard_map/ppermute | solution.py:29
  227.3 54.4 %collective-permute-start.38 = (bf16[768,768]{1,0:T(8,128)(2,1)S(1)}, bf16[768,768]{1,0:T(8,128)(2,1)S(1)}, u32[]{:S(2)}, u32[]{:S(2)}) collective-permute-start(bf16[768,768]{1,0:T(8,128)(2,1)S(1)} %pad_maximum_fusion.10), channel_id=1, source_target_pairs={{0,2},{1,3},{2,0},{3,1},{4,6},{5,7},{6,4},{7,5},{8,10},{9,11},{10,... | collective-permute-start | bytes 3538952 | tf_op jit(solution)/shard_map/ppermute | solution.py:29
  228.7 53.0 %collective-permute-start.39 = (bf16[384,1536]{1,0:T(8,128)(2,1)S(1)}, bf16[384,1536]{1,0:T(8,128)(2,1)S(1)}, u32[]{:S(2)}, u32[]{:S(2)}) collective-permute-start(bf16[384,1536]{1,0:T(8,128)(2,1)S(1)} %pad_maximum_fusion.11), channel_id=1, source_target_pairs={{0,4},{4,0},{8,12},{12,8},{16,20},{20,16},{24,28},{28,24},{1,5},{5... | collective-permute-start | bytes 3538952 | tf_op jit(solution)/shard_map/ppermute | solution.py:29
  241.2 23.5 %collective-permute-start.37 = (bf16[2,6,144,128]{3,2,1,0:T(8,128)(2,1)}, bf16[2,6,144,128]{3,2,1,0:T(8,128)(2,1)S(1)}, u32[]{:S(2)}, u32[]{:S(2)}) collective-permute-start(bf16[2,6,144,128]{3,2,1,0:T(8,128)(2,1)} %local_state.3), channel_id=1, source_target_pairs={{0,2},{1,3},{4,6},{5,7},{8,10},{9,11},{12,14},{13,15},{16,18},{17,... | collective-permute-start | bytes 1327112 | tf_op jit(solution)/shard_map/ppermute | solution.py:34
  334.5 38.3 %collective-permute-start.42 = (bf16[768,1536]{1,0:T(8,128)(2,1)}, bf16[768,1536]{1,0:T(8,128)(2,1)}, u32[]{:S(2)}, u32[]{:S(2)}) collective-permute-start(bf16[768,1536]{1,0:T(8,128)(2,1)} %convolution_convert_fusion.3), channel_id=1, source_target_pairs={{0,1},{1,0},{2,3},{3,2},{4,5},{5,4},{6,7},{7,6},{8,9},{9,8},{10,11... | collective-permute-start | bytes 7077896 | tf_op jit(solution)/shard_map/ppermute | solution.py:29
  366.4 28.9 %collective-permute-start.43 = (bf16[768,1536]{1,0:T(8,128)(2,1)}, bf16[768,1536]{1,0:T(8,128)(2,1)S(1)}, u32[]{:S(2)}, u32[]{:S(2)}) collective-permute-start(bf16[768,1536]{1,0:T(8,128)(2,1)} %convolution_convert_fusion.2), channel_id=1, source_target_pairs={{0,1},{1,0},{2,3},{3,2},{4,5},{5,4},{6,7},{7,6},{8,9},{9,8},{10,11... | collective-permute-start | bytes 7077896 | tf_op jit(solution)/shard_map/ppermute | solution.py:29
  394.0 22.1 %collective-permute-start.45 = (bf16[2,6,144,128]{3,2,1,0:T(8,128)(2,1)}, bf16[2,6,144,128]{3,2,1,0:T(8,128)(2,1)}, u32[]{:S(2)}, u32[]{:S(2)}) collective-permute-start(bf16[2,6,144,128]{3,2,1,0:T(8,128)(2,1)} %get-tuple-element.358), channel_id=1, source_target_pairs={{2,0},{3,1},{6,4},{7,5},{10,8},{11,9},{14,12},{15,13},{18,16},{19,... | collective-permute-start | bytes 1327112 | tf_op jit(solution)/shard_map/ppermute | solution.py:39
  400.3 46.8 %collective-permute-start.47 = (bf16[384,1536]{1,0:T(8,128)(2,1)}, bf16[384,1536]{1,0:T(8,128)(2,1)}, u32[]{:S(2)}, u32[]{:S(2)}) collective-permute-start(bf16[384,1536]{1,0:T(8,128)(2,1)} %slice.1312), channel_id=1, source_target_pairs={{0,4},{4,0},{8,12},{12,8},{16,20},{20,16},{24,28},{28,24},{1,5},{5... | collective-permute-start | bytes 3538952 | tf_op jit(solution)/shard_map/ppermute | solution.py:29
  401.3 45.8 %collective-permute-start.48 = (bf16[768,768]{1,0:T(8,128)(2,1)}, bf16[768,768]{1,0:T(8,128)(2,1)}, u32[]{:S(2)}, u32[]{:S(2)}) collective-permute-start(bf16[768,768]{1,0:T(8,128)(2,1)} %slice.1311), channel_id=1, source_target_pairs={{0,2},{1,3},{2,0},{3,1},{4,6},{5,7},{6,4},{7,5},{8,10},{9,11},{10,... | collective-permute-start | bytes 3538952 | tf_op jit(solution)/shard_map/ppermute | solution.py:29
  406.7 40.4 %collective-permute-start.46 = (bf16[768,384]{1,0:T(8,128)(2,1)}, bf16[768,384]{1,0:T(8,128)(2,1)}, u32[]{:S(2)}, u32[]{:S(2)}) collective-permute-start(bf16[768,384]{1,0:T(8,128)(2,1)} %convolution_convert_fusion.7), channel_id=1, source_target_pairs={{0,1},{1,0},{2,3},{3,2},{4,5},{5,4},{6,7},{7,6},{8,9},{9,8},{10,11... | collective-permute-start | bytes 1769480 | tf_op jit(solution)/shard_map/ppermute | solution.py:29
  460.0 30.5 %collective-permute-start.49 = (bf16[768,1152]{1,0:T(8,128)(2,1)}, bf16[768,1152]{1,0:T(8,128)(2,1)S(1)}, u32[]{:S(2)}, u32[]{:S(2)}) collective-permute-start(bf16[768,1152]{1,0:T(8,128)(2,1)} %convolution_convert_fusion.5), channel_id=1, source_target_pairs={{0,1},{1,0},{2,3},{3,2},{4,5},{5,4},{6,7},{7,6},{8,9},{9,8},{10,11... | collective-permute-start | bytes 5308424 | tf_op jit(solution)/shard_map/ppermute | solution.py:29
  463.4 27.0 %collective-permute-start.51 = (bf16[384,768]{1,0:T(8,128)(2,1)S(1)}, bf16[384,768]{1,0:T(8,128)(2,1)S(1)}, u32[]{:S(2)}, u32[]{:S(2)}) collective-permute-start(bf16[384,768]{1,0:T(8,128)(2,1)S(1)} %slice.1318), channel_id=1, source_target_pairs={{0,2},{1,3},{2,0},{3,1},{4,6},{5,7},{6,4},{7,5},{8,10},{9,11},{10,... | collective-permute-start | bytes 1769480 | tf_op jit(solution)/shard_map/ppermute | solution.py:29
  463.4 27.0 %collective-permute-start.52 = (bf16[384,768]{1,0:T(8,128)(2,1)S(1)}, bf16[384,768]{1,0:T(8,128)(2,1)S(1)}, u32[]{:S(2)}, u32[]{:S(2)}) collective-permute-start(bf16[384,768]{1,0:T(8,128)(2,1)S(1)} %slice.1317), channel_id=1, source_target_pairs={{0,4},{4,0},{8,12},{12,8},{16,20},{20,16},{24,28},{28,24},{1,5},{5... | collective-permute-start | bytes 1769480 | tf_op jit(solution)/shard_map/ppermute | solution.py:29
  506.0 44.7 %collective-permute-start.53 = (bf16[768,1536]{1,0:T(8,128)(2,1)}, bf16[768,1536]{1,0:T(8,128)(2,1)S(1)}, u32[]{:S(2)}, u32[]{:S(2)}) collective-permute-start(bf16[768,1536]{1,0:T(8,128)(2,1)} %convolution_convert_fusion.1), channel_id=1, source_target_pairs={{0,1},{1,0},{2,3},{3,2},{4,5},{5,4},{6,7},{7,6},{8,9},{9,8},{10,11... | collective-permute-start | bytes 7077896 | tf_op jit(solution)/shard_map/ppermute | solution.py:29
  506.0 47.3 %collective-permute-start.54 = (bf16[96,768]{1,0:T(8,128)(2,1)}, bf16[96,768]{1,0:T(8,128)(2,1)}, u32[]{:S(2)}, u32[]{:S(2)}) collective-permute-start(bf16[96,768]{1,0:T(8,128)(2,1)} %get-tuple-element.387), channel_id=1, source_target_pairs={{0,8},{4,12},{8,0},{12,4},{16,24},{20,28},{24,16},{28,20},{1,9},{5... | collective-permute-start | bytes 442376 | tf_op jit(solution)/shard_map/ppermute | solution.py:29
  506.3 48.9 %collective-permute-start.55 = (bf16[96,768]{1,0:T(8,128)(2,1)}, bf16[96,768]{1,0:T(8,128)(2,1)}, u32[]{:S(2)}, u32[]{:S(2)}) collective-permute-start(bf16[96,768]{1,0:T(8,128)(2,1)} %get-tuple-element.388), channel_id=1, source_target_pairs={{0,16},{4,20},{8,24},{12,28},{16,0},{20,4},{24,8},{28,12},{1,17},{... | collective-permute-start | bytes 442376 | tf_op jit(solution)/shard_map/ppermute | solution.py:29
  507.9 49.8 %collective-permute-start.56 = (bf16[96,768]{1,0:T(8,128)(2,1)}, bf16[96,768]{1,0:T(8,128)(2,1)}, u32[]{:S(2)}, u32[]{:S(2)}) collective-permute-start(bf16[96,768]{1,0:T(8,128)(2,1)} %get-tuple-element.389), channel_id=1, source_target_pairs={{0,24},{4,28},{8,16},{12,20},{16,8},{20,12},{24,0},{28,4},{1,25},{... | collective-permute-start | bytes 442376 | tf_op jit(solution)/shard_map/ppermute | solution.py:29
  510.4 48.3 %collective-permute-start.57 = (bf16[96,768]{1,0:T(8,128)(2,1)}, bf16[96,768]{1,0:T(8,128)(2,1)}, u32[]{:S(2)}, u32[]{:S(2)}) collective-permute-start(bf16[96,768]{1,0:T(8,128)(2,1)} %get-tuple-element.390), channel_id=1, source_target_pairs={{0,8},{4,12},{8,0},{12,4},{16,24},{20,28},{24,16},{28,20},{1,9},{5... | collective-permute-start | bytes 442376 | tf_op jit(solution)/shard_map/ppermute | solution.py:29
  550.7 25.5 %collective-permute-start.61 = (bf16[384,1152]{1,0:T(8,128)(2,1)S(1)}, bf16[384,1152]{1,0:T(8,128)(2,1)S(1)}, u32[]{:S(2)}, u32[]{:S(2)}) collective-permute-start(bf16[384,1152]{1,0:T(8,128)(2,1)S(1)} %copy-done.37), channel_id=1, source_target_pairs={{0,4},{4,0},{8,12},{12,8},{16,20},{20,16},{24,28},{28,24},{1,5},{5... | collective-permute-start | bytes 2654216 | tf_op jit(solution)/shard_map/ppermute | solution.py:29
  557.7 18.5 %collective-permute-start.60 = (bf16[384,192]{1,0:T(8,128)(2,1)S(1)}, bf16[384,192]{1,0:T(8,128)(2,1)S(1)}, u32[]{:S(2)}, u32[]{:S(2)}) collective-permute-start(bf16[384,192]{1,0:T(8,128)(2,1)S(1)} %copy-done.44), channel_id=1, source_target_pairs={{0,4},{4,0},{8,12},{12,8},{16,20},{20,16},{24,28},{28,24},{1,5},{5... | collective-permute-start | bytes 442376 | tf_op jit(solution)/shard_map/ppermute | solution.py:29
  558.7 40.2 %collective-permute-start.62 = (bf16[768,1536]{1,0:T(8,128)(2,1)}, bf16[768,1536]{1,0:T(8,128)(2,1)}, u32[]{:S(2)}, u32[]{:S(2)}) collective-permute-start(bf16[768,1536]{1,0:T(8,128)(2,1)} %convolution_convert_fusion), channel_id=1, source_target_pairs={{0,1},{1,0},{2,3},{3,2},{4,5},{5,4},{6,7},{7,6},{8,9},{9,8},{10,11... | collective-permute-start | bytes 7077896 | tf_op jit(solution)/shard_map/ppermute | solution.py:29
  598.9 18.7 %collective-permute-start.63 = (bf16[96,192]{1,0:T(8,128)(2,1)}, bf16[96,192]{1,0:T(8,128)(2,1)}, u32[]{:S(2)}, u32[]{:S(2)}) collective-permute-start(bf16[96,192]{1,0:T(8,128)(2,1)} %get-tuple-element.406), channel_id=1, source_target_pairs={{0,8},{4,12},{8,0},{12,4},{16,24},{20,28},{24,16},{28,20},{1,9},{5... | collective-permute-start | bytes 110600 | tf_op jit(solution)/shard_map/ppermute | solution.py:29
  600.7 18.3 %collective-permute-start.64 = (bf16[96,192]{1,0:T(8,128)(2,1)}, bf16[96,192]{1,0:T(8,128)(2,1)}, u32[]{:S(2)}, u32[]{:S(2)}) collective-permute-start(bf16[96,192]{1,0:T(8,128)(2,1)} %get-tuple-element.407), channel_id=1, source_target_pairs={{0,16},{4,20},{8,24},{12,28},{16,0},{20,4},{24,8},{28,12},{1,17},{... | collective-permute-start | bytes 110600 | tf_op jit(solution)/shard_map/ppermute | solution.py:29
  601.1 19.1 %collective-permute-start.65 = (bf16[96,192]{1,0:T(8,128)(2,1)}, bf16[96,192]{1,0:T(8,128)(2,1)}, u32[]{:S(2)}, u32[]{:S(2)}) collective-permute-start(bf16[96,192]{1,0:T(8,128)(2,1)} %get-tuple-element.408), channel_id=1, source_target_pairs={{0,24},{4,28},{8,16},{12,20},{16,8},{20,12},{24,0},{28,4},{1,25},{... | collective-permute-start | bytes 110600 | tf_op jit(solution)/shard_map/ppermute | solution.py:29
  619.0 46.6 %collective-permute-start.69 = (bf16[768,384]{1,0:T(8,128)(2,1)}, bf16[768,384]{1,0:T(8,128)(2,1)}, u32[]{:S(2)}, u32[]{:S(2)}) collective-permute-start(bf16[768,384]{1,0:T(8,128)(2,1)} %convolution_convert_fusion.6), channel_id=1, source_target_pairs={{0,1},{1,0},{2,3},{3,2},{4,5},{5,4},{6,7},{7,6},{8,9},{9,8},{10,11... | collective-permute-start | bytes 1769480 | tf_op jit(solution)/shard_map/ppermute | solution.py:29
  620.2 47.7 %collective-permute-start.70 = (bf16[384,1536]{1,0:T(8,128)(2,1)}, bf16[384,1536]{1,0:T(8,128)(2,1)}, u32[]{:S(2)}, u32[]{:S(2)}) collective-permute-start(bf16[384,1536]{1,0:T(8,128)(2,1)} %slice.1310), channel_id=1, source_target_pairs={{0,4},{4,0},{8,12},{12,8},{16,20},{20,16},{24,28},{28,24},{1,5},{5... | collective-permute-start | bytes 3538952 | tf_op jit(solution)/shard_map/ppermute | solution.py:29
  621.2 46.7 %collective-permute-start.71 = (bf16[768,768]{1,0:T(8,128)(2,1)}, bf16[768,768]{1,0:T(8,128)(2,1)}, u32[]{:S(2)}, u32[]{:S(2)}) collective-permute-start(bf16[768,768]{1,0:T(8,128)(2,1)} %slice.1309), channel_id=1, source_target_pairs={{0,2},{1,3},{2,0},{3,1},{4,6},{5,7},{6,4},{7,5},{8,10},{9,11},{10,... | collective-permute-start | bytes 3538952 | tf_op jit(solution)/shard_map/ppermute | solution.py:29
  632.7 44.1 %collective-permute-start.72 = (bf16[96,576]{1,0:T(8,128)(2,1)}, bf16[96,576]{1,0:T(8,128)(2,1)}, u32[]{:S(2)}, u32[]{:S(2)}) collective-permute-start(bf16[96,576]{1,0:T(8,128)(2,1)} %get-tuple-element.424), channel_id=1, source_target_pairs={{0,8},{4,12},{8,0},{12,4},{16,24},{20,28},{24,16},{28,20},{1,9},{5... | collective-permute-start | bytes 331784 | tf_op jit(solution)/shard_map/ppermute | solution.py:29
  633.6 43.2 %collective-permute-start.73 = (bf16[96,576]{1,0:T(8,128)(2,1)}, bf16[96,576]{1,0:T(8,128)(2,1)}, u32[]{:S(2)}, u32[]{:S(2)}) collective-permute-start(bf16[96,576]{1,0:T(8,128)(2,1)} %get-tuple-element.425), channel_id=1, source_target_pairs={{0,16},{4,20},{8,24},{12,28},{16,0},{20,4},{24,8},{28,12},{1,17},{... | collective-permute-start | bytes 331784 | tf_op jit(solution)/shard_map/ppermute | solution.py:29
  698.2 32.6 %collective-permute-start.75 = (bf16[768,1152]{1,0:T(8,128)(2,1)}, bf16[768,1152]{1,0:T(8,128)(2,1)}, u32[]{:S(2)}, u32[]{:S(2)}) collective-permute-start(bf16[768,1152]{1,0:T(8,128)(2,1)} %convolution_convert_fusion.4), channel_id=1, source_target_pairs={{0,1},{1,0},{2,3},{3,2},{4,5},{5,4},{6,7},{7,6},{8,9},{9,8},{10,11... | collective-permute-start | bytes 5308424 | tf_op jit(solution)/shard_map/ppermute | solution.py:29
  707.1 23.7 %collective-permute-start.77 = (bf16[384,768]{1,0:T(8,128)(2,1)S(1)}, bf16[384,768]{1,0:T(8,128)(2,1)S(1)}, u32[]{:S(2)}, u32[]{:S(2)}) collective-permute-start(bf16[384,768]{1,0:T(8,128)(2,1)S(1)} %slice.1316), channel_id=1, source_target_pairs={{0,2},{1,3},{2,0},{3,1},{4,6},{5,7},{6,4},{7,5},{8,10},{9,11},{10,... | collective-permute-start | bytes 1769480 | tf_op jit(solution)/shard_map/ppermute | solution.py:29
  708.9 21.9 %collective-permute-start.78 = (bf16[384,768]{1,0:T(8,128)(2,1)S(1)}, bf16[384,768]{1,0:T(8,128)(2,1)S(1)}, u32[]{:S(2)}, u32[]{:S(2)}) collective-permute-start(bf16[384,768]{1,0:T(8,128)(2,1)S(1)} %slice.1315), channel_id=1, source_target_pairs={{0,4},{4,0},{8,12},{12,8},{16,20},{20,16},{24,28},{28,24},{1,5},{5... | collective-permute-start | bytes 1769480 | tf_op jit(solution)/shard_map/ppermute | solution.py:29
  740.1 24.1 %collective-permute-start.86 = (bf16[384,1152]{1,0:T(8,128)(2,1)S(1)}, bf16[384,1152]{1,0:T(8,128)(2,1)S(1)}, u32[]{:S(2)}, u32[]{:S(2)}) collective-permute-start(bf16[384,1152]{1,0:T(8,128)(2,1)S(1)} %slice.1313), channel_id=1, source_target_pairs={{0,4},{4,0},{8,12},{12,8},{16,20},{20,16},{24,28},{28,24},{1,5},{5... | collective-permute-start | bytes 2654216 | tf_op jit(solution)/shard_map/ppermute | solution.py:29
  742.7 19.4 %collective-permute-start.83 = (bf16[96,768]{1,0:T(8,128)(2,1)S(1)}, bf16[96,768]{1,0:T(8,128)(2,1)S(1)}, u32[]{:S(2)}, u32[]{:S(2)}) collective-permute-start(bf16[96,768]{1,0:T(8,128)(2,1)S(1)} %get-tuple-element.443), channel_id=1, source_target_pairs={{0,16},{4,20},{8,24},{12,28},{16,0},{20,4},{24,8},{28,12},{1,17},{... | collective-permute-start | bytes 442376 | tf_op jit(solution)/shard_map/ppermute | solution.py:29
  (154 other events, 1646.8 us)

commit v3 on v2

v3 whole, which is shorter than its diff:
```python
from functools import partial
import math

import jax
import jax.numpy as jnp
from jax import lax
from jax.experimental import pallas as pl
from jax.experimental.pallas import tpu as pltpu
from jax.sharding import PartitionSpec as P

HD = 64
ROW = 2048
NORM_EPS = 1e-05
BF = jnp.bfloat16
F32 = jnp.float32


def xor_groups(n):
    groups, span = [[1]], 2
    while span < n:
        radix = min(4, n // span)
        groups.append([span * k for k in range(1, radix)])
        span *= radix
    return groups[::-1]


def swap(x, axis, mask):
    n = lax.axis_size(axis)
    return lax.ppermute(x, axis, [(i, i ^ mask) for i in range(n)])


def forward_shift(x, by):
    n = lax.axis_size("head")
    return lax.ppermute(x, "head", [(i, i + by) for i in range(n - by)])


def backward_shift(x, by):
    n = lax.axis_size("head")
    return lax.ppermute(x, "head", [(i + by, i) for i in range(n - by)])


def block_order(groups):
    order = [0]
    for masks in groups:
        order = order + [r ^ m for m in masks for r in order]
    return order


def spread(x, axis, masks, dim):
    return jnp.concatenate([x] + [swap(x, axis, m) for m in masks], axis=dim)


def pair_columns(own, other):
    heads = own.shape[1] // (4 * HD)
    pieces = []
    for part, j in [(part, j) for j in range(heads) for part in range(3)] + [(3, j) for j in range(heads)]:
        at = (part * heads + j) * HD
        pieces += [own[:, at : at + HD], other[:, at : at + HD]]
    return jnp.concatenate(pieces, axis=1)


class Transfers:
    def __init__(self, steps):
        self.steps, self.coming, self.result = steps, None, None
        self.wanted = next(steps)

    def give(self, arrived):
        try:
            self.wanted = self.steps.send(arrived)
        except StopIteration as end:
            self.wanted, self.result = [], end.value


def finish(value, chains):
    while True:
        chains = [chain for chain in chains if chain.result is None]
        if not chains:
            return value
        value = advance(value, *chains)


def shift_steps(state, shift):
    arrived = yield [(state, lambda array: shift(array, 1)), (state, lambda array: shift(array, 2))]
    return arrived


def together(values):
    return lax.optimization_barrier(values)


def start(*chains):
    for chain in chains:
        chain.coming = [exchange(array) for array, exchange in chain.wanted]


def advance(value, *chains):
    value, arrived = together((value, [chain.coming for chain in chains]))
    for chain, pieces in zip(chains, arrived):
        chain.give(pieces)
    value, sends = together((value, [[array for array, _ in chain.wanted] for chain in chains]))
    for chain, arrays in zip(chains, sends):
        chain.coming = [exchange(array) for array, (_, exchange) in zip(arrays, chain.wanted)]
    return value


def to(axis, mask):
    return lambda array: swap(array, axis, mask)


def spread_steps(x, masks):
    arrived = yield [(x, to("dp", m)) for m in masks]
    return jnp.concatenate([x] + arrived, axis=0)


def outer_steps(x, groups):
    for masks in groups[:-1]:
        x = yield from spread_steps(x, masks)
    return x


def heads_steps(shard, groups):
    x = yield from outer_steps(shard, groups)
    masks = groups[-1]
    c = x.shape[1] // 2
    qk, vo = x[:, :c], x[:, c:]
    arrived = yield [(qk, to("dp", m)) for m in masks] + [(vo, to("head", 2))]
    qk = jnp.concatenate([qk] + arrived[:-1], axis=0)
    vo = jnp.concatenate([vo, arrived[-1]], axis=1)
    arrived = yield [(qk, to("head", 2))] + [(vo, to("dp", m)) for m in masks]
    vo = jnp.concatenate([vo] + arrived[1:], axis=0)
    own = jnp.concatenate([qk, vo[:, :c]], axis=1)
    other = jnp.concatenate([arrived[0], vo[:, c:]], axis=1)
    half = pair_columns(own, other)
    arrived = yield [(half, to("head", 1))]
    return half, arrived[0]


def hidden_steps(shard, groups):
    x = yield from outer_steps(shard, groups)
    masks = groups[-1]
    c = x.shape[1] // 2
    up, down = x[:, :c], x[:, c:]
    arrived = yield [(up, to("dp", m)) for m in masks] + [(down, to("head", 2))]
    up = jnp.concatenate([up] + arrived[:-1], axis=0)
    down = jnp.concatenate([down, arrived[-1]], axis=1)
    arrived = yield [(up, to("head", 2))] + [(down, to("dp", m)) for m in masks]
    down = jnp.concatenate([down] + arrived[1:], axis=0)
    half = jnp.stack([jnp.stack([up, arrived[0]]), jnp.stack([down[:, :c], down[:, c:]])])
    arrived = yield [(half, to("head", 1))]
    return half, arrived[0]


def add(kept, *pieces):
    return (kept.astype(F32) + sum(piece.astype(F32) for piece in pieces)).astype(BF)


def last_rows(parts, groups):
    x = jnp.concatenate(parts, axis=1)
    for masks in groups[:-1][::-1]:
        rows = x.shape[0] // (len(masks) + 1)
        pieces = [x[j * rows : (j + 1) * rows] for j in range(len(masks) + 1)]
        arrived = yield [(piece, to("dp", m)) for piece, m in zip(pieces[1:], masks)]
        x = add(pieces[0], *arrived) if masks is not groups[0] else pieces[0].astype(F32) + sum(a.astype(F32) for a in arrived)
    return x


def sum_steps(other, join, split, groups):
    arrived = yield [(other, to("head", 1))]
    y_first, x_first = split(join(arrived[0]))
    (mask,) = groups[-1]
    rows = x_first.shape[1] // 2
    arrived = yield [(y_first[:, rows:], to("dp", mask)), (x_first[1], to("head", 2))]
    y_first = add(y_first[:, :rows], arrived[0])
    x_first = add(x_first[0], arrived[1])
    arrived = yield [(y_first[1], to("head", 2)), (x_first[rows:], to("dp", mask))]
    y_first = add(y_first[0], arrived[0])
    x_first = add(x_first[:rows], arrived[1])
    return (yield from last_rows([y_first, x_first], groups))


def dot(a, b):
    return lax.dot_general(a, b, (((1,), (0,)), ((), ())), preferred_element_type=F32)


def dot_t(a, b):
    return lax.dot_general(a, b, (((1,), (1,)), ((), ())), preferred_element_type=F32)


def t_dot(a, b):
    return lax.dot_general(a, b, (((0,), (0,)), ((), ())), preferred_element_type=F32)


def places(lengths, position):
    n = lengths.shape[0]
    upto = jnp.arange(n)[:, None] <= jnp.arange(n)[None, :]
    ends = jnp.sum(jnp.where(upto, lengths[:, None], 0), axis=0)
    passed = (position[:, None] >= ends[None, :]).astype(jnp.int32)
    doc = jnp.sum(passed, axis=1)
    start = jnp.sum(passed * lengths[None, :], axis=1)
    here = (doc[:, None] == jnp.arange(n)[None, :]).astype(jnp.int32)
    size = jnp.sum(here * lengths[None, :], axis=1)
    return doc, start, size


STATE_ROWS = 144
PAIR = 2 * HD
QKV = 3 * PAIR
VMEM_LIMIT = 60 * 2**20
EXPECTED_US = {
    "project": 10,
    "attend": 15,
    "hidden": 28,
    "hidden_back_other": 16,
    "hidden_back": 26,
    "attend_back": 28,
    "project_sums": 15,
    "project_back": 10,
}


def run(kernel, grid, ins, outs, scratch=(), name=None):
    in_specs, arrays = [], []
    for array, block, index in ins:
        arrays.append(array)
        if block is None:
            in_specs.append(pl.BlockSpec(memory_space=index))
        else:
            in_specs.append(pl.BlockSpec(block, index))
    return pl.pallas_call(
        kernel,
        grid=grid,
        in_specs=in_specs,
        out_specs=[
            pl.BlockSpec(memory_space=index) if block is None else pl.BlockSpec(block, index)
            for _, _, block, index in outs
        ],
        out_shape=[jax.ShapeDtypeStruct(shape, dtype) for shape, dtype, _, _ in outs],
        scratch_shapes=list(scratch),
        compiler_params=pltpu.CompilerParams(
            dimension_semantics=("arbitrary",) * len(grid), vmem_limit_bytes=VMEM_LIMIT
        ),
        cost_estimate=pl.CostEstimate(flops=EXPECTED_US[name] * 10**9, bytes_accessed=1000, transcendentals=0),
        name=name,
    )(*arrays)


def low_lanes(shape):
    return lax.broadcasted_iota(jnp.int32, shape, 1) < HD


def relu(x):
    return jnp.maximum(x, jnp.zeros_like(x))


def moments(x):
    mean = jnp.mean(x, axis=-1, keepdims=True)
    centred = x - mean
    rstd = lax.rsqrt(jnp.mean(centred * centred, axis=-1, keepdims=True) + NORM_EPS)
    return centred * rstd, rstd


def packed(c, s, c_sum, s_sum):
    lo = low_lanes((HD, PAIR))
    first = jnp.where(lo, c[:HD], c[HD:])
    second = jnp.where(lo, s[:HD], s[HD:])
    at = lax.broadcasted_iota(jnp.int32, (STATE_ROWS - PAIR, PAIR), 0)
    sums = jnp.where(at == 0, c_sum, jnp.where(at == 1, s_sum, 0.0))
    return jnp.concatenate([first, second, sums], axis=0).astype(BF)


def unpacked(st):
    lo = low_lanes((HD, PAIR))
    both = []
    for at in (0, HD):
        x = st[at : at + HD]
        both.append(jnp.concatenate([jnp.where(lo, x, 0.0), jnp.where(lo, 0.0, x)], axis=0))
    return both[0], both[1], st[PAIR : PAIR + 1], st[PAIR + 1 : PAIR + 2]


def received(near, far, flag_ref, b):
    near, far = near.astype(F32), far.astype(F32)
    return (
        near * flag_ref[b, 0]
        + pltpu.roll(near, HD, 1) * flag_ref[b, 1]
        + pltpu.roll(far, HD, 1) * flag_ref[b, 2]
    )


def project_kernel(row, x_ref, par_ref, col_ref, own_ref, other_ref, normed_ref, mixed_ref, state_ref):
    xhat, _ = moments(x_ref[...])
    normed = (xhat * par_ref[row : row + 1, :] + par_ref[row + 2 : row + 3, :]).astype(BF)
    normed_ref[...] = normed
    half = own_ref.shape[1]
    mixed_ref[:, :half] = dot(normed, own_ref[...]).astype(BF)
    mixed_ref[:, half:] = dot(normed, other_ref[...]).astype(BF)
    for p in range(2 * half // QKV):
        at = p * QKV
        k = relu(mixed_ref[:, at + PAIR : at + 2 * PAIR]).astype(F32)
        v = mixed_ref[:, at + 2 * PAIR : at + QKV]
        kc = (k * col_ref[:, 2:3]).astype(BF)
        ks = (k * col_ref[:, 3:4]).astype(BF)
        state_ref[0, p] = packed(
            t_dot(kc, v),
            t_dot(ks, v),
            jnp.sum(kc.astype(F32), axis=0, keepdims=True),
            jnp.sum(ks.astype(F32), axis=0, keepdims=True),
        )


def project(x, params, row, own, other, col, rows):
    tokens, width = x.shape
    half = 3 * width // 2
    pairs = 2 * half // QKV
    return run(
        partial(project_kernel, row),
        (tokens // rows,),
        [
            (x, (rows, width), lambda i: (i, 0)),
            (params, params.shape, lambda i: (0, 0)),
            (col, (rows, col.shape[1]), lambda i: (i, 0)),
            (own, (width, half), lambda i: (0, 0)),
            (other, (width, half), lambda i: (0, 0)),
        ],
        [
            ((tokens, width), BF, (rows, width), lambda i: (i, 0)),
            ((tokens, 2 * half), BF, (rows, 2 * half), lambda i: (i, 0)),
            ((tokens // rows, pairs, STATE_ROWS, PAIR), BF, (1, pairs, STATE_ROWS, PAIR), lambda i: (i, 0, 0, 0)),
        ],
        name="project",
    )


def pair_grid(mixed, rows):
    tokens, width = mixed.shape
    return (tokens // rows, width // QKV)


def mask_of(col_ref, row_ref):
    rows = col_ref.shape[0]
    shape = (rows, rows)
    t = lax.broadcasted_iota(jnp.int32, shape, 0)
    u = lax.broadcasted_iota(jnp.int32, shape, 1)
    cosine = col_ref[:, 4:5] * row_ref[0:1, :] + col_ref[:, 5:6] * row_ref[1:2, :]
    same = col_ref[:, 6:7] == row_ref[2:3, :]
    return cosine, same, t, u


def attend_kernel(col_ref, row_ref, mixed_ref, num_ref, den_ref, mask_ref):
    rows = mixed_ref.shape[0]

    @pl.when(pl.program_id(1) == 0)
    def _():
        cosine, same, t, u = mask_of(col_ref, row_ref)
        mask_ref[...] = jnp.where(same & (t >= u), cosine, 0.0)

    q, k, v = relu(mixed_ref[:, :PAIR]), relu(mixed_ref[:, PAIR : 2 * PAIR]), mixed_ref[:, 2 * PAIR :]
    lo = low_lanes((rows, PAIR))
    zero = jnp.zeros_like(q)
    q_of = [jnp.where(lo, q, zero), jnp.where(lo, zero, q)]
    v_one = jnp.concatenate([v, jnp.ones_like(v)], axis=1)
    step = min(256, rows)
    for at in range(0, rows, step):
        end = at + step
        here = slice(at, end)
        mask = mask_ref[here, :end]
        parts = []
        for head in range(2):
            w = (dot_t(q_of[head][here], k[:end]) * mask).astype(BF)
            parts.append(dot(w, v_one[:end]))
        pick = low_lanes((step, PAIR))
        num_ref[here, :] = jnp.where(pick, parts[0][:, :PAIR], parts[1][:, :PAIR])
        den_ref[here, :] = jnp.where(pick, parts[0][:, PAIR:], parts[1][:, PAIR:])


def attend(mixed, col, row, rows):
    grid = pair_grid(mixed, rows)
    tokens = mixed.shape[0]
    width = grid[1] * PAIR
    return run(
        attend_kernel,
        grid,
        [
            (col, (rows, col.shape[1]), lambda b, p: (b, 0)),
            (row, (row.shape[0], rows), lambda b, p: (0, b)),
            (mixed, (rows, QKV), lambda b, p: (b, p)),
        ],
        [
            ((tokens, width), F32, (rows, PAIR), lambda b, p: (b, p)),
            ((tokens, width), F32, (rows, PAIR), lambda b, p: (b, p)),
        ],
        scratch=[pltpu.VMEM((rows, rows), F32)],
        name="attend",
    )


def head_ones():
    return jnp.where(
        (lax.broadcasted_iota(jnp.int32, (PAIR, PAIR), 0) < HD) == low_lanes((PAIR, PAIR)), 1.0, 0.0
    ).astype(BF)


def gelu_and_slope(x):
    c = math.sqrt(2.0 / math.pi)
    k = 0.044715 * c
    x2 = x * x
    half = 0.5 + 0.5 * jnp.tanh(x * (c + k * x2))
    act = x * half
    slope = half + act * (1.0 - half) * (2.0 * c + (6.0 * k) * x2)
    return act.astype(BF), slope.astype(BF)


def copy(source, target, sem):
    made = pltpu.make_async_copy(source, target, sem)
    made.start()
    return made


def hidden_kernel(
    row, seq, flag_ref, par_ref, col_ref, near_ref, far_ref,
    x_hbm, num_hbm, den_hbm, mixed_hbm, ao_hbm, ax_hbm, wo_hbm, wx_hbm,
    mid_hbm, normed_hbm, act_hbm, slope_hbm, out_hbm, att_hbm, inv_hbm,
    x_v, num_v, den_v, q_v, att_v, inv_v, a_v, w_v, mid_v, normed_v, act_v, slope_v,
    x_sem, num_sem, q_sem, a_sem, w_sem, row_sem, chunk_sem,
):
    tokens, width = x_v.shape
    rows = min(256, tokens)
    n = tokens // rows
    half = width // 2
    pairs = width // PAIR
    here = [pl.ds(i * rows, rows) for i in range(n)]
    seqs = [pl.ds(b * seq, seq) for b in range(tokens // seq)]
    q_in = []
    for p in range(pairs):
        q_in.append(copy(mixed_hbm.at[:, pl.ds(p * QKV, PAIR)], q_v.at[:, pl.ds(p * PAIR, PAIR)], q_sem.at[p]))
    num_in = []
    for b, at in enumerate(seqs):
        num_in.append(
            [copy(num_hbm.at[at], num_v.at[at], num_sem.at[0, b]), copy(den_hbm.at[at], den_v.at[at], num_sem.at[1, b])]
        )
    into = [copy(hbm.at[:, pl.ds(3 * half, half)], a_v.at[i], a_sem.at[i]) for i, hbm in enumerate((ao_hbm, ax_hbm))]
    x_in = [copy(x_hbm.at[here[i]], x_v.at[here[i]], x_sem.at[i]) for i in range(n)]
    for c in range(4):
        hbm = wo_hbm if c < 2 else wx_hbm
        for kind in range(2):
            copy(hbm.at[kind, c % 2], w_v.at[kind, c], w_sem.at[kind, c])
    for made in q_in:
        made.wait()
    out = []
    ones = head_ones()
    for b, at in enumerate(seqs):
        for made in num_in[b]:
            made.wait()
        for p in range(pairs):
            lanes = pl.ds(p * PAIR, PAIR)
            c, s, c_sum, s_sum = unpacked(received(near_ref[b, (p + pairs // 2) % pairs], far_ref[b, p], flag_ref, b))
            q = relu(q_v[at, lanes]).astype(F32)
            qc, qs = q * col_ref[at, 0:1], q * col_ref[at, 1:2]
            num = num_v[at, lanes] + dot(
                jnp.concatenate([qc, qs], axis=1).astype(BF), jnp.concatenate([c, s], axis=0).astype(BF)
            )
            den = den_v[at, lanes] + dot((qc * c_sum + qs * s_sum).astype(BF), ones)
            inv = 1.0 / (den + 1.0)
            att_v[at, lanes] = (num * inv).astype(BF)
            inv_v[at, lanes] = inv.astype(BF)
        out.append(copy(att_v.at[at], att_hbm.at[at], num_sem.at[2, b]))
        out.append(copy(inv_v.at[at], inv_hbm.at[at], num_sem.at[3, b]))
    for made in into:
        made.wait()
    for i in range(n):
        x_in[i].wait()
        mid = x_v[here[i], :] + dot_t(att_v[here[i], :half], a_v[0]) + dot_t(att_v[here[i], half:], a_v[1])
        mid_v[here[i], :] = mid
        x_v[here[i], :] = mid
        xhat, _ = moments(mid)
        normed_v[here[i], :] = (xhat * par_ref[row : row + 1, :] + par_ref[row + 2 : row + 3, :]).astype(BF)
        out.append(copy(mid_v.at[here[i]], mid_hbm.at[here[i]], row_sem.at[0, i]))
        out.append(copy(normed_v.at[here[i]], normed_hbm.at[here[i]], row_sem.at[1, i]))

    @pl.loop(0, 4)
    def _(c):
        for kind in range(2):
            pltpu.make_async_copy(wo_hbm.at[kind, 0], w_v.at[kind, c], w_sem.at[kind, c]).wait()
        for i in range(n):
            act, slope = gelu_and_slope(dot(normed_v[here[i], :], w_v[0, c]))
            act_v[c, here[i], :] = act
            slope_v[c, here[i], :] = slope
            x_v[here[i], :] += dot_t(act, w_v[1, c])
        copy(act_v.at[c], act_hbm.at[c], chunk_sem.at[0, c])
        copy(slope_v.at[c], slope_hbm.at[c], chunk_sem.at[1, c])

    out.append(copy(x_v, out_hbm, row_sem.at[2, 0]))
    for c in range(4):
        pltpu.make_async_copy(act_v.at[c], act_hbm.at[c], chunk_sem.at[0, c]).wait()
        pltpu.make_async_copy(slope_v.at[c], slope_hbm.at[c], chunk_sem.at[1, c]).wait()
    for made in out:
        made.wait()


def hidden(x, params, row, intra, mixed, states, flags, col, w_att, w_hid, seq):
    tokens, width = x.shape
    chunk = w_hid[0].shape[3]
    pairs = width // PAIR
    n = tokens // min(256, tokens)
    dma = pltpu.SemaphoreType.DMA
    whole = lambda i: (0, 0)
    rows_of = lambda dtype: pltpu.VMEM((tokens, width), dtype)
    return run(
        partial(hidden_kernel, row, seq),
        (1,),
        [(flags, None, pltpu.SMEM), (params, params.shape, whole), (col, col.shape, whole)]
        + [(s, s.shape, lambda i: (0, 0, 0, 0)) for s in states]
        + [(a, None, pl.ANY) for a in (x, *intra, mixed, *w_att, *w_hid)],
        [
            ((tokens, width), F32, None, pl.ANY),
            ((tokens, width), BF, None, pl.ANY),
            ((4, tokens, chunk), BF, None, pl.ANY),
            ((4, tokens, chunk), BF, None, pl.ANY),
            ((tokens, width), F32, None, pl.ANY),
            ((tokens, width), BF, None, pl.ANY),
            ((tokens, width), BF, None, pl.ANY),
        ],
        scratch=[
            rows_of(F32), rows_of(F32), rows_of(F32), rows_of(BF), rows_of(BF), rows_of(BF),
            pltpu.VMEM((2, width, width // 2), BF),
            pltpu.VMEM((2, 4, width, chunk), BF),
            rows_of(F32), rows_of(BF),
            pltpu.VMEM((4, tokens, chunk), BF),
            pltpu.VMEM((4, tokens, chunk), BF),
            dma((n,)), dma((4, tokens // seq)), dma((pairs,)), dma((2,)), dma((2, 4)), dma((3, n)), dma((2, 4)),
        ],
        name="hidden",
    )


def hidden_sums(w_hbm, act_hbm, slope_hbm, sum_hbm, low_v, acc_v, normed_v, pre_v, act_v, slope_v, w_v, sum_v, w_sem, act_sem, sum_sem):
    tokens, width = low_v.shape
    rows = min(256, tokens)

    @pl.loop(0, 2)
    def _(c):
        for kind in range(2):
            pltpu.make_async_copy(w_hbm.at[kind, 0], w_v.at[kind, c], w_sem.at[kind, c]).wait()
        pltpu.make_async_copy(act_hbm.at[0], act_v.at[c], act_sem.at[0, c]).wait()
        pltpu.make_async_copy(slope_hbm.at[0], slope_v.at[c], act_sem.at[1, c]).wait()
        for i in range(tokens // rows):
            here = pl.ds(i * rows, rows)
            pre = (dot(low_v[here, :], w_v[1, c]) * slope_v[c, here, :].astype(F32)).astype(BF)
            pre_v[here, :] = pre
            acc_v[here, :] += dot_t(pre, w_v[0, c])
        sum_v[c, 1] = t_dot(low_v[...], act_v[c]).astype(BF)
        sum_v[c, 0] = t_dot(normed_v[...], pre_v[...]).astype(BF)
        for kind in range(2):
            copy(sum_v.at[c, kind], sum_hbm.at[kind, c], sum_sem.at[c, kind])


def start_hidden(w_hbm, act_hbm, slope_hbm, first, act_v, slope_v, w_v, w_sem, act_sem):
    for c in range(2):
        copy(w_hbm.at[1, c], w_v.at[1, c], w_sem.at[1, c])
        copy(slope_hbm.at[first + c], slope_v.at[c], act_sem.at[1, c])
        copy(w_hbm.at[0, c], w_v.at[0, c], w_sem.at[0, c])
        copy(act_hbm.at[first + c], act_v.at[c], act_sem.at[0, c])


def wait_sums(sum_v, sum_hbm, sum_sem):
    for c in range(2):
        for kind in range(2):
            pltpu.make_async_copy(sum_v.at[c, kind], sum_hbm.at[kind, c], sum_sem.at[c, kind]).wait()


def hidden_back_other_kernel(
    g_hbm, normed_hbm, act_hbm, slope_hbm, w_hbm,
    acc_hbm, sum_hbm,
    g_v, normed_v, act_v, slope_v, w_v, low_v, acc_v, pre_v, sum_v,
    g_sem, w_sem, act_sem, sum_sem,
):
    tokens, width = g_v.shape
    rows = min(256, tokens)
    n = tokens // rows
    here = [pl.ds(i * rows, rows) for i in range(n)]
    g_in = [copy(g_hbm.at[here[i]], g_v.at[here[i]], g_sem.at[i]) for i in range(n)]
    normed_in = copy(normed_hbm, normed_v, g_sem.at[n])
    start_hidden(w_hbm, act_hbm, slope_hbm, 2, act_v, slope_v, w_v, w_sem, act_sem)
    for i in range(n):
        g_in[i].wait()
        low_v[here[i], :] = g_v[here[i], :].astype(BF)
        acc_v[here[i], :] = jnp.zeros((rows, width), F32)
    normed_in.wait()
    hidden_sums(w_hbm, act_hbm, slope_hbm, sum_hbm, low_v, acc_v, normed_v, pre_v, act_v, slope_v, w_v, sum_v, w_sem, act_sem, sum_sem)
    out = copy(acc_v, acc_hbm, g_sem.at[0])
    wait_sums(sum_v, sum_hbm, sum_sem)
    out.wait()


def hidden_back_kernel(
    row, seq, par_ref, col_ref, g_hbm, acc_hbm, mid_hbm, normed_hbm, act_hbm, slope_hbm, w_hbm,
    ao_hbm, ax_hbm, mixed_hbm, att_hbm, inv_hbm,
    out_hbm, gn_hbm, norm_ref, state_ref, sum_hbm,
    g_v, mid_v, normed_v, act_v, slope_v, w_v, a_v, q_v, att_v, inv_v,
    low_v, acc_v, pre_v, sum_v, gn_v,
    g_sem, w_sem, act_sem, in_sem, q_sem, sum_sem, out_sem,
):
    tokens, width = g_v.shape
    rows = min(256, tokens)
    n = tokens // rows
    half = width // 2
    pairs = width // PAIR
    here = [pl.ds(i * rows, rows) for i in range(n)]
    g_in = [copy(g_hbm.at[here[i]], g_v.at[here[i]], g_sem.at[0, i]) for i in range(n)]
    acc_in = [copy(acc_hbm.at[here[i]], acc_v.at[here[i]], g_sem.at[1, i]) for i in range(n)]
    normed_in = copy(normed_hbm, normed_v, in_sem.at[0])
    start_hidden(w_hbm, act_hbm, slope_hbm, 0, act_v, slope_v, w_v, w_sem, act_sem)
    late = [
        copy(mid_hbm, mid_v, in_sem.at[1]),
        copy(att_hbm, att_v, in_sem.at[2]),
        copy(inv_hbm, inv_v, in_sem.at[3]),
    ]
    late += [copy(hbm.at[:, pl.ds(3 * half, half)], a_v.at[i], in_sem.at[4 + i]) for i, hbm in enumerate((ao_hbm, ax_hbm))]
    for p in range(pairs):
        late.append(copy(mixed_hbm.at[:, pl.ds(p * QKV, PAIR)], q_v.at[:, pl.ds(p * PAIR, PAIR)], q_sem.at[p]))
    norm_ref[...] = jnp.zeros_like(norm_ref)
    for i in range(n):
        g_in[i].wait()
        low_v[here[i], :] = g_v[here[i], :].astype(BF)
    for made in (*acc_in, normed_in):
        made.wait()
    hidden_sums(w_hbm, act_hbm, slope_hbm, sum_hbm, low_v, acc_v, normed_v, pre_v, act_v, slope_v, w_v, sum_v, w_sem, act_sem, sum_sem)
    for made in late:
        made.wait()
    out = []
    for i in range(n):
        grad = g_v[here[i], :] + norm_gradient(
            acc_v[here[i], :], mid_v[here[i], :], par_ref[row : row + 1, :], norm_ref
        )
        g_v[here[i], :] = grad
        out.append(copy(g_v.at[here[i]], out_hbm.at[here[i]], out_sem.at[0, i]))
        low = grad.astype(BF)
        inv = inv_v[here[i], :].astype(F32)
        gn_v[here[i], :half] = (dot(low, a_v[0]) * inv[:, :half]).astype(BF)
        gn_v[here[i], half:] = (dot(low, a_v[1]) * inv[:, half:]).astype(BF)
        out.append(copy(gn_v.at[here[i]], gn_hbm.at[here[i]], out_sem.at[1, i]))
    for b in range(tokens // seq):
        at = pl.ds(b * seq, seq)
        for p in range(pairs):
            lanes = pl.ds(p * PAIR, PAIR)
            gn = gn_v[at, lanes]
            e = dot((gn.astype(F32) * att_v[at, lanes].astype(F32)).astype(BF), head_ones())
            q = relu(q_v[at, lanes]).astype(F32)
            qc = (q * col_ref[at, 0:1]).astype(BF)
            qs = (q * col_ref[at, 1:2]).astype(BF)
            state_ref[b, p] = packed(
                t_dot(qc, gn),
                t_dot(qs, gn),
                -jnp.sum(qc.astype(F32) * e, axis=0, keepdims=True),
                -jnp.sum(qs.astype(F32) * e, axis=0, keepdims=True),
            )
    wait_sums(sum_v, sum_hbm, sum_sem)
    for made in out:
        made.wait()


def hidden_scratch(tokens, width, chunk):
    return [
        pltpu.VMEM((2, tokens, chunk), BF),
        pltpu.VMEM((2, tokens, chunk), BF),
        pltpu.VMEM((2, 2, width, chunk), BF),
    ]


def hidden_back_other(grad, saved, w_other):
    mid, normed, act, slope, mixed, att, inv = saved
    tokens, width = grad.shape
    chunk = w_other.shape[3]
    n = tokens // min(256, tokens)
    dma = pltpu.SemaphoreType.DMA
    rows_of = lambda dtype: pltpu.VMEM((tokens, width), dtype)
    return run(
        hidden_back_other_kernel,
        (1,),
        [(a, None, pl.ANY) for a in (grad, normed, act, slope, w_other)],
        [((tokens, width), F32, None, pl.ANY), ((2, 2, width, chunk), BF, None, pl.ANY)],
        scratch=[rows_of(F32), rows_of(BF)]
        + hidden_scratch(tokens, width, chunk)
        + [
            rows_of(BF), rows_of(F32),
            pltpu.VMEM((tokens, chunk), BF),
            pltpu.VMEM((2, 2, width, chunk), BF),
            dma((n + 1,)), dma((2, 2)), dma((2, 2)), dma((2, 2)),
        ],
        name="hidden_back_other",
    )


def hidden_back(grad, acc, params, row, saved, w_att, w_own, col, seq):
    mid, normed, act, slope, mixed, att, inv = saved
    tokens, width = grad.shape
    chunk = w_own.shape[3]
    pairs = width // PAIR
    n = tokens // min(256, tokens)
    dma = pltpu.SemaphoreType.DMA
    whole = lambda i: (0, 0)
    rows_of = lambda dtype: pltpu.VMEM((tokens, width), dtype)
    states = (tokens // seq, pairs, STATE_ROWS, PAIR)
    return run(
        partial(hidden_back_kernel, row, seq),
        (1,),
        [(params, params.shape, whole), (col, col.shape, whole)]
        + [(a, None, pl.ANY) for a in (grad, acc, mid, normed, act, slope, w_own, *w_att, mixed, att, inv)],
        [
            ((tokens, width), F32, None, pl.ANY),
            ((tokens, width), BF, None, pl.ANY),
            ((8, width), F32, (8, width), whole),
            (states, BF, states, lambda i: (0, 0, 0, 0)),
            ((2, 2, width, chunk), BF, None, pl.ANY),
        ],
        scratch=[rows_of(F32), rows_of(F32), rows_of(BF)]
        + hidden_scratch(tokens, width, chunk)
        + [
            pltpu.VMEM((2, width, width // 2), BF),
            rows_of(BF), rows_of(BF), rows_of(BF),
            rows_of(BF), rows_of(F32),
            pltpu.VMEM((tokens, chunk), BF),
            pltpu.VMEM((2, 2, width, chunk), BF),
            rows_of(BF),
            dma((2, n)), dma((2, 2)), dma((2, 2)), dma((6,)), dma((pairs,)), dma((2, 2)), dma((2, n)),
        ],
        name="hidden_back",
    )


def norm_gradient(grad, stream, gain, norm_ref):
    xhat, rstd = moments(stream)
    gx = grad * xhat
    norm_ref[0:1, :] += jnp.sum(gx, axis=0, keepdims=True)
    norm_ref[1:2, :] += jnp.sum(grad, axis=0, keepdims=True)
    g = grad * gain
    return rstd * (
        g - jnp.mean(g, axis=-1, keepdims=True) - xhat * jnp.mean(gx * gain, axis=-1, keepdims=True)
    )


def attend_back_kernel(
    flag_ref, col_ref, row_ref, mixed_ref, gn_ref, att_ref, near_ref, far_ref, out_ref, mask_ref, turned_ref,
):
    b, p = pl.program_id(0), pl.program_id(1)
    rows = mixed_ref.shape[0]

    @pl.when(p == 0)
    def _():
        cosine, same, t, u = mask_of(col_ref, row_ref)
        mask_ref[...] = jnp.where(same & (t >= u), cosine, 0.0)
        turned_ref[...] = jnp.where(same & (t <= u), cosine, 0.0)

    q = relu(mixed_ref[:, :PAIR])
    k = relu(mixed_ref[:, PAIR : 2 * PAIR])
    v = mixed_ref[:, 2 * PAIR :]
    gn = gn_ref[...]
    shape = (rows, PAIR)
    lo = low_lanes(shape)
    lane = lax.broadcasted_iota(jnp.int32, shape, 1)
    zero = jnp.zeros_like(q)
    e = dot((gn.astype(F32) * att_ref[...].astype(F32)).astype(BF), head_ones())
    v_one = jnp.concatenate([v, jnp.where(lane < 2, 1.0, 0.0).astype(BF)], axis=1)
    step = min(256, rows)
    gq_of, gk_of, gv_of = [], [], []
    for head in range(2):
        own = lo if head == 0 else ~lo
        k_own = jnp.where(own, k, zero)
        e_own = e if head == 0 else pltpu.roll(e, HD, 1)
        e_high = e_own.astype(BF)
        e_low = (e_own - e_high.astype(F32)).astype(BF)
        tail = jnp.where(lane == 0, -e_high, jnp.where(lane == 1, -e_low, zero))
        g_tail = jnp.concatenate([jnp.where(own, gn, zero), tail], axis=1)
        gq, gk, gv = [], [], []
        for at in range(0, rows, step):
            end = at + step
            gs = (dot_t(g_tail[at:end], v_one[:end]) * mask_ref[at:end, :end]).astype(BF)
            gq.append(dot(gs, k[:end]))
            turned = turned_ref[at:end, at:]
            w_t = (dot_t(k_own[at:end], q[at:]) * turned).astype(BF)
            gv.append(dot(w_t, gn[at:]))
            gs_t = (dot_t(v_one[at:end], g_tail[at:]) * turned).astype(BF)
            gk.append(dot(gs_t, q[at:]))
        gq_of.append(jnp.concatenate(gq, axis=0))
        gk_of.append(jnp.concatenate(gk, axis=0))
        gv_of.append(jnp.concatenate(gv, axis=0))

    c, s, c_sum, s_sum = unpacked(received(near_ref[0, 0], far_ref[0, 0], flag_ref, b))
    both = dot_t(gn, jnp.concatenate([c, s], axis=0).astype(BF))
    gq = jnp.where(lo, gq_of[0], gq_of[1])
    gq += col_ref[:, 0:1] * (both[:, :PAIR] - e * c_sum) + col_ref[:, 1:2] * (both[:, PAIR:] - e * s_sum)
    out_ref[:, :PAIR] = jnp.where(q > 0, gq, 0.0).astype(BF)
    out_ref[:, PAIR : 2 * PAIR] = jnp.where(lo, gk_of[0], gk_of[1]).astype(BF)
    out_ref[:, 2 * PAIR :] = jnp.where(lo, gv_of[0], gv_of[1]).astype(BF)


def attend_back(mixed, gn, att, near, far, flags, col, row, rows):
    grid = pair_grid(mixed, rows)
    pairs = grid[1]
    half = pairs // 2
    state = (1, 1, STATE_ROWS, PAIR)
    return run(
        attend_back_kernel,
        grid,
        [
            (flags, None, pltpu.SMEM),
            (col, (rows, col.shape[1]), lambda b, p: (b, 0)),
            (row, (row.shape[0], rows), lambda b, p: (0, b)),
            (mixed, (rows, QKV), lambda b, p: (b, p)),
            (gn, (rows, PAIR), lambda b, p: (b, p)),
            (att, (rows, PAIR), lambda b, p: (b, p)),
            (near, state, lambda b, p: (b, lax.rem(p + half, pairs), 0, 0)),
            (far, state, lambda b, p: (b, p, 0, 0)),
        ],
        [(mixed.shape, BF, (rows, QKV), lambda b, p: (b, p))],
        scratch=[pltpu.VMEM((rows, rows), F32), pltpu.VMEM((rows, rows), F32)],
        name="attend_back",
    )[0]


def regroup_pairs(tiles):
    lo = low_lanes(tiles[0].shape)
    first, second = [], []
    for a, b in zip(tiles[::2], tiles[1::2]):
        first.append(jnp.where(lo, a, pltpu.roll(b, HD, 1)))
        second.append(jnp.where(lo, pltpu.roll(a, HD, 1), b))
    return first, second


def project_sums_kernel(
    seq, flag_ref, col_ref, near_ref, far_ref, gm_hbm, mixed_hbm, g_hbm, normed_hbm, att_hbm,
    gm_out_hbm, sum_own_hbm, sum_other_hbm,
    gm_v, mixed_v, g_v, normed_v, att_v, low_v, sum_v,
    gm_sem, mixed_sem, in_sem, sum_sem, out_sem,
):
    tokens, width = g_v.shape
    half = gm_v.shape[2]
    pairs = half // QKV
    order = (1, 0)
    parts = [pl.ds(side * half, half) for side in range(2)]
    came = [None, None]
    for side in order:
        came[side] = [
            copy(gm_hbm.at[:, parts[side]], gm_v.at[side], gm_sem.at[side]),
            copy(mixed_hbm.at[:, parts[side]], mixed_v.at[side], mixed_sem.at[side]),
        ]
        if side == order[0]:
            normed_in = copy(normed_hbm, normed_v, in_sem.at[0])
            g_in = copy(g_hbm, g_v, in_sem.at[1])
            att_in = copy(att_hbm, att_v, in_sem.at[2])
    out = []
    for side, hbm in ((1, sum_other_hbm), (0, sum_own_hbm)):
        for made in came[side]:
            made.wait()
        for b in range(tokens // seq):
            at = slice(b * seq, (b + 1) * seq)
            for j in range(pairs):
                p = side * pairs + j
                k_at = slice(j * QKV + PAIR, j * QKV + 2 * PAIR)
                v_at = slice(j * QKV + 2 * PAIR, (j + 1) * QKV)
                st = received(near_ref[b, (p + pairs) % (2 * pairs)], far_ref[b, p], flag_ref, b)
                c, s, c_sum, s_sum = unpacked(st)
                both = jnp.concatenate([c, s], axis=0).astype(BF)
                k, v = relu(mixed_v[side, at, k_at]), mixed_v[side, at, v_at]
                memcos, memsin = col_ref[at, 2:3], col_ref[at, 3:4]
                toward = dot_t(v, both)
                gk = gm_v[side, at, k_at].astype(F32)
                gk += memcos * (toward[:, :PAIR] + c_sum) + memsin * (toward[:, PAIR:] + s_sum)
                gm_v[side, at, k_at] = jnp.where(k > 0, gk, 0.0).astype(BF)
                kf = k.astype(F32)
                features = jnp.concatenate([kf * memcos, kf * memsin], axis=1).astype(BF)
                gm_v[side, at, v_at] = (gm_v[side, at, v_at].astype(F32) + dot(features, both)).astype(BF)
        out.append(copy(gm_v.at[side], gm_out_hbm.at[:, parts[side]], out_sem.at[side]))
        if side == order[0]:
            for made in (normed_in, g_in, att_in):
                made.wait()
            low_v[...] = g_v[...].astype(BF)
        qkv = t_dot(normed_v[...], gm_v[side])
        o = t_dot(low_v[...], att_v[:, side * width // 2 : (side + 1) * width // 2])
        tiles = [
            qkv[:, (j * 3 + part) * PAIR : (j * 3 + part + 1) * PAIR] for part in range(3) for j in range(pairs)
        ] + [o[:, j * PAIR : (j + 1) * PAIR] for j in range(pairs)]
        for i, columns in enumerate(regroup_pairs(tiles)):
            for j, column in enumerate(columns):
                sum_v[side, i, :, j * PAIR : (j + 1) * PAIR] = column.astype(BF)
        out.append(copy(sum_v.at[side], hbm, sum_sem.at[side]))
    for made in out:
        made.wait()


def project_sums(gmixed, mixed, states, flags, col, grad, normed, att, seq):
    tokens, width = grad.shape
    half = gmixed.shape[1] // 2
    dma = pltpu.SemaphoreType.DMA
    whole = lambda i: (0, 0)
    sums = ((2, width, width), BF, None, pl.ANY)
    return run(
        partial(project_sums_kernel, seq),
        (1,),
        [(flags, None, pltpu.SMEM), (col, col.shape, whole)]
        + [(s, s.shape, lambda i: (0, 0, 0, 0)) for s in states]
        + [(a, None, pl.ANY) for a in (gmixed, mixed, grad, normed, att)],
        [(gmixed.shape, BF, None, pl.ANY), sums, sums],
        scratch=[
            pltpu.VMEM((2, tokens, half), BF),
            pltpu.VMEM((2, tokens, half), BF),
            pltpu.VMEM((tokens, width), F32),
            pltpu.VMEM((tokens, width), BF),
            pltpu.VMEM((tokens, width), BF),
            pltpu.VMEM((tokens, width), BF),
            pltpu.VMEM((2, 2, width, width), BF),
            dma((2,)), dma((2,)), dma((3,)), dma((2,)), dma((2,)),
        ],
        name="project_sums",
    )


def project_back_kernel(row, gm_ref, own_ref, other_ref, x_ref, par_ref, g_ref, out_ref, norm_ref):
    @pl.when(pl.program_id(0) == 0)
    def _():
        norm_ref[...] = jnp.zeros_like(norm_ref)

    half = own_ref.shape[1]
    grad = dot_t(gm_ref[:, :half], own_ref[...]) + dot_t(gm_ref[:, half:], other_ref[...])
    out_ref[...] = g_ref[...] + norm_gradient(grad, x_ref[...], par_ref[row : row + 1, :], norm_ref)


def project_back(gmixed, own, other, x, params, row, grad):
    tokens, width = x.shape
    half = gmixed.shape[1] // 2
    rows = min(256, tokens)
    whole = lambda i: (0, 0)
    by_row = lambda i: (i, 0)
    return run(
        partial(project_back_kernel, row),
        (tokens // rows,),
        [
            (gmixed, (rows, 2 * half), by_row),
            (own, (width, half), whole),
            (other, (width, half), whole),
            (x, (rows, width), by_row),
            (params, params.shape, whole),
            (grad, (rows, width), by_row),
        ],
        [
            ((tokens, width), F32, (rows, width), by_row),
            ((8, width), F32, (8, width), whole),
        ],
        name="project_back",
    )


def shards(
    layer_input,
    doc_lengths,
    ln1_gain,
    ln1_bias,
    qkv_weight,
    out_weight,
    ln2_gain,
    ln2_bias,
    in_weight,
    down_weight,
    cotangent,
):
    batches, rows, width = layer_input.shape
    layers = qkv_weight.shape[0]
    n_dp = lax.axis_size("dp")
    d, h = lax.axis_index("dp"), lax.axis_index("head")
    block = width // n_dp
    groups = xor_groups(n_dp)
    order = block_order(groups)
    tokens = batches * rows

    first_row = h * rows
    col, row, flags, back_flags = [], [], [], []
    for b in range(batches):
        lengths = doc_lengths[b]
        position = first_row + jnp.arange(rows, dtype=jnp.int32)
        doc, begin, size = places(lengths, position)
        angle = math.pi / 2 * (position - begin).astype(F32) / size.astype(F32)
        cos, sin = jnp.cos(angle), jnp.sin(angle)
        edges = first_row + jnp.array([-rows - 1, -1, 0, rows - 1, rows, 2 * rows], jnp.int32)
        at, _, _ = places(lengths, edges)
        first = (doc == at[2]).astype(F32)
        final = (doc == at[3]).astype(F32)
        place = doc.astype(F32)
        zero = jnp.zeros_like(cos)
        col.append(jnp.stack([first * cos, first * sin, final * cos, final * sin, cos, sin, place, zero], axis=1))
        row.append(jnp.stack([cos, sin, place, zero, zero, zero, zero, zero]))
        last = lax.axis_size("head") - 1
        near = (h >= 1) & (at[1] == at[2])
        far = (h >= 2) & (at[0] == at[2])
        flags.append(jnp.stack([near & (h != 2), near & (h == 2), far]))
        near = (h <= last - 1) & (at[3] == at[4])
        far = (h <= last - 2) & (at[3] == at[5])
        back_flags.append(jnp.stack([near & (h != 1), near & (h == 1), far]))
    col, row = jnp.concatenate(col), jnp.concatenate(row, axis=1)
    flags, back_flags = jnp.stack(flags).astype(F32), jnp.stack(back_flags).astype(F32)

    target = jnp.arange(width)
    source = (jnp.array(order)[target // block] ^ d) * block + target % block
    permutation = (jnp.arange(width)[:, None] == source[None, :]).astype(BF)
    x = dot(layer_input.reshape(tokens, width), permutation)
    cot = dot(cotangent.reshape(tokens, width), permutation)

    weights = []
    for l in range(layers):
        qkvo = jnp.concatenate([qkv_weight[l], out_weight[l].T], axis=1)
        updown = jnp.concatenate([in_weight[l], down_weight[l].T], axis=1)
        weights.append((Transfers(heads_steps(qkvo, groups)), Transfers(hidden_steps(updown, groups))))
    heads0, hidden0 = weights[0]
    start(heads0)

    params = jnp.concatenate([ln1_gain, ln1_bias, ln2_gain, ln2_bias], axis=0)[None]
    for masks in groups:
        params = spread(params, "dp", masks, 0)
    params = params.transpose(1, 0, 2).reshape(4 * layers, width).astype(F32)

    outer = len(groups) - 1
    stream = x
    for _ in range(outer):
        stream = advance(stream, heads0)
    start(hidden0)
    stream = advance(stream, heads0)
    stream = advance(stream, heads0)
    for _ in range(outer - 1):
        stream = advance(stream, hidden0)
    stream = advance(stream, heads0, hidden0)

    saved = []
    for l in range(layers):
        heads, units = weights[l]
        w_att = heads.result
        normed1, mixed, state = project(stream, params, l, *w_att, col, rows)
        states = Transfers(shift_steps(state, forward_shift))
        if l == 0:
            mixed = advance(mixed, units)
        start(states)
        if l + 1 < layers:
            nheads, nunits = weights[l + 1]
            start(nheads)
        intra = attend(mixed, col, row, rows)
        intra = advance(intra, states)
        if l + 1 < layers:
            for _ in range(outer):
                intra = advance(intra, nheads)
            start(nunits)
        intra = advance(intra, units)
        if l + 1 < layers:
            intra = advance(intra, nheads)
            for _ in range(outer):
                intra = advance(intra, nunits)
        intra = advance(intra, units)
        w_hid = units.result
        mid, normed2, act, slope, out, att, inv = hidden(
            stream, params, 2 * layers + l, intra, mixed, states.result, flags, col, w_att, w_hid, rows
        )
        saved.append((stream, normed1, states.result, (mid, normed2, act, slope, mixed, att, inv), w_att, w_hid))
        stream = out
        if l + 1 < layers:
            stream = advance(stream, nheads, nunits)
            stream = advance(stream, nheads)

    layer_output = dot_t(stream.astype(BF), permutation).astype(BF).reshape(layer_input.shape)

    def moving(chains):
        return [chain for chain in chains if chain.result is None]

    grad = cot
    sums = []
    norm_grads = [None] * layers
    for l in reversed(range(layers)):
        stream, normed1, states, kept, w_att, w_hid = saved[l]
        mixed, att = kept[4], kept[5]
        previous = sums[-1] if sums else ()
        acc, other = hidden_back_other(grad, kept, w_hid[1])
        acc = advance(acc, *moving(previous))
        mine = []
        hid_g = Transfers(
            sum_steps(other, lambda came, mine=mine: add(mine[0], came), lambda total: (total[1], total[0]), groups)
        )
        start(hid_g)
        grad, gn, norm2_g, gstate, own = hidden_back(
            grad, acc, params, 2 * layers + l, kept, w_att, w_hid[0], col, rows
        )
        mine.append(own)
        gstates = Transfers(shift_steps(gstate, backward_shift))
        start(gstates)
        gn = advance(gn, hid_g, *moving(previous))
        gmixed = attend_back(mixed, gn, att, *states, flags, col, row, rows)
        gmixed = advance(gmixed, gstates, hid_g, *moving(previous))
        gmixed, own, other = project_sums(
            gmixed, mixed, gstates.result, back_flags, col, grad, normed1, att, rows
        )
        att_g = Transfers(sum_steps(other, partial(add, own), lambda total: jnp.split(total, 2, axis=2), groups))
        start(att_g)
        grad, norm1_g = project_back(gmixed, *w_att, stream, params, l, grad)
        grad = advance(grad, att_g, hid_g)
        sums.append((hid_g, att_g))
        norm_grads[l] = (norm1_g[0], norm1_g[1], norm2_g[0], norm2_g[1])

    high = lax.reduce_precision(grad, 8, 7)
    input_grad = dot_t(high.astype(BF), permutation) + dot_t((grad - high).astype(BF), permutation)
    input_grad = input_grad.reshape(layer_input.shape)

    small = jnp.stack([norm_grads[l][i] for i in range(4) for l in range(layers)])
    small = small + swap(small, "head", 1)
    small = small + swap(small, "head", 2)
    small = small.reshape(4 * layers, n_dp, block).transpose(1, 0, 2)
    for masks in groups[::-1]:
        count = small.shape[0] // (len(masks) + 1)
        total = small[:count]
        for j, m in enumerate(masks):
            total = total + swap(small[(j + 1) * count : (j + 2) * count], "dp", m)
        small = total
    part = block // lax.axis_size("head")
    small = lax.dynamic_slice_in_dim(small.reshape(4, layers, block), h * part, part, 2)

    input_grad = finish(input_grad, [chain for layer in sums for chain in layer])
    sums = sums[::-1]
    third = sums[0][1].result.shape[1] * 3 // 4
    qkv_grad = jnp.stack([s[1].result[:, :third] for s in sums])
    out_grad = jnp.stack([s[1].result[:, third:].T for s in sums])
    units = sums[0][0].result.shape[1] // 2
    down_grad = jnp.stack([s[0].result[:, :units].T for s in sums])
    in_grad = jnp.stack([s[0].result[:, units:] for s in sums])
    return (
        layer_output,
        input_grad,
        small[0],
        small[1],
        qkv_grad,
        out_grad,
        small[2],
        small[3],
        in_grad,
        down_grad,
    )


def solution(mesh):
    in_specs = (
        P("dp", "head", None),
        P("dp", None),
        P(None, "dp"),
        P(None, "dp"),
        P(None, "dp", "head"),
        P(None, "head", "dp"),
        P(None, "dp"),
        P(None, "dp"),
        P(None, "dp", "head"),
        P(None, "head", "dp"),
        P("dp", "head", None),
    )
    out_specs = (
        P("dp", "head", None),
        P("dp", "head", None),
        P(None, ("dp", "head")),
        P(None, ("dp", "head")),
        P(None, "dp", "head"),
        P(None, "head", "dp"),
        P(None, ("dp", "head")),
        P(None, ("dp", "head")),
        P(None, "dp", "head"),
        P(None, "head", "dp"),
    )
    return jax.shard_map(shards, mesh=mesh, in_specs=in_specs, out_specs=out_specs, check_vma=False)
```

time: 808 us -> 725 us (0.90)
  matrix products: 80.9 us -> 15.7 us
  local copies, waits for them, and re-layouts: 72 us -> 49.3 us
  Pallas kernels: 295 us -> 306 us
  other arithmetic: 72.8 us -> 63.9 us
    dot_general x16 -> x0, matrix products: 67.7 us -> none  [t_dot(): lax.dot_general(a, b, (((0,), (0,)), ((), ())), preferred_element_type=F32)]
    ppermute x92 -> x74, waiting for transfers between devices: 88.6 us -> 136 us  [swap(): return lax.ppermute(x, axis, [(i, i ^ mask) for i in range(n)])]
    ppermute x4, waiting for transfers between devices: 30.4 us -> 2.78 us  [forward_shift(): return lax.ppermute(x, 'head', [(i, i + by) for i in range(n - by)])]
    convert_element_type x0 -> x20, other arithmetic: none -> 26.8 us  [add(): (kept.astype(F32) + sum((piece.astype(F32) for piece in pieces))).astype(BF)]
    add x12 -> x4, other arithmetic: 20.7 us -> 2.45 us  [last_rows(): pieces[0].astype(F32) + sum((a.astype(F32) for a in arrived))]
    ppermute x4, waiting for transfers between devices: 14.5 us -> 0.01 us  [backward_shift(): return lax.ppermute(x, 'head', [(i + by, i) for i in range(n - by)])]
    another operation x22 -> x12, other arithmetic: 25.2 us -> 13.4 us  [the longest x6 6.39 us: hidden_steps(): jnp.stack([jnp.stack([up, arrived[0]]), jnp.stack([down[:, :c], down[:, c...]
    pallas_call x16, Pallas kernels: 295 us -> 306 us  [run(): pl.pallas_call(kernel, grid=grid, in_specs=in_specs, out_specs=[pl.BlockS...]
  transfers between devices with their start and end apart: 100 -> 82, of which waited for: 26 -> 29; matrix products, arithmetic and copies ran while one was open for 18% -> 10% of each run, Pallas kernels for 32% -> 28%
where the time goes in v3:
time: 725 us; the launch traced here: 714 us
  Pallas kernels  306 us (42%)
  waiting for transfers between devices  139 us (19%)
  starting transfers between devices  129 us (18%)
  other arithmetic  63.9 us (9%)
  local copies, waits for them, and re-layouts  49.3 us (7%)
  matrix products  15.7 us (2%)
  between operations  12.2 us (2%)
    pallas_call x16, Pallas kernels, run(): pl.pallas_call(kernel, grid=grid, in_specs=in_specs, out_specs=[pl.BlockS...  306 us
    ppermute x74, waiting for transfers between devices, swap(): return lax.ppermute(x, axis, [(i, i ^ mask) for i in range(n)])  136 us
    ppermute x74, starting transfers between devices, swap(): return lax.ppermute(x, axis, [(i, i ^ mask) for i in range(n)])  112 us
    convert_element_type x20, other arithmetic, add(): (kept.astype(F32) + sum((piece.astype(F32) for piece in pieces))).astype(BF)  26.8 us
  transfers between devices with their start and end apart: 82, of which 29 were waited for; matrix products, arithmetic and copies ran while one was open for 10% of the time, Pallas kernels for 28%

profile of v3, /device:TPU:0, one launch (start us, length us, event | category | flops | bytes accessed | tf_op | source)
XLA Modules:
  0.0 714.4 jit_solution(16075621421015442426)
XLA Ops:
  9.7 3.9 collective-permute-start.6
  18.3 4.9 collective-permute-done.5
  26.5 3.7 collective-permute-done.7
  30.2 3.8 collective-permute-done.8
  37.8 6.5 collective-permute-done.9
  50.7 6.5 concatenate.104.own_ref.ao_hbm
  69.8 15.6 %collective-permute-done.13 = bf16[96,1536]{1,0:T(8,128)(2,1)S(1)} collective-permute-done((bf16[96,1536]{1,0:T(8,128)(2,1)}, bf16[96,1536]{1,0:T(8,128)(2,1)S(1)}, u32[]{:S(2)}, u32[]{:S(2)}) %collective-permute-start.13) | collective-permute-done | bytes 294944 | tf_op jit(solution)/shard_map/ppermute | solution.py:29
  87.9 10.1 %project.2 = (bf16[1024,768]{1,0:T(8,128)(2,1)}, bf16[1024,2304]{1,0:T(8,128)(2,1)}, bf16[2,6,144,128]{3,2,1,0:T(8,128)(2,1)}) custom-call(f32[1024,768]{1,0:T(8,128)} %fusion.8.x_ref.x_hbm, f32[8,768]{1,0:T(8,128)} %reshape.490.par_ref, f32[1024,8]{1,0:T(8,128)} %copy.77.col_ref, bf16[768,1536]{1,0:T(8,128)(2,1)} %concatenate.104.own_ref.ao_hbm, ...), custom_call_target="tpu_custom_call" | custom-call | flops 10000000000 | bytes 1000 | tf_op jit(solution)/shard_map/project/pallas_call | solution.py:229
  100.2 3.9 collective-permute-start.18
  104.7 5.9 collective-permute-start.20
  118.4 14.2 %attend.2 = (f32[1024,768]{1,0:T(8,128)}, f32[1024,768]{1,0:T(8,128)}) custom-call(f32[1024,8]{1,0:T(8,128)} %copy.77.col_ref, f32[8,1024]{1,0:T(8,128)} %pad_maximum_fusion.31.row_ref, bf16[1024,2304]{1,0:T(8,128)(2,1)} %get-tuple-element.276.mixed_ref.mixed_hbm), custom_call_target="tpu_custom_call" | custom-call | flops 15000000512 | bytes 1000 | tf_op jit(solution)/shard_map/attend/pallas_call | solution.py:229
  132.8 11.2 %collective-permute-done.22 = bf16[768,768]{1,0:T(8,128)(2,1)} collective-permute-done((bf16[768,768]{1,0:T(8,128)(2,1)}, bf16[768,768]{1,0:T(8,128)(2,1)}, u32[]{:S(2)}, u32[]{:S(2)}) %collective-permute-start.22) | collective-permute-done | bytes 1179680 | tf_op jit(solution)/shard_map/ppermute | solution.py:29
  151.8 5.1 collective-permute-start.26
  167.5 3.4 collective-permute-done.25
  172.6 7.7 %collective-permute-done.27 = bf16[96,1536]{1,0:T(8,128)(2,1)S(1)} collective-permute-done((bf16[96,1536]{1,0:T(8,128)(2,1)S(1)}, bf16[96,1536]{1,0:T(8,128)(2,1)S(1)}, u32[]{:S(2)}, u32[]{:S(2)}) %collective-permute-start.27) | collective-permute-done | bytes 294944 | tf_op jit(solution)/shard_map/ppermute | solution.py:29
  186.4 30.5 %hidden.2 = (f32[1024,768]{1,0:T(8,128)}, bf16[1024,768]{1,0:T(8,128)(2,1)}, bf16[4,1024,768]{2,1,0:T(8,128)(2,1)}, bf16[4,1024,768]{2,1,0:T(8,128)(2,1)}, f32[1...) custom-call(f32[2,3]{1,0:T(2,128)} %add_convert_fusion.12.flag_ref, ...), custom_call_target="tpu_custom_call" | custom-call | flops 28000000000 | bytes 1000 | tf_op jit(solution)/shard_map/hidden/pallas_call | solution.py:229
  224.7 6.0 concatenate.117.own_ref.ao_hbm
  235.7 10.1 %project.3 = (bf16[1024,768]{1,0:T(8,128)(2,1)}, bf16[1024,2304]{1,0:T(8,128)(2,1)}, bf16[2,6,144,128]{3,2,1,0:T(8,128)(2,1)}) custom-call(f32[1024,768]{1,0:T(8,128)} %get-tuple-element.334.x_ref.x_hbm, f32[8,768]{1,0:T(8,128)} %reshape.490.par_ref, f32[1024,8]{1,0:T(8,128)} %copy.77.col_ref, bf16[768,1536]{1,0:T(8,128)(2,1)} %concatenate.117.own_ref.ao_hbm, ...), custom_call_target="tpu_custom_call" | custom-call | flops 10000000000 | bytes 1000 | tf_op jit(solution)/shard_map/project/pallas_call | solution.py:229
  247.8 3.8 collective-permute-start.36
  251.7 14.4 %attend.3 = (f32[1024,768]{1,0:T(8,128)}, f32[1024,768]{1,0:T(8,128)}) custom-call(f32[1024,8]{1,0:T(8,128)} %copy.77.col_ref, f32[8,1024]{1,0:T(8,128)} %pad_maximum_fusion.31.row_ref, bf16[1024,2304]{1,0:T(8,128)(2,1)} %get-tuple-element.336.mixed_ref.mixed_hbm), custom_call_target="tpu_custom_call" | custom-call | flops 15000000512 | bytes 1000 | tf_op jit(solution)/shard_map/attend/pallas_call | solution.py:229
  273.4 4.5 collective-permute-start.39
  281.2 4.2 collective-permute-done.39.wx_hbm.w_hbm
  287.6 30.3 %hidden.3 = (f32[1024,768]{1,0:T(8,128)}, bf16[1024,768]{1,0:T(8,128)(2,1)}, bf16[4,1024,768]{2,1,0:T(8,128)(2,1)}, bf16[4,1024,768]{2,1,0:T(8,128)(2,1)}, f32[1...) custom-call(f32[2,3]{1,0:T(2,128)} %add_convert_fusion.12.flag_ref, ...), custom_call_target="tpu_custom_call" | custom-call | flops 28000000000 | bytes 1000 | tf_op jit(solution)/shard_map/hidden/pallas_call | solution.py:229
  317.9 16.7 %hidden_back_other.2 = (f32[1024,768]{1,0:T(8,128)}, bf16[2,2,768,768]{3,2,1,0:T(8,128)(2,1)}) custom-call(f32[1024,768]{1,0:T(8,128)} %fusion.9.g_hbm, bf16[1024,768]{1,0:T(8,128)(2,1)} %get-tuple-element.361.normed_hbm, bf16[4,1024,768]{2,1,0:T(8,128)(2,1)} %get-tuple-element.362.act_hbm, bf16[4,1024,768]{2,1,0:T(8,128)(2,1)} %get-tuple-element.363.slope_hbm, ...), custom_call_target="tpu_custom_call" | custom-call | flops 16000000000 | bytes 1000 | tf_op jit(solution)/shard_map/hidden_back_other/pallas_call | solution.py:229
  340.8 26.9 %hidden_back.2 = (f32[1024,768]{1,0:T(8,128)}, bf16[1024,768]{1,0:T(8,128)(2,1)}, f32[8,768]{1,0:T(8,128)}, bf16[2,6,144,128]{3,2,1,0:T(8,128)(2,1)}, bf16[2,2,768,768]{3,2,1,0:T(8,128)(2,1)}) custom-call(f32[8,768]{1,0:T(8,128)} %reshape.490.par_ref, f32[1024,8]{1,0:T(8,128)} %copy.77.col_ref, f32[1024,768]{1,0:T(8,128)} %fusion.9.g_hbm, ...), custom_call_target="tpu_custom_call" | custom-call | flops 25999998976 | bytes 1000 | tf_op jit(solution)/shard_map/hidden_back/pallas_call | solution.py:229
  370.3 4.9 add_convert_fusion.1
  379.4 3.5 collective-permute-start.44
  382.9 28.3 %attend_back.2.gm_hbm = bf16[1024,2304]{1,0:T(8,128)(2,1)} custom-call(f32[2,3]{1,0:T(2,128)} %add_convert_fusion.12.flag_ref, f32[1024,8]{1,0:T(8,128)} %copy.77.col_ref, f32[8,1024]{1,0:T(8,128)} %pad_maximum_fusion.31.row_ref, bf16[1024,2304]{1,0:T(8,128)(2,1)} %get-tuple-element.336.mixed_ref.mixed_hbm, bf16[1024,768]{1,0:T(8,128)(2,1)} %get-tuple-element.373.gn_ref, ...), custom_call_target="tpu_custom_call" | custom-call | flops 28000000000 | bytes 1000 | tf_op jit(solution)/shard_map/attend_back/pallas_call | solution.py:229
  417.8 15.5 %project_sums.2 = (bf16[1024,2304]{1,0:T(8,128)(2,1)}, bf16[2,768,768]{2,1,0:T(8,128)(2,1)}, bf16[2,768,768]{2,1,0:T(8,128)(2,1)}) custom-call(f32[2,3]{1,0:T(2,128)} %add_convert_fusion.13.flag_ref, f32[1024,8]{1,0:T(8,128)} %copy.77.col_ref, bf16[2,6,144,128]{3,2,1,0:T(8,128)(2,1)} %collective-permute-done.41.near_ref, ...), custom_call_target="tpu_custom_call" | custom-call | flops 15000000512 | bytes 1000 | tf_op jit(solution)/shard_map/project_sums/pallas_call | solution.py:229
  435.1 10.6 %project_back.2 = (f32[1024,768]{1,0:T(8,128)}, f32[8,768]{1,0:T(8,128)}) custom-call(bf16[1024,2304]{1,0:T(8,128)(2,1)} %get-tuple-element.385.gm_ref, bf16[768,1536]{1,0:T(8,128)(2,1)} %concatenate.117.own_ref.ao_hbm, bf16[768,1536]{1,0:T(8,128)(2,1)} %collective-permute-done.34.other_ref.ax_hbm, f32[1024,768]{1,0:T(8,128)} %get-tuple-element.334.x_ref.x_hbm, ...), custom_call_target="tpu_custom_call" | custom-call | flops 10000000000 | bytes 1000 | tf_op jit(solution)/shard_map/project_back/pallas_call | solution.py:229
  445.7 3.5 collective-permute-done.46
  455.5 16.7 %hidden_back_other.3 = (f32[1024,768]{1,0:T(8,128)}, bf16[2,2,768,768]{3,2,1,0:T(8,128)(2,1)}) custom-call(f32[1024,768]{1,0:T(8,128)} %get-tuple-element.395.g_hbm, bf16[1024,768]{1,0:T(8,128)(2,1)} %get-tuple-element.396.normed_hbm, bf16[4,1024,768]{2,1,0:T(8,128)(2,1)} %get-tuple-element.397.act_hbm, bf16[4,1024,768]{2,1,0:T(8,128)(2,1)} %get-tuple-element.398.slope_hbm, ...), custom_call_target="tpu_custom_call" | custom-call | flops 16000000000 | bytes 1000 | tf_op jit(solution)/shard_map/hidden_back_other/pallas_call | solution.py:229
  472.3 5.4 collective-permute-start.48
  480.3 4.6 fusion.11
  489.1 17.9 %collective-permute-done.49 = bf16[96,1536]{1,0:T(8,128)(2,1)S(1)} collective-permute-done((bf16[96,1536]{1,0:T(8,128)(2,1)}, bf16[96,1536]{1,0:T(8,128)(2,1)S(1)}, u32[]{:S(2)}, u32[]{:S(2)}) %collective-permute-start.49) | collective-permute-done | bytes 294944 | tf_op jit(solution)/shard_map/ppermute | solution.py:29
  510.3 26.9 %hidden_back.3 = (f32[1024,768]{1,0:T(8,128)}, bf16[1024,768]{1,0:T(8,128)(2,1)}, f32[8,768]{1,0:T(8,128)}, bf16[2,6,144,128]{3,2,1,0:T(8,128)(2,1)}, bf16[2,2,768,768]{3,2,1,0:T(8,128)(2,1)}) custom-call(f32[8,768]{1,0:T(8,128)} %reshape.490.par_ref, f32[1024,8]{1,0:T(8,128)} %copy.77.col_ref, f32[1024,768]{1,0:T(8,128)} %get-tuple-element.395.g_hbm, ...), custom_call_target="tpu_custom_call" | custom-call | flops 25999998976 | bytes 1000 | tf_op jit(solution)/shard_map/hidden_back/pallas_call | solution.py:229
  541.4 4.9 add_convert_fusion
  553.2 3.4 collective-permute-start.59
  556.6 6.8 collective-permute-start.60
  565.8 28.3 %attend_back.3.gm_hbm = bf16[1024,2304]{1,0:T(8,128)(2,1)} custom-call(f32[2,3]{1,0:T(2,128)} %add_convert_fusion.12.flag_ref, f32[1024,8]{1,0:T(8,128)} %copy.77.col_ref, f32[8,1024]{1,0:T(8,128)} %pad_maximum_fusion.31.row_ref, bf16[1024,2304]{1,0:T(8,128)(2,1)} %get-tuple-element.276.mixed_ref.mixed_hbm, bf16[1024,768]{1,0:T(8,128)(2,1)} %get-tuple-element.421.gn_ref, ...), custom_call_target="tpu_custom_call" | custom-call | flops 28000000000 | bytes 1000 | tf_op jit(solution)/shard_map/attend_back/pallas_call | solution.py:229
  599.4 15.5 %project_sums.3 = (bf16[1024,2304]{1,0:T(8,128)(2,1)}, bf16[2,768,768]{2,1,0:T(8,128)(2,1)}, bf16[2,768,768]{2,1,0:T(8,128)(2,1)}) custom-call(f32[2,3]{1,0:T(2,128)} %add_convert_fusion.13.flag_ref, f32[1024,8]{1,0:T(8,128)} %copy.77.col_ref, bf16[2,6,144,128]{3,2,1,0:T(8,128)(2,1)} %collective-permute-done.56.near_ref, ...), custom_call_target="tpu_custom_call" | custom-call | flops 15000000512 | bytes 1000 | tf_op jit(solution)/shard_map/project_sums/pallas_call | solution.py:229
  614.9 10.7 %project_back.3 = (f32[1024,768]{1,0:T(8,128)}, f32[8,768]{1,0:T(8,128)}) custom-call(bf16[1024,2304]{1,0:T(8,128)(2,1)} %get-tuple-element.436.gm_ref, bf16[768,1536]{1,0:T(8,128)(2,1)} %concatenate.104.own_ref.ao_hbm, bf16[768,1536]{1,0:T(8,128)(2,1)} %collective-permute-done.11.other_ref.ax_hbm, f32[1024,768]{1,0:T(8,128)} %fusion.8.x_ref.x_hbm, ...), custom_call_target="tpu_custom_call" | custom-call | flops 10000000000 | bytes 1000 | tf_op jit(solution)/shard_map/project_back/pallas_call | solution.py:229
  636.5 11.9 %collective-permute-done.78 = f32[4,8,96]{2,0,1:T(4,128)S(1)} collective-permute-done((f32[4,8,96]{2,0,1:T(4,128)S(1)}, f32[4,8,96]{2,0,1:T(4,128)S(1)}, u32[]{:S(2)}, u32[]{:S(2)}) %collective-permute-start.78) | collective-permute-done | bytes 12320 | tf_op jit(solution)/shard_map/ppermute | solution.py:29
  674.5 5.1 collective-permute-done.66
  679.6 8.9 %collective-permute-done.67 = bf16[96,1536]{1,0:T(8,128)(2,1)S(1)} collective-permute-done((bf16[96,1536]{1,0:T(8,128)(2,1)S(1)}, bf16[96,1536]{1,0:T(8,128)(2,1)S(1)}, u32[]{:S(2)}, u32[]{:S(2)}) %collective-permute-start.67) | collective-permute-done | bytes 294944 | tf_op jit(solution)/shard_map/ppermute | solution.py:29
  691.6 4.1 collective-permute-done.71
  697.4 4.4 collective-permute-start.73
  707.6 4.8 collective-permute-done.74
  (408 shorter events, 201.6 us)
Async XLA Ops:
  1.5 60.2 %collective-permute-start = (bf16[1,8,96]{2,1,0:T(8,128)(2,1)S(1)}, bf16[1,8,96]{2,1,0:T(8,128)(2,1)S(1)}, u32[]{:S(2)}, u32[]{:S(2)}) collective-permute-start(bf16[1,8,96]{2,1,0:T(8,128)(2,1)S(1)} %maximum_bitcast_fusion.4), channel_id=1, source_target_pairs={{0,8},{4,12},{8,0},{12,4},{16,24},{20,28},{24,16},{28,20},{1,9},{5... | collective-permute-start | bytes 4616 | tf_op jit(solution)/shard_map/ppermute | solution.py:29
  4.6 57.4 %collective-permute-start.1 = (bf16[1,8,96]{2,1,0:T(8,128)(2,1)S(1)}, bf16[1,8,96]{2,1,0:T(8,128)(2,1)S(1)}, u32[]{:S(2)}, u32[]{:S(2)}) collective-permute-start(bf16[1,8,96]{2,1,0:T(8,128)(2,1)S(1)} %maximum_bitcast_fusion.4), channel_id=1, source_target_pairs={{0,16},{4,20},{8,24},{12,28},{16,0},{20,4},{24,8},{28,12},{1,17},{... | collective-permute-start | bytes 4616 | tf_op jit(solution)/shard_map/ppermute | solution.py:29
  18.2 47.1 %collective-permute-start.2 = (bf16[1,8,96]{2,1,0:T(8,128)(2,1)S(1)}, bf16[1,8,96]{2,1,0:T(8,128)(2,1)S(1)}, u32[]{:S(2)}, u32[]{:S(2)}) collective-permute-start(bf16[1,8,96]{2,1,0:T(8,128)(2,1)S(1)} %maximum_bitcast_fusion.4), channel_id=1, source_target_pairs={{0,24},{4,28},{8,16},{12,20},{16,8},{20,12},{24,0},{28,4},{1,25},{... | collective-permute-start | bytes 4616 | tf_op jit(solution)/shard_map/ppermute | solution.py:29
  44.3 25.4 %collective-permute-start.12 = (bf16[96,1536]{1,0:T(8,128)(2,1)}, bf16[96,1536]{1,0:T(8,128)(2,1)}, u32[]{:S(2)}, u32[]{:S(2)}) collective-permute-start(bf16[96,1536]{1,0:T(8,128)(2,1)} %pad_maximum_fusion.23), channel_id=1, source_target_pairs={{0,8},{4,12},{8,0},{12,4},{16,24},{20,28},{24,16},{28,20},{1,9},{5... | collective-permute-start | bytes 884744 | tf_op jit(solution)/shard_map/ppermute | solution.py:29
  57.2 28.2 %collective-permute-start.11 = (bf16[768,1536]{1,0:T(8,128)(2,1)}, bf16[768,1536]{1,0:T(8,128)(2,1)}, u32[]{:S(2)}, u32[]{:S(2)}) collective-permute-start(bf16[768,1536]{1,0:T(8,128)(2,1)} %concatenate.104.own_ref.ao_hbm), channel_id=1, source_target_pairs={{0,1},{1,0},{2,3},{3,2},{4,5},{5,4},{6,7},{7,6},{8,9},{9,8},{10,11... | collective-permute-start | bytes 7077896 | tf_op jit(solution)/shard_map/ppermute | solution.py:29
  61.7 23.7 %collective-permute-start.13 = (bf16[96,1536]{1,0:T(8,128)(2,1)}, bf16[96,1536]{1,0:T(8,128)(2,1)S(1)}, u32[]{:S(2)}, u32[]{:S(2)}) collective-permute-start(bf16[96,1536]{1,0:T(8,128)(2,1)} %pad_maximum_fusion.23), channel_id=1, source_target_pairs={{0,16},{4,20},{8,24},{12,28},{16,0},{20,4},{24,8},{28,12},{1,17},{... | collective-permute-start | bytes 884744 | tf_op jit(solution)/shard_map/ppermute | solution.py:29
  62.0 23.3 %collective-permute-start.14 = (bf16[96,1536]{1,0:T(8,128)(2,1)}, bf16[96,1536]{1,0:T(8,128)(2,1)S(1)}, u32[]{:S(2)}, u32[]{:S(2)}) collective-permute-start(bf16[96,1536]{1,0:T(8,128)(2,1)} %pad_maximum_fusion.23), channel_id=1, source_target_pairs={{0,24},{4,28},{8,16},{12,20},{16,8},{20,12},{24,0},{28,4},{1,25},{... | collective-permute-start | bytes 884744 | tf_op jit(solution)/shard_map/ppermute | solution.py:29
  69.0 63.5 %collective-permute-start.19 = (bf16[96,768]{1,0:T(8,128)(2,1)S(1)}, bf16[96,768]{1,0:T(8,128)(2,1)S(1)}, u32[]{:S(2)}, u32[]{:S(2)}) collective-permute-start(bf16[96,768]{1,0:T(8,128)(2,1)S(1)} %pad_maximum_fusion.29), channel_id=1, source_target_pairs={{0,8},{4,12},{8,0},{12,4},{16,24},{20,28},{24,16},{28,20},{1,9},{5... | collective-permute-start | bytes 442376 | tf_op jit(solution)/shard_map/ppermute | solution.py:29
  87.1 23.5 %collective-permute-start.16 = (bf16[384,768]{1,0:T(8,128)(2,1)S(1)}, bf16[384,768]{1,0:T(8,128)(2,1)S(1)}, u32[]{:S(2)}, u32[]{:S(2)}) collective-permute-start(bf16[384,768]{1,0:T(8,128)(2,1)S(1)} %get-tuple-element.272), channel_id=1, source_target_pairs={{0,2},{1,3},{2,0},{3,1},{4,6},{5,7},{6,4},{7,5},{8,10},{9,11},{10,... | collective-permute-start | bytes 1769480 | tf_op jit(solution)/shard_map/ppermute | solution.py:29
  104.7 27.9 %collective-permute-start.20 = (bf16[96,768]{1,0:T(8,128)(2,1)S(1)}, bf16[96,768]{1,0:T(8,128)(2,1)S(1)}, u32[]{:S(2)}, u32[]{:S(2)}) collective-permute-start(bf16[96,768]{1,0:T(8,128)(2,1)S(1)} %pad_maximum_fusion.29), channel_id=1, source_target_pairs={{0,16},{4,20},{8,24},{12,28},{16,0},{20,4},{24,8},{28,12},{1,17},{... | collective-permute-start | bytes 442376 | tf_op jit(solution)/shard_map/ppermute | solution.py:29
  110.6 22.0 %collective-permute-start.21 = (bf16[96,768]{1,0:T(8,128)(2,1)S(1)}, bf16[96,768]{1,0:T(8,128)(2,1)S(1)}, u32[]{:S(2)}, u32[]{:S(2)}) collective-permute-start(bf16[96,768]{1,0:T(8,128)(2,1)S(1)} %pad_maximum_fusion.29), channel_id=1, source_target_pairs={{0,24},{4,28},{8,16},{12,20},{16,8},{20,12},{24,0},{28,4},{1,25},{... | collective-permute-start | bytes 442376 | tf_op jit(solution)/shard_map/ppermute | solution.py:29
  116.9 27.1 %collective-permute-start.22 = (bf16[768,768]{1,0:T(8,128)(2,1)}, bf16[768,768]{1,0:T(8,128)(2,1)}, u32[]{:S(2)}, u32[]{:S(2)}) collective-permute-start(bf16[768,768]{1,0:T(8,128)(2,1)} %get-tuple-element.293), channel_id=1, source_target_pairs={{0,2},{1,3},{2,0},{3,1},{4,6},{5,7},{6,4},{7,5},{8,10},{9,11},{10,... | collective-permute-start | bytes 3538952 | tf_op jit(solution)/shard_map/ppermute | solution.py:29
  116.9 27.6 %collective-permute-start.23 = (bf16[384,1536]{1,0:T(8,128)(2,1)}, bf16[384,1536]{1,0:T(8,128)(2,1)}, u32[]{:S(2)}, u32[]{:S(2)}) collective-permute-start(bf16[384,1536]{1,0:T(8,128)(2,1)} %pad_maximum_fusion.7), channel_id=1, source_target_pairs={{0,4},{4,0},{8,12},{12,8},{16,20},{20,16},{24,28},{28,24},{1,5},{5... | collective-permute-start | bytes 3538952 | tf_op jit(solution)/shard_map/ppermute | solution.py:29
  150.4 36.1 %collective-permute-start.29 = (bf16[2,2,768,768]{3,2,1,0:T(8,128)(2,1)}, bf16[2,2,768,768]{3,2,1,0:T(8,128)(2,1)}, u32[]{:S(2)}, u32[]{:S(2)}) collective-permute-start(bf16[2,2,768,768]{3,2,1,0:T(8,128)(2,1)} %pad_maximum_fusion.wo_hbm.w_hbm), channel_id=1, source_target_pairs={{0,1},{1,0},{2,3},{3,2},{4,5},{5,4},{6,7},{7,6},{8,9},{9,8},{10,11... | collective-permute-start | bytes 14155784 | tf_op jit(solution)/shard_map/ppermute | solution.py:29
  151.8 20.8 %collective-permute-start.26 = (bf16[96,1536]{1,0:T(8,128)(2,1)S(1)}, bf16[96,1536]{1,0:T(8,128)(2,1)S(1)}, u32[]{:S(2)}, u32[]{:S(2)}) collective-permute-start(bf16[96,1536]{1,0:T(8,128)(2,1)S(1)} %pad_maximum_fusion.24), channel_id=1, source_target_pairs={{0,8},{4,12},{8,0},{12,4},{16,24},{20,28},{24,16},{28,20},{1,9},{5... | collective-permute-start | bytes 884744 | tf_op jit(solution)/shard_map/ppermute | solution.py:29
  156.9 23.5 %collective-permute-start.27 = (bf16[96,1536]{1,0:T(8,128)(2,1)S(1)}, bf16[96,1536]{1,0:T(8,128)(2,1)S(1)}, u32[]{:S(2)}, u32[]{:S(2)}) collective-permute-start(bf16[96,1536]{1,0:T(8,128)(2,1)S(1)} %pad_maximum_fusion.24), channel_id=1, source_target_pairs={{0,16},{4,20},{8,24},{12,28},{16,0},{20,4},{24,8},{28,12},{1,17},{... | collective-permute-start | bytes 884744 | tf_op jit(solution)/shard_map/ppermute | solution.py:29
  180.6 36.4 %collective-permute-start.30 = (bf16[768,384]{1,0:T(8,128)(2,1)}, bf16[768,384]{1,0:T(8,128)(2,1)S(1)}, u32[]{:S(2)}, u32[]{:S(2)}) collective-permute-start(bf16[768,384]{1,0:T(8,128)(2,1)} %pad_maximum_fusion.13), channel_id=1, source_target_pairs={{0,2},{1,3},{2,0},{3,1},{4,6},{5,7},{6,4},{7,5},{8,10},{9,11},{10,... | collective-permute-start | bytes 1769480 | tf_op jit(solution)/shard_map/ppermute | solution.py:29
  183.1 33.9 %collective-permute-start.31 = (bf16[384,768]{1,0:T(8,128)(2,1)}, bf16[384,768]{1,0:T(8,128)(2,1)}, u32[]{:S(2)}, u32[]{:S(2)}) collective-permute-start(bf16[384,768]{1,0:T(8,128)(2,1)} %pad_maximum_fusion.17), channel_id=1, source_target_pairs={{0,4},{4,0},{8,12},{12,8},{16,20},{20,16},{24,28},{28,24},{1,5},{5... | collective-permute-start | bytes 1769480 | tf_op jit(solution)/shard_map/ppermute | solution.py:29
  183.7 33.3 %collective-permute-start.32 = (bf16[384,768]{1,0:T(8,128)(2,1)S(1)}, bf16[384,768]{1,0:T(8,128)(2,1)}, u32[]{:S(2)}, u32[]{:S(2)}) collective-permute-start(bf16[384,768]{1,0:T(8,128)(2,1)S(1)} %get-tuple-element.325), channel_id=1, source_target_pairs={{0,4},{4,0},{8,12},{12,8},{16,20},{20,16},{24,28},{28,24},{1,5},{5... | collective-permute-start | bytes 1769480 | tf_op jit(solution)/shard_map/ppermute | solution.py:29
  185.1 31.8 %collective-permute-start.33 = (bf16[384,768]{1,0:T(8,128)(2,1)S(1)}, bf16[384,768]{1,0:T(8,128)(2,1)S(1)}, u32[]{:S(2)}, u32[]{:S(2)}) collective-permute-start(bf16[384,768]{1,0:T(8,128)(2,1)S(1)} %get-tuple-element.326), channel_id=1, source_target_pairs={{0,2},{1,3},{2,0},{3,1},{4,6},{5,7},{6,4},{7,5},{8,10},{9,11},{10,... | collective-permute-start | bytes 1769480 | tf_op jit(solution)/shard_map/ppermute | solution.py:29
  230.8 38.1 %collective-permute-start.37 = (bf16[768,768]{1,0:T(8,128)(2,1)}, bf16[768,768]{1,0:T(8,128)(2,1)}, u32[]{:S(2)}, u32[]{:S(2)}) collective-permute-start(bf16[768,768]{1,0:T(8,128)(2,1)} %get-tuple-element.346), channel_id=1, source_target_pairs={{0,2},{1,3},{2,0},{3,1},{4,6},{5,7},{6,4},{7,5},{8,10},{9,11},{10,... | collective-permute-start | bytes 3538952 | tf_op jit(solution)/shard_map/ppermute | solution.py:29
  232.8 36.1 %collective-permute-start.38 = (bf16[384,1536]{1,0:T(8,128)(2,1)}, bf16[384,1536]{1,0:T(8,128)(2,1)}, u32[]{:S(2)}, u32[]{:S(2)}) collective-permute-start(bf16[384,1536]{1,0:T(8,128)(2,1)} %pad_maximum_fusion.11), channel_id=1, source_target_pairs={{0,4},{4,0},{8,12},{12,8},{16,20},{20,16},{24,28},{28,24},{1,5},{5... | collective-permute-start | bytes 3538952 | tf_op jit(solution)/shard_map/ppermute | solution.py:29
  247.8 21.0 %collective-permute-start.36 = (bf16[2,6,144,128]{3,2,1,0:T(8,128)(2,1)}, bf16[2,6,144,128]{3,2,1,0:T(8,128)(2,1)S(1)}, u32[]{:S(2)}, u32[]{:S(2)}) collective-permute-start(bf16[2,6,144,128]{3,2,1,0:T(8,128)(2,1)} %get-tuple-element.339), channel_id=1, source_target_pairs={{0,2},{1,3},{4,6},{5,7},{8,10},{9,11},{12,14},{13,15},{16,18},{17,... | collective-permute-start | bytes 1327112 | tf_op jit(solution)/shard_map/ppermute | solution.py:34
  334.6 35.7 %collective-permute-start.40 = (bf16[2,2,768,768]{3,2,1,0:T(8,128)(2,1)}, bf16[2,2,768,768]{3,2,1,0:T(8,128)(2,1)}, u32[]{:S(2)}, u32[]{:S(2)}) collective-permute-start(bf16[2,2,768,768]{3,2,1,0:T(8,128)(2,1)} %get-tuple-element.369), channel_id=1, source_target_pairs={{0,1},{1,0},{2,3},{3,2},{4,5},{5,4},{6,7},{7,6},{8,9},{9,8},{10,11... | collective-permute-start | bytes 14155784 | tf_op jit(solution)/shard_map/ppermute | solution.py:29
  367.7 43.4 %collective-permute-start.41 = (bf16[2,6,144,128]{3,2,1,0:T(8,128)(2,1)}, bf16[2,6,144,128]{3,2,1,0:T(8,128)(2,1)}, u32[]{:S(2)}, u32[]{:S(2)}) collective-permute-start(bf16[2,6,144,128]{3,2,1,0:T(8,128)(2,1)} %get-tuple-element.374), channel_id=1, source_target_pairs={{1,0},{2,1},{3,2},{5,4},{6,5},{7,6},{9,8},{10,9},{11,10},{13,12},{... | collective-permute-start | bytes 1327112 | tf_op jit(solution)/shard_map/ppermute | solution.py:39
  369.0 42.1 %collective-permute-start.42 = (bf16[2,6,144,128]{3,2,1,0:T(8,128)(2,1)}, bf16[2,6,144,128]{3,2,1,0:T(8,128)(2,1)}, u32[]{:S(2)}, u32[]{:S(2)}) collective-permute-start(bf16[2,6,144,128]{3,2,1,0:T(8,128)(2,1)} %get-tuple-element.374), channel_id=1, source_target_pairs={{2,0},{3,1},{6,4},{7,5},{10,8},{11,9},{14,12},{15,13},{18,16},{19,... | collective-permute-start | bytes 1327112 | tf_op jit(solution)/shard_map/ppermute | solution.py:39
  378.8 32.3 %collective-permute-start.43 = (bf16[2,384,768]{2,1,0:T(8,128)(2,1)}, bf16[2,384,768]{2,1,0:T(8,128)(2,1)S(1)}, u32[]{:S(2)}, u32[]{:S(2)}) collective-permute-start(bf16[2,384,768]{2,1,0:T(8,128)(2,1)} %slice.756), channel_id=1, source_target_pairs={{0,4},{4,0},{8,12},{12,8},{16,20},{20,16},{24,28},{28,24},{1,5},{5... | collective-permute-start | bytes 3538952 | tf_op jit(solution)/shard_map/ppermute | solution.py:29
  379.4 33.7 %collective-permute-start.44 = (bf16[768,768]{1,0:T(8,128)(2,1)}, bf16[768,768]{1,0:T(8,128)(2,1)}, u32[]{:S(2)}, u32[]{:S(2)}) collective-permute-start(bf16[768,768]{1,0:T(8,128)(2,1)} %slice_bitcast_fusion.5), channel_id=1, source_target_pairs={{0,2},{1,3},{2,0},{3,1},{4,6},{5,7},{6,4},{7,5},{8,10},{9,11},{10,... | collective-permute-start | bytes 3538952 | tf_op jit(solution)/shard_map/ppermute | solution.py:29
  472.2 68.5 %collective-permute-start.53 = (bf16[2,2,768,768]{3,2,1,0:T(8,128)(2,1)}, bf16[2,2,768,768]{3,2,1,0:T(8,128)(2,1)}, u32[]{:S(2)}, u32[]{:S(2)}) collective-permute-start(bf16[2,2,768,768]{3,2,1,0:T(8,128)(2,1)} %get-tuple-element.413), channel_id=1, source_target_pairs={{0,1},{1,0},{2,3},{3,2},{4,5},{5,4},{6,7},{7,6},{8,9},{9,8},{10,11... | collective-permute-start | bytes 14155784 | tf_op jit(solution)/shard_map/ppermute | solution.py:29
  477.7 29.3 %collective-permute-start.51 = (bf16[2,384,384]{2,1,0:T(8,128)(2,1)S(1)}, bf16[2,384,384]{2,1,0:T(8,128)(2,1)S(1)}, u32[]{:S(2)}, u32[]{:S(2)}) collective-permute-start(bf16[2,384,384]{2,1,0:T(8,128)(2,1)S(1)} %copy-done.28), channel_id=1, source_target_pairs={{0,4},{4,0},{8,12},{12,8},{16,20},{20,16},{24,28},{28,24},{1,5},{5... | collective-permute-start | bytes 1769480 | tf_op jit(solution)/shard_map/ppermute | solution.py:29
  478.6 28.4 %collective-permute-start.52 = (bf16[768,384]{1,0:T(8,128)(2,1)S(1)}, bf16[768,384]{1,0:T(8,128)(2,1)S(1)}, u32[]{:S(2)}, u32[]{:S(2)}) collective-permute-start(bf16[768,384]{1,0:T(8,128)(2,1)S(1)} %slice_bitcast_fusion.16), channel_id=1, source_target_pairs={{0,2},{1,3},{2,0},{3,1},{4,6},{5,7},{6,4},{7,5},{8,10},{9,11},{10,... | collective-permute-start | bytes 1769480 | tf_op jit(solution)/shard_map/ppermute | solution.py:29
  484.9 22.1 %collective-permute-start.49 = (bf16[96,1536]{1,0:T(8,128)(2,1)}, bf16[96,1536]{1,0:T(8,128)(2,1)S(1)}, u32[]{:S(2)}, u32[]{:S(2)}) collective-permute-start(bf16[96,1536]{1,0:T(8,128)(2,1)} %get-tuple-element.401), channel_id=1, source_target_pairs={{0,16},{4,20},{8,24},{12,28},{16,0},{20,4},{24,8},{28,12},{1,17},{... | collective-permute-start | bytes 884744 | tf_op jit(solution)/shard_map/ppermute | solution.py:29
  485.3 21.7 %collective-permute-start.50 = (bf16[96,1536]{1,0:T(8,128)(2,1)S(1)}, bf16[96,1536]{1,0:T(8,128)(2,1)S(1)}, u32[]{:S(2)}, u32[]{:S(2)}) collective-permute-start(bf16[96,1536]{1,0:T(8,128)(2,1)S(1)} %copy-done.39), channel_id=1, source_target_pairs={{0,24},{4,28},{8,16},{12,20},{16,8},{20,12},{24,0},{28,4},{1,25},{... | collective-permute-start | bytes 884744 | tf_op jit(solution)/shard_map/ppermute | solution.py:29
  508.8 31.8 %collective-permute-start.54 = (bf16[384,384]{1,0:T(8,128)(2,1)S(1)}, bf16[384,384]{1,0:T(8,128)(2,1)S(1)}, u32[]{:S(2)}, u32[]{:S(2)}) collective-permute-start(bf16[384,384]{1,0:T(8,128)(2,1)S(1)} %slice_bitcast_fusion.25), channel_id=1, source_target_pairs={{0,2},{1,3},{2,0},{3,1},{4,6},{5,7},{6,4},{7,5},{8,10},{9,11},{10,... | collective-permute-start | bytes 884744 | tf_op jit(solution)/shard_map/ppermute | solution.py:29
  509.2 31.5 %collective-permute-start.55 = (bf16[384,384]{1,0:T(8,128)(2,1)S(1)}, bf16[384,384]{1,0:T(8,128)(2,1)S(1)}, u32[]{:S(2)}, u32[]{:S(2)}) collective-permute-start(bf16[384,384]{1,0:T(8,128)(2,1)S(1)} %slice.775), channel_id=1, source_target_pairs={{0,4},{4,0},{8,12},{12,8},{16,20},{20,16},{24,28},{28,24},{1,5},{5... | collective-permute-start | bytes 884744 | tf_op jit(solution)/shard_map/ppermute | solution.py:29
  537.2 26.2 %collective-permute-start.56 = (bf16[2,6,144,128]{3,2,1,0:T(8,128)(2,1)}, bf16[2,6,144,128]{3,2,1,0:T(8,128)(2,1)}, u32[]{:S(2)}, u32[]{:S(2)}) collective-permute-start(bf16[2,6,144,128]{3,2,1,0:T(8,128)(2,1)} %get-tuple-element.422), channel_id=1, source_target_pairs={{1,0},{2,1},{3,2},{5,4},{6,5},{7,6},{9,8},{10,9},{11,10},{13,12},{... | collective-permute-start | bytes 1327112 | tf_op jit(solution)/shard_map/ppermute | solution.py:39
  538.5 24.9 %collective-permute-start.57 = (bf16[2,6,144,128]{3,2,1,0:T(8,128)(2,1)}, bf16[2,6,144,128]{3,2,1,0:T(8,128)(2,1)}, u32[]{:S(2)}, u32[]{:S(2)}) collective-permute-start(bf16[2,6,144,128]{3,2,1,0:T(8,128)(2,1)} %get-tuple-element.422), channel_id=1, source_target_pairs={{2,0},{3,1},{6,4},{7,5},{10,8},{11,9},{14,12},{15,13},{18,16},{19,... | collective-permute-start | bytes 1327112 | tf_op jit(solution)/shard_map/ppermute | solution.py:39
  552.3 41.9 %collective-permute-start.58 = (bf16[2,384,768]{2,1,0:T(8,128)(2,1)}, bf16[2,384,768]{2,1,0:T(8,128)(2,1)}, u32[]{:S(2)}, u32[]{:S(2)}) collective-permute-start(bf16[2,384,768]{2,1,0:T(8,128)(2,1)} %slice.777), channel_id=1, source_target_pairs={{0,4},{4,0},{8,12},{12,8},{16,20},{20,16},{24,28},{28,24},{1,5},{5... | collective-permute-start | bytes 3538952 | tf_op jit(solution)/shard_map/ppermute | solution.py:29
  553.2 40.9 %collective-permute-start.59 = (bf16[768,768]{1,0:T(8,128)(2,1)}, bf16[768,768]{1,0:T(8,128)(2,1)}, u32[]{:S(2)}, u32[]{:S(2)}) collective-permute-start(bf16[768,768]{1,0:T(8,128)(2,1)} %slice_bitcast_fusion.3), channel_id=1, source_target_pairs={{0,2},{1,3},{2,0},{3,1},{4,6},{5,7},{6,4},{7,5},{8,10},{9,11},{10,... | collective-permute-start | bytes 3538952 | tf_op jit(solution)/shard_map/ppermute | solution.py:29
  556.6 37.5 %collective-permute-start.60 = (bf16[96,768]{1,0:T(8,128)(2,1)}, bf16[96,768]{1,0:T(8,128)(2,1)S(1)}, u32[]{:S(2)}, u32[]{:S(2)}) collective-permute-start(bf16[96,768]{1,0:T(8,128)(2,1)} %get-tuple-element.425), channel_id=1, source_target_pairs={{0,8},{4,12},{8,0},{12,4},{16,24},{20,28},{24,16},{28,20},{1,9},{5... | collective-permute-start | bytes 442376 | tf_op jit(solution)/shard_map/ppermute | solution.py:29
  563.4 30.7 %collective-permute-start.61 = (bf16[96,768]{1,0:T(8,128)(2,1)}, bf16[96,768]{1,0:T(8,128)(2,1)}, u32[]{:S(2)}, u32[]{:S(2)}) collective-permute-start(bf16[96,768]{1,0:T(8,128)(2,1)} %get-tuple-element.426), channel_id=1, source_target_pairs={{0,16},{4,20},{8,24},{12,28},{16,0},{20,4},{24,8},{28,12},{1,17},{... | collective-permute-start | bytes 442376 | tf_op jit(solution)/shard_map/ppermute | solution.py:29
  563.4 30.7 %collective-permute-start.62 = (bf16[96,768]{1,0:T(8,128)(2,1)}, bf16[96,768]{1,0:T(8,128)(2,1)}, u32[]{:S(2)}, u32[]{:S(2)}) collective-permute-start(bf16[96,768]{1,0:T(8,128)(2,1)} %get-tuple-element.427), channel_id=1, source_target_pairs={{0,24},{4,28},{8,16},{12,20},{16,8},{20,12},{24,0},{28,4},{1,25},{... | collective-permute-start | bytes 442376 | tf_op jit(solution)/shard_map/ppermute | solution.py:29
  625.7 32.6 %collective-permute-start.63 = (bf16[2,768,768]{2,1,0:T(8,128)(2,1)}, bf16[2,768,768]{2,1,0:T(8,128)(2,1)}, u32[]{:S(2)}, u32[]{:S(2)}) collective-permute-start(bf16[2,768,768]{2,1,0:T(8,128)(2,1)} %get-tuple-element.438), channel_id=1, source_target_pairs={{0,1},{1,0},{2,3},{3,2},{4,5},{5,4},{6,7},{7,6},{8,9},{9,8},{10,11... | collective-permute-start | bytes 7077896 | tf_op jit(solution)/shard_map/ppermute | solution.py:29
  631.1 27.1 %collective-permute-start.64 = (bf16[384,768]{1,0:T(8,128)(2,1)}, bf16[384,768]{1,0:T(8,128)(2,1)S(1)}, u32[]{:S(2)}, u32[]{:S(2)}) collective-permute-start(bf16[384,768]{1,0:T(8,128)(2,1)} %slice_bitcast_fusion.13), channel_id=1, source_target_pairs={{0,2},{1,3},{2,0},{3,1},{4,6},{5,7},{6,4},{7,5},{8,10},{9,11},{10,... | collective-permute-start | bytes 1769480 | tf_op jit(solution)/shard_map/ppermute | solution.py:29
  633.1 25.2 %collective-permute-start.65 = (bf16[384,768]{1,0:T(8,128)(2,1)}, bf16[384,768]{1,0:T(8,128)(2,1)}, u32[]{:S(2)}, u32[]{:S(2)}) collective-permute-start(bf16[384,768]{1,0:T(8,128)(2,1)} %slice.790), channel_id=1, source_target_pairs={{0,4},{4,0},{8,12},{12,8},{16,20},{20,16},{24,28},{28,24},{1,5},{5... | collective-permute-start | bytes 1769480 | tf_op jit(solution)/shard_map/ppermute | solution.py:29
  664.0 24.5 %collective-permute-start.69 = (bf16[2,384,384]{2,1,0:T(8,128)(2,1)S(1)}, bf16[2,384,384]{2,1,0:T(8,128)(2,1)S(1)}, u32[]{:S(2)}, u32[]{:S(2)}) collective-permute-start(bf16[2,384,384]{2,1,0:T(8,128)(2,1)S(1)} %slice.791), channel_id=1, source_target_pairs={{0,4},{4,0},{8,12},{12,8},{16,20},{20,16},{24,28},{28,24},{1,5},{5... | collective-permute-start | bytes 1769480 | tf_op jit(solution)/shard_map/ppermute | solution.py:29
  665.2 23.4 %collective-permute-start.70 = (bf16[768,384]{1,0:T(8,128)(2,1)S(1)}, bf16[768,384]{1,0:T(8,128)(2,1)S(1)}, u32[]{:S(2)}, u32[]{:S(2)}) collective-permute-start(bf16[768,384]{1,0:T(8,128)(2,1)S(1)} %slice_bitcast_fusion.12), channel_id=1, source_target_pairs={{0,2},{1,3},{2,0},{3,1},{4,6},{5,7},{6,4},{7,5},{8,10},{9,11},{10,... | collective-permute-start | bytes 1769480 | tf_op jit(solution)/shard_map/ppermute | solution.py:29
  667.0 21.5 %collective-permute-start.67 = (bf16[96,1536]{1,0:T(8,128)(2,1)S(1)}, bf16[96,1536]{1,0:T(8,128)(2,1)S(1)}, u32[]{:S(2)}, u32[]{:S(2)}) collective-permute-start(bf16[96,1536]{1,0:T(8,128)(2,1)S(1)} %get-tuple-element.448), channel_id=1, source_target_pairs={{0,16},{4,20},{8,24},{12,28},{16,0},{20,4},{24,8},{28,12},{1,17},{... | collective-permute-start | bytes 884744 | tf_op jit(solution)/shard_map/ppermute | solution.py:29
  (85 other events, 1005.4 us)
